TPU v7x, 128 devices: a whole 4x4x4 slice. The times are simulated.
128 devices in a mesh: ctx: 8 (over y_hi, z), exp: 16 (over y_lo, x, core).
Axes of the slice: x: 4, y: 4 (y_hi: 2, y_lo: 2; y = y_hi * 2 + y_lo), z: 4, core: 2. Of those that a mesh axis runs over, the one named last changes fastest.
Arguments:
- moe_input: bfloat16 [16384, 4096], P(('ctx', 'exp')), may hold values from -6 to 6
- out_grad: bfloat16 [16384, 4096], P(('ctx', 'exp')), may hold values from -6 to 6
- w_gate: bfloat16 [32, 4096, 1408], P('exp', None, 'ctx'), may hold values from -0.09375 to 0.09375
- w_up: bfloat16 [32, 4096, 1408], P('exp', None, 'ctx'), may hold values from -0.09375 to 0.09375
- w_down: bfloat16 [32, 1408, 4096], P('exp', 'ctx'), may hold values from -0.15625 to 0.15625
- expert_picks: int32 [32, 128], replicated, may hold values from 0 to 16383, as said below
- gate_probs: float32 [32, 128], replicated, may hold values from 0.2 to 1
- queries: bfloat16 [16384, 2048], P('ctx', 'exp'), may hold values from -6 to 6
- attn_keys: bfloat16 [16384, 2048], P('ctx', 'exp'), may hold values from -6 to 6
- values: bfloat16 [16384, 2048], P('ctx', 'exp'), may hold values from -6 to 6
- attn_out: bfloat16 [16384, 2048], P('ctx', 'exp'), may hold values from -1.5 to 1.5
- log_norm: float32 [16, 16384], P('exp'), may hold values from -1 to 12
- w_out: bfloat16 [2048, 4096], P('exp'), may hold values from -0.09375 to 0.09375
Outputs:
- d_resid: bfloat16 [16384, 4096], P(('ctx', 'exp'))
- dw_gate: bfloat16 [32, 4096, 1408], P('exp', None, 'ctx')
- dw_up: bfloat16 [32, 4096, 1408], P('exp', None, 'ctx')
- dw_down: bfloat16 [32, 1408, 4096], P('exp', 'ctx')
- d_gates: float32 [32, 128], P('exp', 'ctx')
- dw_out: bfloat16 [2048, 4096], P('exp', 'ctx')
- grad_q: bfloat16 [16384, 2048], P('ctx', 'exp')
- grad_k: bfloat16 [16384, 2048], P('ctx', 'exp')
- grad_v: bfloat16 [16384, 2048], P('ctx', 'exp')
Inputs may be any that keep to these rules, and one draw needn't show every extreme that they name: expert_picks[e] lists distinct tokens in ascending order: exactly 16 from each context group of 2048 consecutive tokens and at most 2 from each aligned block of 128 tokens; in every group some block gives exactly 2.
All inputs are finite; a program needn't handle non-finite values.
Results may differ from a plain program's by a relative error of at most 0.023.
Values may be sent and summed in bfloat16 or wider, within the bound.
A program may use at most 256 MiB of HBM per device.

v0:
```python
import math

import jax
import jax.numpy as jnp
from jax import lax
from jax.sharding import PartitionSpec as P

MOST = 2


def activation(pre_act):
    sigmoid_val = jax.nn.sigmoid(pre_act)
    return (pre_act * sigmoid_val, sigmoid_val * (1.0 + pre_act * (1.0 - sigmoid_val)))


def settle(value):
    return lax.optimization_barrier(value.astype(jnp.bfloat16)).astype(jnp.float32)


def contract_first(left, right):
    return lax.dot_general(
        left, right, (((0,), (0,)), ((), ())), preferred_element_type=jnp.float32
    )


def contract_last(left, right):
    return lax.dot_general(
        left, right, (((1,), (1,)), ((), ())), preferred_element_type=jnp.float32
    )


def tile_grads(
    q_rows, do_rows, norm_rows, delta_rows, keys_here, values_here, key_pos, key_scale, piece_count
):
    row_count, head_dim = q_rows.shape
    block_rows = math.gcd(row_count, 2048)
    block_total = row_count // block_rows
    piece_len = keys_here.shape[0] // piece_count

    def one_block(block_idx, carried):
        grad_rows, grad_keys, grad_values = carried
        row_start = block_idx * block_rows
        q_block = lax.dynamic_slice_in_dim(q_rows, row_start, block_rows, 0)
        do_block = lax.dynamic_slice_in_dim(do_rows, row_start, block_rows, 0)
        norm_block = lax.dynamic_slice_in_dim(norm_rows, row_start, block_rows, 0)
        delta_block = lax.dynamic_slice_in_dim(delta_rows, row_start, block_rows, 0)
        q_positions = row_start + jnp.arange(block_rows, dtype=jnp.int32)
        last_query = row_start + block_rows - 1
        keys_piece = keys_here
        values_piece = values_here
        pos_piece = key_pos

        def compute_tile(
            unused, keys_piece=keys_piece, values_piece=values_piece, pos_piece=pos_piece
        ):
            scores = contract_last(q_block, keys_piece) * key_scale
            causal = pos_piece[None, :] <= q_positions[:, None]
            attn_probs = jnp.exp(jnp.where(causal, scores - norm_block[:, None], -1e30))
            d_probs = contract_last(do_block, values_piece)
            d_scores = (attn_probs * (d_probs - delta_block[:, None])).astype(jnp.bfloat16)
            probs_low = attn_probs.astype(jnp.bfloat16)
            piece_q = jnp.dot(d_scores, keys_piece, preferred_element_type=jnp.float32) * key_scale
            piece_k = contract_first(d_scores, q_block) * key_scale
            piece_v = contract_first(probs_low, do_block)
            return (piece_q, piece_k, piece_v)

        def skip_tile(unused):
            return (
                jnp.zeros((block_rows, head_dim), jnp.float32),
                jnp.zeros((piece_len, head_dim), jnp.float32),
                jnp.zeros((piece_len, head_dim), jnp.float32),
            )

        piece_q, piece_k, piece_v = lax.cond(
            last_query >= jnp.min(pos_piece), compute_tile, skip_tile, 0
        )
        key_parts = [piece_k]
        value_parts = [piece_v]
        add_k = jnp.concatenate(key_parts, axis=0)
        add_v = jnp.concatenate(value_parts, axis=0)
        grad_rows = lax.dynamic_update_slice_in_dim(grad_rows, piece_q, row_start, 0)
        return (grad_rows, grad_keys + add_k, grad_values + add_v)

    start_state = (
        jnp.zeros((row_count, head_dim), jnp.float32),
        jnp.zeros(keys_here.shape, jnp.float32),
        jnp.zeros(values_here.shape, jnp.float32),
    )
    return lax.fori_loop(0, block_total, one_block, start_state)


def body(
    moe_input,
    out_grad,
    w_gate,
    w_up,
    w_down,
    expert_picks,
    gate_probs,
    queries,
    attn_keys,
    values,
    attn_out,
    log_norm,
    w_out,
):
    n_ctx = lax.axis_size("ctx")
    n_exp = lax.axis_size("exp")
    ctx_id = lax.axis_index("ctx")
    exp_id = lax.axis_index("exp")
    tok_dev, feat_width = moe_input.shape
    n_local = w_gate.shape[0]
    slot_count = MOST
    group_picks = expert_picks.shape[1] // n_ctx
    block_id = ctx_id * n_exp + exp_id
    base_row = block_id * tok_dev
    count_below = jnp.sum((expert_picks < base_row).astype(jnp.int32), axis=1)
    inside = jnp.sum(
        ((expert_picks >= base_row) & (expert_picks < base_row + tok_dev)).astype(jnp.int32), axis=1
    )
    offsets = jnp.arange(slot_count, dtype=jnp.int32)
    slot_spots = jnp.minimum(count_below[:, None] + offsets[None, :], expert_picks.shape[1] - 1)
    is_valid = offsets[None, :] < inside[:, None]
    chosen = jnp.where(
        is_valid, jnp.take_along_axis(expert_picks, slot_spots, axis=1) - base_row, 0
    )
    send_rows = jnp.where(is_valid[..., None], moe_input[chosen], jnp.zeros((), jnp.bfloat16))
    send_grads = jnp.where(is_valid[..., None], out_grad[chosen], jnp.zeros((), jnp.bfloat16))
    got_rows, got_grads = (
        lax.all_to_all(
            send_rows.reshape(n_exp, n_local, slot_count, feat_width),
            "exp",
            split_axis=0,
            concat_axis=0,
            tiled=True,
        ),
        lax.all_to_all(
            send_grads.reshape(n_exp, n_local, slot_count, feat_width),
            "exp",
            split_axis=0,
            concat_axis=0,
            tiled=True,
        ),
    )
    my_picks = lax.dynamic_slice(
        expert_picks, (exp_id * n_local, ctx_id * group_picks), (n_local, group_picks)
    )
    src_exp = my_picks // tok_dev - ctx_id * n_exp
    starts = my_picks // tok_dev * tok_dev
    slot_rank = jnp.arange(group_picks, dtype=jnp.int32)[None, :] - jnp.sum(
        (my_picks[:, None, :] < starts[:, :, None]).astype(jnp.int32), axis=2
    )
    flat_pos = (
        (src_exp * n_local + jnp.arange(n_local, dtype=jnp.int32)[:, None]) * slot_count + slot_rank
    ).reshape(-1)
    mine_rows = jnp.take(got_rows.reshape(-1, feat_width), flat_pos, axis=0).reshape(
        n_local, group_picks, feat_width
    )
    mine_grads = jnp.take(got_grads.reshape(-1, feat_width), flat_pos, axis=0).reshape(
        n_local, group_picks, feat_width
    )
    slot_rows, slot_grads = (
        lax.all_gather(mine_rows, "ctx", axis=1, tiled=True),
        lax.all_gather(mine_grads, "ctx", axis=1, tiled=True),
    )
    gate_rows = lax.dynamic_slice_in_dim(gate_probs, exp_id * n_local, n_local, 0)
    pre_gate = jnp.einsum("kcd,kdf->kcf", slot_rows, w_gate, preferred_element_type=jnp.float32)
    pre_up = jnp.einsum("kcd,kdf->kcf", slot_rows, w_up, preferred_element_type=jnp.float32)
    gated_act, act_slope = activation(pre_gate)
    hidden_full = gated_act * pre_up
    hidden = hidden_full.astype(jnp.bfloat16)
    down_back = jnp.einsum("kcd,kfd->kcf", slot_grads, w_down, preferred_element_type=jnp.float32)
    gate_part = settle(jnp.sum(down_back * hidden_full, axis=2))
    scaled = gate_rows[..., None] * down_back
    d_gate = (scaled * pre_up * act_slope).astype(jnp.bfloat16)
    d_up = (scaled * gated_act).astype(jnp.bfloat16)
    weighted = (gate_rows[..., None] * slot_grads.astype(jnp.float32)).astype(jnp.bfloat16)
    dw_down = jnp.einsum(
        "kcf,kcd->kfd", hidden, weighted, preferred_element_type=jnp.float32
    ).astype(jnp.bfloat16)
    dw_gate = jnp.einsum(
        "kcd,kcf->kdf", slot_rows, d_gate, preferred_element_type=jnp.float32
    ).astype(jnp.bfloat16)
    dw_up = jnp.einsum("kcd,kcf->kdf", slot_rows, d_up, preferred_element_type=jnp.float32).astype(
        jnp.bfloat16
    )
    dx_part = settle(
        jnp.einsum("kcf,kdf->kcd", d_gate, w_gate, preferred_element_type=jnp.float32)
        + jnp.einsum("kcf,kdf->kcd", d_up, w_up, preferred_element_type=jnp.float32)
    )
    dx_sum, d_gates = (
        lax.psum_scatter(
            dx_part.astype(jnp.bfloat16), "ctx", scatter_dimension=1, tiled=True
        ).astype(jnp.float32),
        lax.psum_scatter(
            gate_part.astype(jnp.bfloat16), "ctx", scatter_dimension=1, tiled=True
        ).astype(jnp.float32),
    )
    dx_slot = dx_sum.astype(jnp.bfloat16)
    back_rows = (
        jnp.zeros((n_exp * n_local * slot_count, feat_width), jnp.bfloat16)
        .at[flat_pos]
        .set(dx_slot.reshape(-1, feat_width))
    )
    returned = lax.all_to_all(
        back_rows.reshape(n_exp, n_local, slot_count, feat_width),
        "exp",
        split_axis=0,
        concat_axis=0,
        tiled=True,
    )
    returned = returned.reshape(-1, feat_width)
    onehot = (
        (chosen.reshape(-1)[None, :] == jnp.arange(tok_dev, dtype=jnp.int32)[:, None])
        & is_valid.reshape(-1)[None, :]
    ).astype(jnp.bfloat16)
    d_resid = (
        out_grad.astype(jnp.float32) + jnp.dot(onehot, returned, preferred_element_type=jnp.float32)
    ).astype(jnp.bfloat16)
    tok_ctx, head_dim = queries.shape
    key_scale = head_dim ** (-0.5)
    piece_rows = lax.all_gather(d_resid, "exp", axis=0, tiled=True)
    out_rows = contract_last(piece_rows, w_out)
    d_out_acc = out_rows.astype(jnp.bfloat16)
    dw_part = contract_first(attn_out, piece_rows)
    d_out, dw_part = (d_out_acc, dw_part)
    dw_out = lax.psum_scatter(
        settle(dw_part).astype(jnp.bfloat16), "ctx", scatter_dimension=1, tiled=True
    )
    row_delta = jnp.sum(d_out.astype(jnp.float32) * attn_out.astype(jnp.float32), axis=1)
    lse_all = log_norm[0]
    keys_here, values_here = (attn_keys, values)
    key_pos = ctx_id * tok_ctx + jnp.arange(tok_ctx, dtype=jnp.int32)
    key_pieces = 1
    delta_all = lax.all_gather(row_delta, "ctx", axis=0, tiled=True)
    q_rows = lax.all_gather(queries, "ctx", axis=0, tiled=True)
    do_rows = lax.all_gather(d_out, "ctx", axis=0, tiled=True)
    add_q, add_k, add_v = tile_grads(
        q_rows, do_rows, lse_all, delta_all, keys_here, values_here, key_pos, key_scale, key_pieces
    )
    dq_all = add_q
    dq_all, grad_keys, grad_values = (dq_all, add_k, add_v)
    grad_q = lax.psum_scatter(dq_all.astype(jnp.bfloat16), "ctx", scatter_dimension=0, tiled=True)
    grad_k = grad_keys.astype(jnp.bfloat16)
    grad_v = grad_values.astype(jnp.bfloat16)
    return (d_resid, dw_gate, dw_up, dw_down, d_gates, dw_out, grad_q, grad_k, grad_v)


def solution(mesh):
    return jax.shard_map(
        body,
        mesh=mesh,
        in_specs=(
            P(("ctx", "exp"), None),
            P(("ctx", "exp"), None),
            P("exp", None, "ctx"),
            P("exp", None, "ctx"),
            P("exp", "ctx", None),
            P(),
            P(),
            P("ctx", "exp"),
            P("ctx", "exp"),
            P("ctx", "exp"),
            P("ctx", "exp"),
            P("exp", None),
            P("exp", None),
        ),
        out_specs=(
            P(("ctx", "exp"), None),
            P("exp", None, "ctx"),
            P("exp", None, "ctx"),
            P("exp", "ctx", None),
            P("exp", "ctx"),
            P("exp", "ctx"),
            P("ctx", "exp"),
            P("ctx", "exp"),
            P("ctx", "exp"),
        ),
        check_vma=False,
    )
```

profile of v0, /device:TPU:0, one launch (start us, length us, event | category | flops | bytes accessed | tf_op | source)
XLA Modules:
  0.0 887.2 jit_solution(8527836403347974611)
XLA Ops:
  26.4 10.5 %all-to-all-done = bf16[16,2,2,4096]{3,2,1,0:T(2,128)(2,1)S(1)} async-done(((bf16[16,2,2,4096]{3,2,1,0:T(2,128)(2,1)}), bf16[16,2,2,4096]{3,2,1,0:T(2,128)(2,1)S(1)}, u32[]{:S(2)}, u32[]{:S(2)}) %all-to-all-start) | async-done | bytes 524320 | tf_op jit(solution)/shard_map/all_to_all | solution.py:137
  58.2 52.4 %all-gather.8.cloned.1.call-done = bf16[2,128,4096]{2,1,0:T(8,128)(2,1)} async-done(((bf16[2,16,4096]{2,1,0:T(8,128)(2,1)}), bf16[2,128,4096]{2,1,0:T(8,128)(2,1)}) %all-gather.8.cloned.1.call-update) | async-done | bytes 2097168 | tf_op jit(solution)/shard_map/all_gather | solution.py:163
  114.6 50.8 %all-gather.6.cloned.1.call-done = bf16[2,128,4096]{2,1,0:T(8,128)(2,1)} async-done(((bf16[2,16,4096]{2,1,0:T(8,128)(2,1)}), bf16[2,128,4096]{2,1,0:T(8,128)(2,1)}) %all-gather.6.cloned.1.call-update) | async-done | bytes 2097168 | tf_op jit(solution)/shard_map/all_gather | solution.py:164
  172.9 73.0 %reduce-scatter.7.cloned.1.call-done = bf16[2,16,4096]{2,1,0:T(8,128)(2,1)} async-done(((bf16[2,128,4096]{2,1,0:T(8,128)(2,1)}), bf16[2,16,4096]{2,1,0:T(8,128)(2,1)}) %reduce-scatter.7.cloned.1.call-update) | async-done | bytes 262160 | tf_op jit(solution)/shard_map/reduce_scatter | solution.py:192
  253.9 9.9 %all-to-all-done.2 = bf16[16,2,2,4096]{3,2,1,0:T(2,128)(2,1)S(1)} async-done(((bf16[16,2,2,4096]{3,2,1,0:T(2,128)(2,1)}), bf16[16,2,2,4096]{3,2,1,0:T(2,128)(2,1)S(1)}, u32[]{:S(2)}, u32[]{:S(2)}) %all-to-all-start.2) | async-done | bytes 524320 | tf_op jit(solution)/shard_map/all_to_all | solution.py:205
  265.7 88.6 %all-gather.10.cloned.1.call-done = bf16[2048,4096]{1,0:T(8,128)(2,1)} async-done(((bf16[128,4096]{1,0:T(8,128)(2,1)}), bf16[2048,4096]{1,0:T(8,128)(2,1)}) %all-gather.10.cloned.1.call-update) | async-done | bytes 16777232 | tf_op jit(solution)/shard_map/all_gather | solution.py:222
  354.4 12.4 %multiply_reduce_fusion = (f32[2048]{0:T(1024)S(1)}, bf16[2048,128]{0,1:T(8,128)(2,1)}) fusion(bf16[2048,128]{0,1:T(8,128)(2,1)S(1)} %copy.31, bf16[2048,4096]{1,0:T(8,128)(2,1)} %all-gather.10.cloned.1.call-done, bf16[128,4096]{1,0:T(8,128)(2,1)} %param.31), kind=kOutput, calls=%fused_computation.41 | convolution fusion | flops 2148792320 | bytes 18882560 | tf_op jit(solution)/shard_map/dot_general | solution.py:27
  368.9 9.2 %fusion.18 = bf16[128,4096]{0,1:T(8,128)(2,1)} fusion(bf16[2048,4096]{1,0:T(8,128)(2,1)} %all-gather.10.cloned.1.call-done, bf16[2048,128]{1,0:T(8,128)(2,1)S(1)} %copy-done.16), kind=kOutput, calls=%fused_computation.37 | convolution fusion | flops 2148007936 | bytes 18350080 | tf_op jit(solution)/shard_map/dot_general | solution.py:21
  378.1 36.5 %all_gather.23 = f32[16384]{0:T(1024)} all-gather(f32[2048]{0:T(1024)S(1)} %get-tuple-element.634), channel_id=1, replica_groups=mesh['ctx'=8,'exp'=16] {'ctx'}, dimensions={0}, use_global_device_ids=true | all-gather | bytes 73728 | tf_op jit(solution)/shard_map/all_gather | solution.py:235
  414.7 24.9 %all-gather.14.cloned.1.call-done = bf16[16384,128]{0,1:T(8,128)(2,1)} async-done(((bf16[2048,128]{0,1:T(8,128)(2,1)}), bf16[16384,128]{0,1:T(8,128)(2,1)}) %all-gather.14.cloned.1.call-update) | async-done | bytes 4194320 | tf_op jit(solution)/shard_map/all_gather | solution.py:237
  446.0 65.2 %all-gather.12.cloned.1.call-done = bf16[16384,128]{1,0:T(8,128)(2,1)} async-done(((bf16[2048,128]{1,0:T(8,128)(2,1)}), bf16[16384,128]{1,0:T(8,128)(2,1)}) %all-gather.12.cloned.1.call-update) | async-done | bytes 4194320 | tf_op jit(solution)/shard_map/all_gather | solution.py:236
  513.4 285.8 %while.22 = (s32[]{:T(128)}, bf16[16384,128]{1,0:T(8,128)(2,1)}, f32[2048,128]{1,0:T(8,128)}, f32[2048,128]{1,0:T(8,128)}, s32[]{:T(128)}, /*index=5*/bf16[16384...) while((s32[]{:T(128)}, bf16[16384,128]{1,0:T(8,128)(2,1)}, ...), condition=%wide.region_13.15_spmd.clone, body=%wide.region_10.14_spmd.clone.sunk | while | flops 5420617728 | bytes 126487464 | solution.py:89
  524.2 28.8 %conditional.3 = (f32[2048,128]{1,0:T(8,128)}, f32[2048,128]{1,0:T(8,128)S(1)}, f32[2048,128]{1,0:T(8,128)S(1)}) conditional(s32[]{:T(128)} %convert_element_type.156, () %tuple.94, (s32[]{:T(128)}, s32[]{:T(128)}, s32[2048]{0:T(1024)S(1)}, bf16[16384,128]{1,0:T(8,128)(2,1)}, s32[]{:T(128)}, /*index=5*/bf16[2048,128]{1,0:T(8,128)(2,1)S(1)}, ...), branch_computations={%region_11.12_spmd, %region_12.13_spmd} | conditional | flops 5419569152 | bytes 118089824 | solution.py:74
  535.2 8.3 multiply_convert_fusion
  557.4 28.7 %conditional.3 = (f32[2048,128]{1,0:T(8,128)}, f32[2048,128]{1,0:T(8,128)S(1)}, f32[2048,128]{1,0:T(8,128)S(1)}) conditional(s32[]{:T(128)} %convert_element_type.156, () %tuple.94, (s32[]{:T(128)}, s32[]{:T(128)}, s32[2048]{0:T(1024)S(1)}, bf16[16384,128]{1,0:T(8,128)(2,1)}, s32[]{:T(128)}, /*index=5*/bf16[2048,128]{1,0:T(8,128)(2,1)S(1)}, ...), branch_computations={%region_11.12_spmd, %region_12.13_spmd} | conditional | flops 5419569152 | bytes 118089824 | solution.py:74
  592.0 28.8 %conditional.3 = (f32[2048,128]{1,0:T(8,128)}, f32[2048,128]{1,0:T(8,128)S(1)}, f32[2048,128]{1,0:T(8,128)S(1)}) conditional(s32[]{:T(128)} %convert_element_type.156, () %tuple.94, (s32[]{:T(128)}, s32[]{:T(128)}, s32[2048]{0:T(1024)S(1)}, bf16[16384,128]{1,0:T(8,128)(2,1)}, s32[]{:T(128)}, /*index=5*/bf16[2048,128]{1,0:T(8,128)(2,1)S(1)}, ...), branch_computations={%region_11.12_spmd, %region_12.13_spmd} | conditional | flops 5419569152 | bytes 118089824 | solution.py:74
  626.7 28.8 %conditional.3 = (f32[2048,128]{1,0:T(8,128)}, f32[2048,128]{1,0:T(8,128)S(1)}, f32[2048,128]{1,0:T(8,128)S(1)}) conditional(s32[]{:T(128)} %convert_element_type.156, () %tuple.94, (s32[]{:T(128)}, s32[]{:T(128)}, s32[2048]{0:T(1024)S(1)}, bf16[16384,128]{1,0:T(8,128)(2,1)}, s32[]{:T(128)}, /*index=5*/bf16[2048,128]{1,0:T(8,128)(2,1)S(1)}, ...), branch_computations={%region_11.12_spmd, %region_12.13_spmd} | conditional | flops 5419569152 | bytes 118089824 | solution.py:74
  637.7 8.3 multiply_convert_fusion
  661.4 28.7 %conditional.3 = (f32[2048,128]{1,0:T(8,128)}, f32[2048,128]{1,0:T(8,128)S(1)}, f32[2048,128]{1,0:T(8,128)S(1)}) conditional(s32[]{:T(128)} %convert_element_type.156, () %tuple.94, (s32[]{:T(128)}, s32[]{:T(128)}, s32[2048]{0:T(1024)S(1)}, bf16[16384,128]{1,0:T(8,128)(2,1)}, s32[]{:T(128)}, /*index=5*/bf16[2048,128]{1,0:T(8,128)(2,1)S(1)}, ...), branch_computations={%region_11.12_spmd, %region_12.13_spmd} | conditional | flops 5419569152 | bytes 118089824 | solution.py:74
  672.4 8.3 multiply_convert_fusion
  696.0 28.7 %conditional.3 = (f32[2048,128]{1,0:T(8,128)}, f32[2048,128]{1,0:T(8,128)S(1)}, f32[2048,128]{1,0:T(8,128)S(1)}) conditional(s32[]{:T(128)} %convert_element_type.156, () %tuple.94, (s32[]{:T(128)}, s32[]{:T(128)}, s32[2048]{0:T(1024)S(1)}, bf16[16384,128]{1,0:T(8,128)(2,1)}, s32[]{:T(128)}, /*index=5*/bf16[2048,128]{1,0:T(8,128)(2,1)S(1)}, ...), branch_computations={%region_11.12_spmd, %region_12.13_spmd} | conditional | flops 5419569152 | bytes 118089824 | solution.py:74
  730.6 28.7 %conditional.3 = (f32[2048,128]{1,0:T(8,128)}, f32[2048,128]{1,0:T(8,128)S(1)}, f32[2048,128]{1,0:T(8,128)S(1)}) conditional(s32[]{:T(128)} %convert_element_type.156, () %tuple.94, (s32[]{:T(128)}, s32[]{:T(128)}, s32[2048]{0:T(1024)S(1)}, bf16[16384,128]{1,0:T(8,128)(2,1)}, s32[]{:T(128)}, /*index=5*/bf16[2048,128]{1,0:T(8,128)(2,1)S(1)}, ...), branch_computations={%region_11.12_spmd, %region_12.13_spmd} | conditional | flops 5419569152 | bytes 118089824 | solution.py:74
  765.2 28.7 %conditional.3 = (f32[2048,128]{1,0:T(8,128)}, f32[2048,128]{1,0:T(8,128)S(1)}, f32[2048,128]{1,0:T(8,128)S(1)}) conditional(s32[]{:T(128)} %convert_element_type.156, () %tuple.94, (s32[]{:T(128)}, s32[]{:T(128)}, s32[2048]{0:T(1024)S(1)}, bf16[16384,128]{1,0:T(8,128)(2,1)}, s32[]{:T(128)}, /*index=5*/bf16[2048,128]{1,0:T(8,128)(2,1)S(1)}, ...), branch_computations={%region_11.12_spmd, %region_12.13_spmd} | conditional | flops 5419569152 | bytes 118089824 | solution.py:74
  815.5 64.9 %reduce-scatter.11.cloned.1.call-done = bf16[2048,128]{1,0:T(8,128)(2,1)} async-done(((bf16[16384,128]{1,0:T(8,128)(2,1)}), bf16[2048,128]{1,0:T(8,128)(2,1)}) %reduce-scatter.11.cloned.1.call-update) | async-done | bytes 524304 | tf_op jit(solution)/shard_map/reduce_scatter | solution.py:243
  (248 shorter events, 333.6 us)
Async XLA Ops:
  7.2 103.4 %copy-start = (bf16[2,4096,176]{1,2,0:T(8,128)(2,1)S(1)}, bf16[2,4096,176]{1,2,0:T(8,128)(2,1)}, u32[]{:S(2)}) copy-start(bf16[2,4096,176]{1,2,0:T(8,128)(2,1)} %param.21) | copy-start | bytes 8650756
  20.6 16.4 %all-to-all-start = ((bf16[16,2,2,4096]{3,2,1,0:T(2,128)(2,1)}), bf16[16,2,2,4096]{3,2,1,0:T(2,128)(2,1)S(1)}, u32[]{:S(2)}, u32[]{:S(2)}) async-start(bf16[16,2,2,4096]{3,2,1,0:T(2,128)(2,1)} %get-tuple-element.630), calls=%async_computation | async-start | bytes 1048576 | tf_op jit(solution)/shard_map/all_to_all | solution.py:137
  36.9 15.1 %all-to-all-start.1 = ((bf16[16,2,2,4096]{3,2,1,0:T(2,128)(2,1)}), bf16[16,2,2,4096]{3,2,1,0:T(2,128)(2,1)}, u32[]{:S(2)}, u32[]{:S(2)}) async-start(bf16[16,2,2,4096]{3,2,1,0:T(2,128)(2,1)} %get-tuple-element.631), calls=%async_computation.1 | async-start | bytes 1048576 | tf_op jit(solution)/shard_map/all_to_all | solution.py:130
  41.2 69.4 %all-gather.8.cloned.1.call-start = ((), (), s32[]{:S(2)}) async-start(), calls=%async_computation.8 | async-start | bytes 2359296 | tf_op jit(solution)/shard_map/all_gather | solution.py:163
  56.7 108.7 %all-gather.6.cloned.1.call-start = ((), (), s32[]{:S(2)}) async-start(), calls=%async_computation.7 | async-start | bytes 2359296 | tf_op jit(solution)/shard_map/all_gather | solution.py:164
  57.4 188.5 %reduce-scatter.7.cloned.1.call-start = ((), (), s32[]{:S(2)}) async-start(), calls=%async_computation.9 | async-start | bytes 2359296 | tf_op jit(solution)/shard_map/reduce_scatter | solution.py:192
  58.2 107.2 %copy-start.21 = (f32[2,128]{1,0:T(2,128)}, f32[2,128]{1,0:T(2,128)S(1)}, u32[]{:S(2)}) copy-start(f32[2,128]{1,0:T(2,128)S(1)} %constant_dynamic-slice_fusion) | copy-start | bytes 3076
  113.7 55.1 %copy-start.12 = (f32[2,128,176]{1,2,0:T(8,128)}, f32[2,128,176]{1,2,0:T(8,128)S(1)}, u32[]{:S(2)}) copy-start(f32[2,128,176]{1,2,0:T(8,128)S(1)} %fusion.35) | copy-start | bytes 540676
  114.6 55.0 %copy-start.14 = (f32[2,128,176]{1,2,0:T(8,128)}, f32[2,128,176]{1,2,0:T(8,128)S(1)}, u32[]{:S(2)}) copy-start(f32[2,128,176]{1,2,0:T(8,128)S(1)} %fusion.34) | copy-start | bytes 540676
  172.8 91.2 %copy-start.6 = (bf16[128,4096]{1,0:T(8,128)(2,1)S(1)}, bf16[128,4096]{1,0:T(8,128)(2,1)}, u32[]{:S(2)}) copy-start(bf16[128,4096]{1,0:T(8,128)(2,1)} %param.20) | copy-start | bytes 3145732
  172.8 92.7 %copy-start.16 = (bf16[2048,128]{1,0:T(8,128)(2,1)S(1)}, bf16[2048,128]{1,0:T(8,128)(2,1)}, u32[]{:S(2)}) copy-start(bf16[2048,128]{1,0:T(8,128)(2,1)} %param.29) | copy-start | bytes 1572868
  248.6 15.2 %all-to-all-start.2 = ((bf16[16,2,2,4096]{3,2,1,0:T(2,128)(2,1)}), bf16[16,2,2,4096]{3,2,1,0:T(2,128)(2,1)S(1)}, u32[]{:S(2)}, u32[]{:S(2)}) async-start(bf16[16,2,2,4096]{3,2,1,0:T(2,128)(2,1)} %reshape.304), calls=%async_computation.3 | async-start | bytes 1048576 | tf_op jit(solution)/shard_map/all_to_all | solution.py:205
  253.0 101.4 %all-gather.10.cloned.1.call-start = ((), (), s32[]{:S(2)}) async-start(), calls=%async_computation.10 | async-start | bytes 17825792 | tf_op jit(solution)/shard_map/all_gather | solution.py:222
  265.5 174.1 %all-gather.14.cloned.1.call-start = ((), (), s32[]{:S(2)}) async-start(), calls=%async_computation.13 | async-start | bytes 4718592 | tf_op jit(solution)/shard_map/all_gather | solution.py:237
  366.8 144.3 %all-gather.12.cloned.1.call-start = ((), (), s32[]{:S(2)}) async-start(), calls=%async_computation.12 | async-start | bytes 4718592 | tf_op jit(solution)/shard_map/all_gather | solution.py:236
  367.4 441.0 %reduce-scatter.13.cloned.1.call-start = ((), (), s32[]{:S(2)}) async-start(), calls=%async_computation.15 | async-start | bytes 36864
  368.9 440.8 %reduce-scatter.9.cloned.1.call-start = ((), (), s32[]{:S(2)}) async-start(), calls=%async_computation.11 | async-start | bytes 1179648 | tf_op jit(solution)/shard_map/reduce_scatter | solution.py:227
  414.6 465.8 %reduce-scatter.11.cloned.1.call-start = ((), (), s32[]{:S(2)}) async-start(), calls=%async_computation.14 | async-start | bytes 4718592 | tf_op jit(solution)/shard_map/reduce_scatter | solution.py:243
  446.0 67.4 %copy-start.7 = (bf16[2048,128]{1,0:T(8,128)(2,1)S(1)}, bf16[2048,128]{1,0:T(8,128)(2,1)}, u32[]{:S(2)}) copy-start(bf16[2048,128]{1,0:T(8,128)(2,1)} %param.27) | copy-start | bytes 1572868
  529.0 6.2 copy-start.23
  562.2 6.2 copy-start.23
  596.9 6.2 copy-start.23
  666.2 6.2 copy-start.23
  803.3 77.2 %copy-start.1 = (bf16[2,4096,176]{1,2,0:T(8,128)(2,1)S(1)}, bf16[2,4096,176]{1,2,0:T(8,128)(2,1)}, u32[]{:S(2)}) copy-start(bf16[2,4096,176]{1,2,0:T(8,128)(2,1)} %param.21) | copy-start | bytes 8650756
  (27 other events, 124.1 us)
Sparse Core Ops, SparseCore 0:
  56.8 53.7 all-gather.7
  113.5 51.8 all-gather.5
  172.9 72.9 reduce-scatter.6
  265.6 88.7 all-gather.9
  366.9 72.5 all-gather.13
  441.8 69.3 all-gather.11
  514.5 59.8 reduce-scatter.12
  578.0 70.7 reduce-scatter.8
  799.3 81.0 reduce-scatter.10
where the time goes:
time: 898 us; the launch traced here: 887 us
  waiting for transfers between devices  450 us (50%)
  matrix products  258 us (29%)
  local copies, waits for them, and re-layouts  61.6 us (7%)
  blocking collectives  36.5 us (4%)
  other arithmetic  35.8 us (4%)
  loops' own time  15.8 us (2%)
  starting transfers between devices  14.9 us (2%)
  between operations  14.5 us (2%)
    dot_general x17, matrix products, contract_first(): lax.dot_general(left, right, (((0,), (0,)), ((), ())), preferred_element_...  107 us
    dot_general x17, matrix products, contract_last(): lax.dot_general(left, right, (((1,), (1,)), ((), ())), preferred_element_...  106 us
    all_gather x1, waiting for transfers between devices, body(): piece_rows = lax.all_gather(d_resid, 'exp', axis=0, tiled=True)  88.6 us
    reduce_scatter x1, waiting for transfers between devices, body(): lax.psum_scatter(dx_part.astype(jnp.bfloat16), 'ctx', scatter_dimension=1...  73 us
    all_gather x1, waiting for transfers between devices, body(): q_rows = lax.all_gather(queries, 'ctx', axis=0, tiled=True)  65.2 us
    reduce_scatter x1, waiting for transfers between devices, body(): lax.psum_scatter(dq_all.astype(jnp.bfloat16), 'ctx', scatter_dimension=0,...  64.9 us
    all_gather x1, waiting for transfers between devices, body(): lax.all_gather(mine_rows, 'ctx', axis=1, tiled=True)  52.4 us
    all_gather x1, waiting for transfers between devices, body(): lax.all_gather(mine_grads, 'ctx', axis=1, tiled=True)  50.8 us
  transfers between devices with their start and end apart: 12, of which 10 were waited for; matrix products, arithmetic and copies ran while one was open for 35% of the time, Pallas kernels for 0%

commit v1 on v0

v1 whole, which is shorter than its diff:
```python
import functools
import math

import jax
import jax.numpy as jnp
from jax import lax
from jax.experimental import pallas as pl
from jax.experimental.pallas import tpu as pltpu
from jax.sharding import PartitionSpec as P

MOST = 2
MESH = pl.DeviceIdType.MESH
LOG2E = 1.4426950408889634
BF = jnp.bfloat16
F32 = jnp.float32
VLIM = 56 * 1024 * 1024
VM = pltpu.VMEM


def activation(pre_act):
    sigmoid_val = jax.nn.sigmoid(pre_act)
    return (pre_act * sigmoid_val, sigmoid_val * (1.0 + pre_act * (1.0 - sigmoid_val)))


def contract_first(left, right):
    return lax.dot_general(left, right, (((0,), (0,)), ((), ())), preferred_element_type=F32)


def contract_last(left, right):
    return lax.dot_general(left, right, (((1,), (1,)), ((), ())), preferred_element_type=F32)


class Place:
    def __init__(self, axis):
        self.axis = axis
        me = lax.axis_index(axis)
        if axis == "ctx":
            step, span = 1, 4
        else:
            step, span = 2, 8
        low = lax.rem(me, step)
        pos = lax.rem(me // step, 4)
        row = me // span
        other = 1 - row

        def at(r, p):
            return r * span + lax.rem(p + 4, 4) * step + low

        self.me = me
        self.up, self.down, self.far = at(row, pos + 1), at(row, pos - 1), at(row, pos + 2)
        self.mate = at(other, pos)
        self.mate_up, self.mate_down = at(other, pos + 1), at(other, pos - 1)
        self.mate_far = at(other, pos + 2)


def greet(peers):
    barrier = pltpu.get_barrier_semaphore()
    for axis, dev in peers:
        pl.semaphore_signal(barrier, inc=1, device_id={axis: dev}, device_id_type=MESH)
    pl.semaphore_wait(barrier, len(peers))


class Lanes:
    def __init__(self, send_sems, recv_sems):
        self.send_sems, self.recv_sems, self.sent = send_sems, recv_sems, []

    def copy(self, k, src, dst, axis, dev):
        return pltpu.make_async_remote_copy(
            src_ref=src,
            dst_ref=dst,
            send_sem=self.send_sems.at[k],
            recv_sem=self.recv_sems.at[k],
            device_id={axis: dev},
            device_id_type=MESH,
        )

    def send(self, k, src, dst, axis, dev):
        one = self.copy(k, src, dst, axis, dev)
        one.start()
        self.sent.append(one)

    def recv(self, k, dst, axis, dev):
        self.copy(k, dst, dst, axis, dev).wait_recv()

    def finish(self):
        for one in self.sent:
            one.wait_send()


AG_LANES = 14


def gather_ring(pieces, place, lanes, base, arrived=None):
    axis = place.axis
    n = len(pieces)

    def send(k, block, half, dev):
        for i, piece in enumerate(pieces):
            lanes.send(base + k * n + i, piece(block, half), piece(block, half), axis, dev)

    def recv(k, block, half, dev):
        for i, piece in enumerate(pieces):
            lanes.recv(base + k * n + i, piece(block, half), axis, dev)
        if arrived is not None:
            arrived(k, block, half)

    p = place
    send(0, p.me, 0, p.mate)
    send(2, p.me, 0, p.up)
    send(4, p.me, 1, p.down)
    send(1, p.me, 1, p.mate)
    send(3, p.me, 1, p.up)
    send(5, p.me, 0, p.down)
    recv(2, p.down, 0, p.down)
    send(6, p.down, 0, p.up)
    recv(4, p.up, 1, p.up)
    send(7, p.up, 1, p.down)
    recv(0, p.mate, 0, p.mate)
    send(8, p.mate, 0, p.up)
    send(10, p.mate, 0, p.down)
    recv(1, p.mate, 1, p.mate)
    send(11, p.mate, 1, p.down)
    send(9, p.mate, 1, p.up)
    recv(8, p.mate_down, 0, p.down)
    send(12, p.mate_down, 0, p.up)
    recv(11, p.mate_up, 1, p.up)
    send(13, p.mate_up, 1, p.down)
    recv(3, p.down, 1, p.down)
    recv(5, p.up, 0, p.up)
    recv(6, p.far, 0, p.down)
    recv(7, p.far, 1, p.up)
    recv(10, p.mate_up, 0, p.up)
    recv(9, p.mate_down, 1, p.down)
    recv(12, p.mate_far, 0, p.down)
    recv(13, p.mate_far, 1, p.up)


def add_into(dst, *srcs):
    total = srcs[0][...].astype(F32)
    for src in srcs[1:]:
        total = total + src[...].astype(F32)
    dst[...] = total.astype(dst.dtype)


def scatter_ring(parts, place, lanes, base, bufs, outs):
    axis = place.axis
    n = len(parts)
    p = place
    groups = (
        (p.mate_far, p.mate_up, p.mate_down, p.mate),
        (p.far, p.up, p.down, p.me),
    )

    def slot(i, s):
        return bufs[i](s)

    def send(k, i, src, s, dev):
        lanes.send(base + k * n + i, src, slot(i, s), axis, dev)

    def recv(k, i, s, dev):
        lanes.recv(base + k * n + i, slot(i, s), axis, dev)

    every = range(n)
    for g, (far, up, down, own) in enumerate(groups):
        for i in every:
            send(6 * g + 0, i, parts[i](far, 0), 6 * g + 0, p.up)
            send(6 * g + 1, i, parts[i](far, 1), 6 * g + 1, p.down)
        for i in every:
            send(6 * g + 3, i, parts[i](up, 1), 6 * g + 3, p.up)
            send(6 * g + 4, i, parts[i](down, 0), 6 * g + 4, p.down)
        if g == 0:
            continue
    for g, (far, up, down, own) in enumerate(groups):
        for i in every:
            recv(6 * g + 0, i, 6 * g + 0, p.down)
            add_into(slot(i, 6 * g + 0), slot(i, 6 * g + 0), parts[i](up, 0))
            send(6 * g + 2, i, slot(i, 6 * g + 0), 6 * g + 2, p.up)
            recv(6 * g + 1, i, 6 * g + 1, p.up)
            add_into(slot(i, 6 * g + 1), slot(i, 6 * g + 1), parts[i](down, 1))
            send(6 * g + 5, i, slot(i, 6 * g + 1), 6 * g + 5, p.down)
    far, up, down, own = groups[0]
    for half in (1, 0):
        for i in every:
            recv(2 + half, i, 2 + half, p.down)
            recv(4 + half, i, 4 + half, p.up)
            add_into(slot(i, 2 + half), slot(i, 2 + half), slot(i, 4 + half), parts[i](own, half))
            send(12 + half, i, slot(i, 2 + half), 12 + half, p.mate)
    for half in (1, 0):
        for i in every:
            recv(8 + half, i, 8 + half, p.down)
            recv(10 + half, i, 10 + half, p.up)
            recv(12 + half, i, 12 + half, p.mate)
            add_into(
                outs[i](half),
                slot(i, 8 + half),
                slot(i, 10 + half),
                slot(i, 12 + half),
                parts[i](p.me, half),
            )


def around(place):
    return [(place.axis, place.up), (place.axis, place.down), (place.axis, place.mate)]


def dispatch_kernel(mi_ref, og_ref, pick_ref, place_ref, out_ref, send, got, ss, rs):
    ctx = Place("ctx")
    me = lax.axis_index("exp")
    n_exp = send.shape[0]
    peers = [("exp", lax.rem(me + d, n_exp)) for d in range(1, n_exp)]
    greet(peers + around(ctx))
    lanes = Lanes(ss, rs)
    rows = jnp.dot(pick_ref[:, :128], mi_ref[...], preferred_element_type=F32)
    rows = rows + jnp.dot(pick_ref[:, 128:], og_ref[...], preferred_element_type=F32)
    send[...] = rows.reshape(n_exp, 8, rows.shape[1]).astype(BF)
    for d in range(1, n_exp):
        to = lax.rem(me + d, n_exp)
        lanes.send(d - 1, send.at[to], got.at[d], "exp", to)
    got[0] = send[me]
    for d in range(1, n_exp):
        lanes.recv(d - 1, got.at[d], "exp", lax.rem(me + n_exp - d, n_exp))
    flat = got[...].astype(F32).reshape(n_exp * 8, got.shape[2]).astype(BF)
    mine = jnp.dot(place_ref[...], flat, preferred_element_type=F32).astype(BF)
    mine = mine.reshape(2, 2, 16, got.shape[2])
    for a in range(2):
        for k in range(2):
            out_ref[a, k, ctx.me] = mine[a, k]

    def piece(block, half):
        return out_ref.at[half, :, block]

    gather_ring([piece], ctx, lanes, n_exp - 1)
    lanes.finish()


def dispatch(moe_input, out_grad, pick, place):
    n_exp, n_ctx = lax.axis_size("exp"), lax.axis_size("ctx")
    width = moe_input.shape[1]
    n_sem = n_exp - 1 + AG_LANES
    return pl.pallas_call(
        dispatch_kernel,
        out_shape=jax.ShapeDtypeStruct((2, 2, n_ctx, 16, width), BF),
        in_specs=[pl.BlockSpec(memory_space=VM)] * 4,
        out_specs=pl.BlockSpec(memory_space=VM),
        scratch_shapes=[
            VM((n_exp, 8, width), BF),
            VM((n_exp, 8, width), BF),
            pltpu.SemaphoreType.DMA((n_sem,)),
            pltpu.SemaphoreType.DMA((n_sem,)),
        ],
        compiler_params=pltpu.CompilerParams(
            collective_id=1, has_side_effects=True, vmem_limit_bytes=VLIM
        ),
        cost_estimate=pl.CostEstimate(flops=10**9, bytes_accessed=150 * 10**6, transcendentals=0),
    )(moe_input, out_grad, pick, place)


def combine_kernel(part_ref, out_ref, buf, ss, rs):
    ctx, exp = Place("ctx"), Place("exp")
    twin = exp.me + 1 - 2 * lax.rem(exp.me, 2)
    greet(around(ctx) + around(exp) + [("exp", twin)])
    lanes = Lanes(ss, rs)
    scatter_ring(
        [lambda block, half: part_ref.at[half, block]],
        ctx,
        lanes,
        0,
        [lambda s: buf.at[s]],
        [lambda half: out_ref.at[exp.me, half]],
    )

    def piece(block, half):
        return out_ref.at[block, half]

    base = AG_LANES
    over = 2 * AG_LANES
    flip = 1 - 2 * lax.rem(exp.me, 2)
    for half in range(2):
        lanes.send(over + 14 + half, piece(exp.me, half), piece(exp.me, half), "exp", twin)

    def arrived(k, block, half):
        lanes.send(over + k, piece(block, half), piece(block, half), "exp", twin)

    gather_ring([piece], exp, lanes, base, arrived)
    srcs = {
        0: (exp.mate, 0), 1: (exp.mate, 1), 2: (exp.down, 0), 3: (exp.down, 1),
        4: (exp.up, 1), 5: (exp.up, 0), 6: (exp.far, 0), 7: (exp.far, 1),
        8: (exp.mate_down, 0), 9: (exp.mate_down, 1), 10: (exp.mate_up, 0),
        11: (exp.mate_up, 1), 12: (exp.mate_far, 0), 13: (exp.mate_far, 1),
        14: (exp.me, 0), 15: (exp.me, 1),
    }
    for k, (block, half) in srcs.items():
        lanes.recv(over + k, piece(block + flip, half), "exp", twin)
    lanes.finish()


def combine(part):
    n_exp = lax.axis_size("exp")
    rows, width = part.shape[2:]
    n_sem = 2 * AG_LANES + 16
    return pl.pallas_call(
        combine_kernel,
        out_shape=jax.ShapeDtypeStruct((n_exp, 2, rows, width), BF),
        in_specs=[pl.BlockSpec(memory_space=VM)],
        out_specs=pl.BlockSpec(memory_space=VM),
        scratch_shapes=[
            VM((14, rows, width), BF),
            pltpu.SemaphoreType.DMA((n_sem,)),
            pltpu.SemaphoreType.DMA((n_sem,)),
        ],
        compiler_params=pltpu.CompilerParams(
            collective_id=2, has_side_effects=True, vmem_limit_bytes=VLIM
        ),
        cost_estimate=pl.CostEstimate(flops=10**8, bytes_accessed=120 * 10**6, transcendentals=0),
    )(part)


def spread_kernel(do_ref, delta_ref, do_all, delta_all, ss, rs):
    ctx = Place("ctx")
    greet(around(ctx))
    lanes = Lanes(ss, rs)
    do_all[ctx.me] = do_ref[...]
    delta_all[ctx.me] = delta_ref[...]
    rows = do_ref.shape[0] // 2

    def piece_do(block, half):
        return do_all.at[block, pl.ds(half * rows, rows)]

    def piece_delta(block, half):
        return delta_all.at[block, :, pl.ds(half * rows, rows)]

    gather_ring([piece_do, piece_delta], ctx, lanes, 0)
    lanes.finish()


def spread(d_out, delta):
    n_ctx = lax.axis_size("ctx")
    n_sem = 2 * AG_LANES
    return pl.pallas_call(
        spread_kernel,
        out_shape=(
            jax.ShapeDtypeStruct((n_ctx,) + d_out.shape, BF),
            jax.ShapeDtypeStruct((n_ctx,) + delta.shape, F32),
        ),
        in_specs=[pl.BlockSpec(memory_space=VM)] * 2,
        out_specs=(pl.BlockSpec(memory_space=VM),) * 2,
        scratch_shapes=[
            pltpu.SemaphoreType.DMA((n_sem,)),
            pltpu.SemaphoreType.DMA((n_sem,)),
        ],
        compiler_params=pltpu.CompilerParams(
            collective_id=3, has_side_effects=True, vmem_limit_bytes=VLIM
        ),
        cost_estimate=pl.CostEstimate(flops=10**6, bytes_accessed=120 * 10**6, transcendentals=0),
    )(d_out, delta)


def settle_kernel(dq_ref, dw_ref, dq_out, dw_out, dq_buf, dw_buf, ss, rs):
    ctx = Place("ctx")
    greet(around(ctx))
    lanes = Lanes(ss, rs)
    rows_q, rows_w = dq_ref.shape[1] // 2, dw_ref.shape[1] // 2
    scatter_ring(
        [
            lambda block, half: dq_ref.at[block, pl.ds(half * rows_q, rows_q)],
            lambda block, half: dw_ref.at[block, pl.ds(half * rows_w, rows_w)],
        ],
        ctx,
        lanes,
        0,
        [lambda s: dq_buf.at[s], lambda s: dw_buf.at[s]],
        [
            lambda half: dq_out.at[pl.ds(half * rows_q, rows_q)],
            lambda half: dw_out.at[pl.ds(half * rows_w, rows_w)],
        ],
    )
    lanes.finish()


def settle_grads(dq, dw):
    n_sem = 2 * AG_LANES
    return pl.pallas_call(
        settle_kernel,
        out_shape=(
            jax.ShapeDtypeStruct(dq.shape[1:], BF),
            jax.ShapeDtypeStruct(dw.shape[1:], BF),
        ),
        in_specs=[pl.BlockSpec(memory_space=VM)] * 2,
        out_specs=(pl.BlockSpec(memory_space=VM),) * 2,
        scratch_shapes=[
            VM((14, dq.shape[1] // 2, dq.shape[2]), BF),
            VM((14, dw.shape[1] // 2, dw.shape[2]), BF),
            pltpu.SemaphoreType.DMA((n_sem,)),
            pltpu.SemaphoreType.DMA((n_sem,)),
        ],
        compiler_params=pltpu.CompilerParams(
            collective_id=4, has_side_effects=True, vmem_limit_bytes=VLIM
        ),
        cost_estimate=pl.CostEstimate(flops=10**7, bytes_accessed=120 * 10**6, transcendentals=0),
    )(dq, dw)


CHUNK = 1024
TILE = 512


def attention_kernel(
    scale, n_chunk, k_ref, v_ref, q_ref, do_ref, lse_ref, delta_ref,
    dq_ref, dk_ref, dv_ref, dk_acc, dv_acc, dq_acc,
):
    i = pl.program_id(0)
    c = lax.axis_index("ctx")
    first = jnp.where(lax.rem(c, 2) == 0, c, n_chunk - 1 - c)
    ids = (first, n_chunk - 1 - first)

    @pl.when(i == 0)
    def _():
        dk_acc[...] = jnp.zeros_like(dk_acc)
        dv_acc[...] = jnp.zeros_like(dv_acc)

    dq_acc[...] = jnp.zeros_like(dq_acc)

    def tile(part, row, key, key_len, masked):
        q = q_ref[pl.ds(row, TILE), :]
        do = do_ref[0, pl.ds(row, TILE), :]
        lse = lse_ref[:, pl.ds(row, TILE)] * LOG2E
        delta = delta_ref[0, :, pl.ds(row, TILE)]
        k = k_ref[part, pl.ds(key, key_len), :]
        v = v_ref[part, pl.ds(key, key_len), :]
        s = contract_last(k, q) * (scale * LOG2E) - lse
        if masked:
            rk = lax.broadcasted_iota(jnp.int32, s.shape, 0)
            cq = lax.broadcasted_iota(jnp.int32, s.shape, 1)
            s = jnp.where(rk <= cq, s, -1e30)
        p = jnp.exp2(s)
        dp = contract_last(v, do)
        ds = (p * (dp - delta)).astype(BF)
        dv_acc[part, pl.ds(key, key_len), :] += jnp.dot(
            p.astype(BF), do, preferred_element_type=F32
        )
        dk_acc[part, pl.ds(key, key_len), :] += jnp.dot(ds, q, preferred_element_type=F32)
        dq_acc[pl.ds(row, TILE), :] += contract_first(ds, k)

    for part in range(2):

        @pl.when(i > ids[part])
        def _(part=part):
            for row in range(0, CHUNK, TILE):
                for key in range(0, CHUNK, TILE):
                    tile(part, row, key, TILE, False)

        @pl.when(i == ids[part])
        def _(part=part):
            for row in range(0, CHUNK, TILE):
                for key in range(0, row + 1, TILE):
                    tile(part, row, key, TILE, key == row)

    dq_ref[...] = (dq_acc[...] * scale).astype(BF)

    @pl.when(i == n_chunk - 1)
    def _():
        dk_ref[...] = (dk_acc[...] * scale).astype(BF)
        dv_ref[...] = dv_acc[...].astype(BF)


def attention(k, v, q_all, do_all, lse, delta_all, scale):
    total, head = q_all.shape
    n_chunk = total // CHUNK
    per = do_all.shape[1] // CHUNK
    whole = pl.BlockSpec((2, CHUNK, head), lambda i: (0, 0, 0))
    return pl.pallas_call(
        functools.partial(attention_kernel, scale, n_chunk),
        grid=(n_chunk,),
        out_shape=(
            jax.ShapeDtypeStruct((total, head), BF),
            jax.ShapeDtypeStruct(k.shape, BF),
            jax.ShapeDtypeStruct(v.shape, BF),
        ),
        in_specs=[
            whole,
            whole,
            pl.BlockSpec((CHUNK, head), lambda i: (i, 0)),
            pl.BlockSpec((1, CHUNK, head), lambda i: (i // per, i % per, 0)),
            pl.BlockSpec((1, CHUNK), lambda i: (0, i)),
            pl.BlockSpec((1, 1, CHUNK), lambda i: (i // per, 0, i % per)),
        ],
        out_specs=(pl.BlockSpec((CHUNK, head), lambda i: (i, 0)), whole, whole),
        scratch_shapes=[
            VM((2, CHUNK, head), F32),
            VM((2, CHUNK, head), F32),
            VM((CHUNK, head), F32),
        ],
        compiler_params=pltpu.CompilerParams(
            dimension_semantics=("arbitrary",), vmem_limit_bytes=VLIM
        ),
        cost_estimate=pl.CostEstimate(
            flops=40 * 10**9, bytes_accessed=20 * 10**6, transcendentals=17 * 10**6
        ),
    )(k, v, q_all, do_all, lse, delta_all)


def body(
    moe_input,
    out_grad,
    w_gate,
    w_up,
    w_down,
    expert_picks,
    gate_probs,
    queries,
    attn_keys,
    values,
    attn_out,
    log_norm,
    w_out,
):
    n_ctx = lax.axis_size("ctx")
    n_exp = lax.axis_size("exp")
    ctx_id = lax.axis_index("ctx")
    exp_id = lax.axis_index("exp")
    tok_dev, feat_width = moe_input.shape
    n_local = w_gate.shape[0]
    group_picks = expert_picks.shape[1] // n_ctx
    tok_ctx, head_dim = queries.shape
    key_scale = head_dim ** (-0.5)
    i32 = jnp.int32

    og_all = lax.all_gather(out_grad, "exp", axis=0, tiled=True)
    q_all = lax.all_gather(queries, "ctx", axis=0, tiled=True)

    half = tok_ctx // 2
    top = 2 * n_ctx - 1
    to_even = [(g, 2 * g if g < n_ctx // 2 else top - 2 * g) for g in range(n_ctx)]
    to_odd = [(g, 2 * g + 1 if g < n_ctx // 2 else top - 1 - 2 * g) for g in range(n_ctx)]
    kv = jnp.stack([attn_keys, values])
    kv_first = lax.ppermute(kv[:, :half], "ctx", to_even)
    kv_second = lax.ppermute(kv[:, half:], "ctx", to_odd)
    k_dealt = jnp.stack([kv_first[0], kv_second[0]])
    v_dealt = jnp.stack([kv_first[1], kv_second[1]])

    base_row = (ctx_id * n_exp + exp_id) * tok_dev
    below = jnp.sum((expert_picks < base_row).astype(i32), axis=1, keepdims=True)
    inside = (expert_picks >= base_row) & (expert_picks < base_row + tok_dev)
    spot = jnp.arange(expert_picks.shape[1], dtype=i32)[None, :] - below
    local = expert_picks - base_row
    chosen = jnp.stack(
        [jnp.sum(jnp.where(inside & (spot == s), local + 1, 0), axis=1) - 1 for s in range(MOST)],
        axis=1,
    )
    chosen = chosen.reshape(n_exp, n_local * MOST)
    away = jnp.full_like(chosen, -1)
    columns = jnp.arange(2 * tok_dev, dtype=i32)
    wanted = jnp.stack(
        [chosen, jnp.where(chosen >= 0, chosen + tok_dev, away)], axis=1
    ).reshape(-1)
    pick = (wanted[:, None] == columns[None, :]).astype(BF)

    my_picks = lax.dynamic_slice(
        expert_picks, (exp_id * n_local, ctx_id * group_picks), (n_local, group_picks)
    )
    block_of = my_picks // tok_dev
    src_exp = block_of - ctx_id * n_exp
    slot_rank = jnp.arange(group_picks, dtype=i32)[None, :] - jnp.sum(
        (my_picks[:, None, :] < (block_of * tok_dev)[:, :, None]).astype(i32), axis=2
    )
    dist = lax.rem(exp_id - src_exp + n_exp, n_exp)
    spot_x = dist * 8 + jnp.arange(n_local, dtype=i32)[:, None] * MOST + slot_rank
    spots = jnp.stack([spot_x, spot_x + n_local * MOST]).reshape(-1)
    place = (spots[:, None] == jnp.arange(8 * n_exp, dtype=i32)[None, :]).astype(BF)

    slots = dispatch(moe_input, out_grad, pick, place)
    slots = slots.reshape(2, n_local, n_ctx * group_picks, feat_width)
    slot_rows, slot_grads = slots[0], slots[1]

    gate_rows = lax.dynamic_slice_in_dim(gate_probs, exp_id * n_local, n_local, 0)
    pre_gate = jnp.einsum("kcd,kdf->kcf", slot_rows, w_gate, preferred_element_type=F32)
    pre_up = jnp.einsum("kcd,kdf->kcf", slot_rows, w_up, preferred_element_type=F32)
    gated_act, act_slope = activation(pre_gate)
    hidden_full = gated_act * pre_up
    hidden = hidden_full.astype(BF)
    down_back = jnp.einsum("kcd,kfd->kcf", slot_grads, w_down, preferred_element_type=F32)
    gate_part = jnp.sum(down_back * hidden_full, axis=2).astype(BF)
    scaled = gate_rows[..., None] * down_back
    d_gate = (scaled * pre_up * act_slope).astype(BF)
    d_up = (scaled * gated_act).astype(BF)
    dx_part = (
        jnp.einsum("kcf,kdf->kcd", d_gate, w_gate, preferred_element_type=F32)
        + jnp.einsum("kcf,kdf->kcd", d_up, w_up, preferred_element_type=F32)
    ).astype(BF)
    d_gates = lax.psum_scatter(gate_part, "ctx", scatter_dimension=1, tiled=True).astype(F32)

    dx_all = combine(dx_part.reshape(n_local, n_ctx, group_picks, feat_width))
    dx_all = dx_all.reshape(-1, feat_width)

    weighted = (gate_rows[..., None] * slot_grads.astype(F32)).astype(BF)
    dw_down = jnp.einsum("kcf,kcd->kfd", hidden, weighted, preferred_element_type=F32).astype(BF)
    dw_gate = jnp.einsum("kcd,kcf->kdf", slot_rows, d_gate, preferred_element_type=F32).astype(BF)
    dw_up = jnp.einsum("kcd,kcf->kdf", slot_rows, d_up, preferred_element_type=F32).astype(BF)

    group_ids = lax.dynamic_slice_in_dim(
        expert_picks, ctx_id * group_picks, group_picks, 1
    ).reshape(-1) - ctx_id * tok_ctx
    spread_hot = (jnp.arange(tok_ctx, dtype=i32)[:, None] == group_ids[None, :]).astype(BF)
    own_hot = (
        (jnp.arange(tok_dev, dtype=i32) + exp_id * tok_dev)[:, None] == group_ids[None, :]
    ).astype(BF)
    d_resid = (
        out_grad.astype(F32) + jnp.dot(own_hot, dx_all, preferred_element_type=F32)
    ).astype(BF)

    d_out_base = contract_last(og_all, w_out)
    dx_out = contract_last(dx_all, w_out).astype(BF)
    d_out = (d_out_base + jnp.dot(spread_hot, dx_out, preferred_element_type=F32)).astype(BF)
    product = d_out.astype(F32) * attn_out.astype(F32)
    delta = lax.dot_general(
        jnp.ones((1, head_dim), F32), product, (((1,), (1,)), ((), ())),
        precision=lax.Precision.HIGHEST, preferred_element_type=F32,
    )
    do_all, delta_all = spread(d_out, delta)

    dq, dk, dv = attention(k_dealt, v_dealt, q_all, do_all, log_norm, delta_all, key_scale)

    out_taken = contract_first(spread_hot, attn_out).astype(BF)
    dw_part = contract_first(attn_out, og_all) + contract_first(out_taken, dx_all)
    dw_part = dw_part.astype(BF).reshape(head_dim, n_ctx, -1).transpose(1, 0, 2)

    back = jnp.stack([dk, dv], axis=1)
    from_even = [(b, a) for a, b in to_even]
    from_odd = [(b, a) for a, b in to_odd]
    kv_low = lax.ppermute(back[0], "ctx", from_even)
    kv_high = lax.ppermute(back[1], "ctx", from_odd)
    grad_kv = jnp.concatenate([kv_low, kv_high], axis=1)
    grad_q, dw_out = settle_grads(dq.reshape(n_ctx, tok_ctx, head_dim), dw_part)
    return (
        d_resid, dw_gate, dw_up, dw_down, d_gates, dw_out, grad_q, grad_kv[0], grad_kv[1],
    )


def solution(mesh):
    return jax.shard_map(
        body,
        mesh=mesh,
        in_specs=(
            P(("ctx", "exp"), None),
            P(("ctx", "exp"), None),
            P("exp", None, "ctx"),
            P("exp", None, "ctx"),
            P("exp", "ctx", None),
            P(),
            P(),
            P("ctx", "exp"),
            P("ctx", "exp"),
            P("ctx", "exp"),
            P("ctx", "exp"),
            P("exp", None),
            P("exp", None),
        ),
        out_specs=(
            P(("ctx", "exp"), None),
            P("exp", None, "ctx"),
            P("exp", None, "ctx"),
            P("exp", "ctx", None),
            P("exp", "ctx"),
            P("exp", "ctx"),
            P("ctx", "exp"),
            P("ctx", "exp"),
            P("ctx", "exp"),
        ),
        check_vma=False,
    )
```

time: 898 us -> 445 us (0.50)
  waiting for transfers between devices: 450 us -> 23.8 us
  Pallas kernels: 0 us -> 305 us
  matrix products: 258 us -> 45.6 us
  local copies, waits for them, and re-layouts: 61.6 us -> 19.3 us
  blocking collectives: 36.5 us -> 0 us
  other arithmetic: 35.8 us -> 10.5 us
  loops' own time: 15.8 us -> 0 us
    pallas_call x0 -> x5, Pallas kernels: none -> 305 us  [the longest x1 78 us: combine(): pl.pallas_call(combine_kernel, out_shape=jax.ShapeDtypeStruct((n_exp, 2,...]
    all_gather x5 -> x2, waiting for transfers between devices: 282 us -> 0.03 us  [the longest x1 0.03 us: body(): q_all = lax.all_gather(queries, 'ctx', axis=0, tiled=True)]
    reduce_scatter x3 -> x0, waiting for transfers between devices: 138 us -> none  [the longest x1 73 us: body(): lax.psum_scatter(dx_part.astype(jnp.bfloat16), 'ctx', scatter_dimension=1...]
    dot_general x17 -> x1, matrix products: 106 us -> 9.28 us  [contract_last(): lax.dot_general(left, right, (((1,), (1,)), ((), ())), preferred_element_...]
    dot_general x17 -> x2, matrix products: 107 us -> 13.8 us  [contract_first(): lax.dot_general(left, right, (((0,), (0,)), ((), ())), preferred_element_...]
    all_gather x1 -> x0, blocking collectives: 36.5 us -> none  [body(): delta_all = lax.all_gather(row_delta, 'ctx', axis=0, tiled=True)]
    all_to_all x3 -> x0, waiting for transfers between devices: 28.5 us -> none  [the longest x1 10.5 us: body(): lax.all_to_all(send_grads.reshape(n_exp, n_local, slot_count, feat_width)...]
    add x17 -> x1, other arithmetic: 23.7 us -> 0.01 us  [body(): jnp.arange(tok_dev, dtype=i32) + exp_id * tok_dev]
  transfers between devices with their start and end apart: 12 -> 7, of which waited for: 10 -> 1; matrix products, arithmetic and copies ran while one was open for 35% -> 12% of each run, Pallas kernels for 0% -> 43%
where the time goes in v1:
time: 445 us; the launch traced here: 438 us
  Pallas kernels  305 us (69%)
  matrix products  45.6 us (10%)
  waiting for transfers between devices  23.8 us (5%)
  local copies, waits for them, and re-layouts  19.3 us (4%)
  starting transfers between devices  18.7 us (4%)
  between operations  15.8 us (4%)
  other arithmetic  10.5 us (2%)
    pallas_call x1, Pallas kernels, combine(): pl.pallas_call(combine_kernel, out_shape=jax.ShapeDtypeStruct((n_exp, 2,...  78 us
    pallas_call x1, Pallas kernels, dispatch(): pl.pallas_call(dispatch_kernel, out_shape=jax.ShapeDtypeStruct((2, 2, n_c...  62.6 us
    pallas_call x1, Pallas kernels, spread(): pl.pallas_call(spread_kernel, out_shape=(jax.ShapeDtypeStruct((n_ctx,) +...  60.2 us
    pallas_call x1, Pallas kernels, attention(): pl.pallas_call(functools.partial(attention_kernel, scale, n_chunk), grid=...  53.6 us
    pallas_call x1, Pallas kernels, settle_grads(): pl.pallas_call(settle_kernel, out_shape=(jax.ShapeDtypeStruct(dq.shape[1:...  50.2 us
    unnamed x4, waiting for transfers between devices  23.7 us
    dot_general x2, matrix products, contract_first(): lax.dot_general(left, right, (((0,), (0,)), ((), ())), preferred_element_...  13.8 us
    dot_general x1, matrix products, contract_last(): lax.dot_general(left, right, (((1,), (1,)), ((), ())), preferred_element_...  9.28 us
  transfers between devices with their start and end apart: 7, of which 1 were waited for; matrix products, arithmetic and copies ran while one was open for 12% of the time, Pallas kernels for 43%

profile of v1, /device:TPU:0, one launch (start us, length us, event | category | flops | bytes accessed | tf_op | source)
XLA Modules:
  0.0 438.3 jit_solution(7835816241147008973)
XLA Ops:
  13.5 62.6 %shard_map.196 = bf16[2,2,8,16,4096]{4,3,2,1,0:T(8,128)(2,1)} custom-call(bf16[128,4096]{1,0:T(8,128)(2,1)} %mi_ref.1, bf16[128,4096]{1,0:T(8,128)(2,1)} %og_ref.1, bf16[128,256]{1,0:T(8,128)(2,1)} %fusion.23.pick_ref, bf16[64,128]{1,0:T(8,128)(2,1)} %fusion.26.place_ref), custom_call_target="tpu_custom_call" | custom-call | flops 1000000000 | bytes 150000000 | tf_op jit(solution)/shard_map/pallas_call | solution.py:240
  76.1 2.7 fusion.39
  80.0 2.2 copy-done.5
  86.9 2.2 fusion.17
  89.1 5.3 %collective-permute-start = (bf16[2,1024,128]{2,1,0:T(8,128)(2,1)}, bf16[2,1024,128]{2,1,0:T(8,128)(2,1)}, u32[]{:S(2)}, u32[]{:S(2)}) collective-permute-start(bf16[2,1024,128]{2,1,0:T(8,128)(2,1)} %get-tuple-element.36), channel_id=1, source_target_pairs={{0,0},{16,32},{32,64},{48,96},{64,112},{80,80},{96,48},{112,16},{1... | collective-permute-start | bytes 1572872 | tf_op jit(solution)/shard_map/ppermute | solution.py:536
  96.5 2.1 fusion
  98.6 78.0 %shard_map.197 = bf16[16,2,16,4096]{3,2,1,0:T(8,128)(2,1)} custom-call(bf16[2,8,16,4096]{3,2,1,0:T(8,128)(2,1)} %bitcast.63), custom_call_target="tpu_custom_call" | custom-call | flops 100000000 | bytes 120000000 | tf_op jit(solution)/shard_map/pallas_call | solution.py:301
  176.6 2.6 convolution_convert_fusion.2
  180.2 1.8 fusion.1
  182.0 2.5 convolution_convert_fusion.1
  184.4 2.5 convolution_convert_fusion
  186.9 22.7 %reduce-scatter.4.cloned.1.call-done = bf16[16,2]{1,0:T(8,128)(2,1)} async-done(((bf16[128,2]{1,0:T(8,128)(2,1)}), bf16[16,2]{1,0:T(8,128)(2,1)}) %reduce-scatter.4.cloned.1.call-update) | async-done | bytes 80
  214.2 9.3 %fusion.45 = f32[2048,128]{1,0:T(8,128)} fusion(bf16[2048,4096]{1,0:T(8,128)(2,1)} %all-gather.5.cloned.1.call-done, bf16[128,4096]{1,0:T(8,128)(2,1)S(1)} %copy-done.16), kind=kOutput, calls=%fused_computation.95 | convolution fusion | flops 2147483648 | bytes 18874368 | tf_op jit(solution)/shard_map/dot_general | solution.py:30
  223.5 5.8 %fusion.6.do_ref = bf16[2048,128]{1,0:T(8,128)(2,1)S(1)} fusion(f32[2048,128]{1,0:T(8,128)} %fusion.45, s32[512]{0:T(512)S(1)} %sub.71, bf16[512,4096]{1,0:T(8,128)(2,1)} %bitcast.58, bf16[128,4096]{1,0:T(8,128)(2,1)S(1)} %copy-done.16), kind=kOutput, calls=%fused_computation.14 | convolution fusion | flops 806944768 | bytes 6817792 | tf_op jit(solution)/shard_map/dot_general | solution.py:613
  229.3 1.6 fusion.11.delta_ref
  230.9 60.2 %shard_map.198 = (bf16[8,2048,128]{2,1,0:T(8,128)(2,1)}, f32[8,1,2048]{2,1,0:T(1,128)}) custom-call(bf16[2048,128]{1,0:T(8,128)(2,1)} %copy-done.11, f32[1,2048]{1,0:T(1,128)} %fusion.11.delta_ref), custom_call_target="tpu_custom_call" | custom-call | flops 1000000 | bytes 120000000 | tf_op jit(solution)/shard_map/pallas_call | solution.py:339
  291.1 53.6 %shard_map.199 = (bf16[16384,128]{1,0:T(8,128)(2,1)}, bf16[2,1024,128]{2,1,0:T(8,128)(2,1)}, bf16[2,1024,128]{2,1,0:T(8,128)(2,1)}) custom-call(bf16[2,1024,128]{2,1,0:T(8,128)(2,1)} %get-tuple-element.47.k_ref, bf16[2,1024,128]{2,1,0:T(8,128)(2,1)} %get-tuple-element.48.v_ref, bf16[16384,128]{1,0:T(8,128)(2,1)} %all-gather.3.cloned.1.call-done.q_ref, ...), custom_call_target="tpu_custom_call" | custom-call | flops 40000000000 | bytes 20000000 | tf_op jit(solution)/shard_map/pallas_call | solution.py:471
  344.7 2.2 fusion.18
  346.9 7.9 %collective-permute-start.3 = (bf16[2,1024,128]{2,1,0:T(8,128)(2,1)}, bf16[2,1024,128]{2,1,0:T(8,128)(2,1)S(1)}, u32[]{:S(2)}, u32[]{:S(2)}) collective-permute-start(bf16[2,1024,128]{2,1,0:T(8,128)(2,1)} %get-tuple-element.34), channel_id=1, source_target_pairs={{16,0},{48,16},{80,32},{112,48},{96,64},{64,80},{32,96},{0,112},{1... | collective-permute-start | bytes 1572872 | tf_op jit(solution)/shard_map/ppermute | solution.py:631
  354.8 5.3 %collective-permute-start.2 = (bf16[2,1024,128]{2,1,0:T(8,128)(2,1)}, bf16[2,1024,128]{2,1,0:T(8,128)(2,1)}, u32[]{:S(2)}, u32[]{:S(2)}) collective-permute-start(bf16[2,1024,128]{2,1,0:T(8,128)(2,1)} %get-tuple-element.35), channel_id=1, source_target_pairs={{0,0},{32,16},{64,32},{96,48},{112,64},{80,80},{48,96},{16,112},{1... | collective-permute-start | bytes 1572872 | tf_op jit(solution)/shard_map/ppermute | solution.py:630
  360.2 8.1 %fusion.46 = f32[128,4096]{1,0:T(8,128)S(1)} fusion(bf16[2048,128]{1,0:T(8,128)(2,1)S(1)} %copy-done.10, bf16[2048,4096]{1,0:T(8,128)(2,1)} %all-gather.5.cloned.1.call-done), kind=kOutput, calls=%fused_computation.96 | convolution fusion | flops 2147483648 | bytes 19398656 | tf_op jit(solution)/shard_map/dot_general | solution.py:26
  368.3 5.6 %fusion.2 = bf16[128,4096]{1,0:T(8,128)(2,1)} fusion(f32[128,4096]{1,0:T(8,128)S(1)} %fusion.46, bf16[512,4096]{1,0:T(8,128)(2,1)} %bitcast.59, bf16[2048,128]{1,0:T(8,128)(2,1)S(1)} %copy-done.10, s32[512]{0:T(512)S(1)} %sub.71), kind=kOutput, calls=%fused_computation.8 | convolution fusion | flops 807469056 | bytes 7866368 | tf_op jit(solution)/shard_map/dot_general | solution.py:26
  374.0 1.6 copy.39
  376.9 50.2 %shard_map.200 = (bf16[2048,128]{1,0:T(8,128)(2,1)}, bf16[128,512]{1,0:T(8,128)(2,1)}) custom-call(bf16[8,2048,128]{2,1,0:T(8,128)(2,1)} %bitcast.64, bf16[8,128,512]{2,1,0:T(8,128)(2,1)} %bitcast.65), custom_call_target="tpu_custom_call" | custom-call | flops 10000000 | bytes 120000000 | tf_op jit(solution)/shard_map/pallas_call | solution.py:382
  (84 shorter events, 23.7 us)
Async XLA Ops:
  8.0 70.9 %copy-start = (bf16[2,4096,176]{1,2,0:T(8,128)(2,1)S(1)}, bf16[2,4096,176]{1,2,0:T(8,128)(2,1)}, u32[]{:S(2)}) copy-start(bf16[2,4096,176]{1,2,0:T(8,128)(2,1)} %param.15) | copy-start | bytes 8650756
  8.0 201.6 %reduce-scatter.4.cloned.1.call-start = ((), (), s32[]{:S(2)}) async-start(), calls=%async_computation.3 | async-start | bytes 36864
  78.8 4.3 copy-start.2
  78.9 4.3 copy-start.8
  78.9 3.3 copy-start.5
  82.2 1.8 copy-start.15
  85.0 9.5 %copy-start.13 = (s32[32,128]{1,0:T(8,128)S(1)}, s32[32,128]{1,0:T(8,128)}, u32[]{:S(2)}) copy-start(s32[32,128]{1,0:T(8,128)} %param.18) | copy-start | bytes 49156
  85.7 128.4 %all-gather.5.cloned.1.call-start = ((), (), s32[]{:S(2)}) async-start(), calls=%async_computation.2 | async-start | bytes 17825792 | tf_op jit(solution)/shard_map/all_gather | solution.py:528
  86.3 204.8 %all-gather.3.cloned.1.call-start = ((), (), s32[]{:S(2)}) async-start(), calls=%async_computation.1 | async-start | bytes 4718592 | tf_op jit(solution)/shard_map/all_gather | solution.py:529
  89.1 121.8 %collective-permute-start = (bf16[2,1024,128]{2,1,0:T(8,128)(2,1)}, bf16[2,1024,128]{2,1,0:T(8,128)(2,1)}, u32[]{:S(2)}, u32[]{:S(2)}) collective-permute-start(bf16[2,1024,128]{2,1,0:T(8,128)(2,1)} %get-tuple-element.36), channel_id=1, source_target_pairs={{0,0},{16,32},{32,64},{48,96},{64,112},{80,80},{96,48},{112,16},{1... | collective-permute-start | bytes 1572872 | tf_op jit(solution)/shard_map/ppermute | solution.py:536
  94.5 117.5 %collective-permute-start.1 = (bf16[2,1024,128]{2,1,0:T(8,128)(2,1)}, bf16[2,1024,128]{2,1,0:T(8,128)(2,1)}, u32[]{:S(2)}, u32[]{:S(2)}) collective-permute-start(bf16[2,1024,128]{2,1,0:T(8,128)(2,1)} %get-tuple-element.37), channel_id=1, source_target_pairs={{0,16},{16,48},{32,80},{48,112},{64,96},{80,64},{96,32},{112,0},{1... | collective-permute-start | bytes 1572872 | tf_op jit(solution)/shard_map/ppermute | solution.py:537
  94.6 1.8 copy-start.6
  98.6 78.1 %copy-start.9 = (bf16[1,2,8,16,4096]{4,3,2,1,0:T(8,128)(2,1)S(1)}, bf16[1,2,8,16,4096]{4,3,2,1,0:T(8,128)(2,1)}, u32[]{:S(2)}) copy-start(bf16[1,2,8,16,4096]{4,3,2,1,0:T(8,128)(2,1)} %copy-done.8) | copy-start | bytes 6291460
  176.6 2.7 copy-start.4
  176.6 3.5 copy-start.7
  180.2 1.8 copy-start.3
  186.9 27.2 %copy-start.16 = (bf16[128,4096]{1,0:T(8,128)(2,1)S(1)}, bf16[128,4096]{1,0:T(8,128)(2,1)}, u32[]{:S(2)}) copy-start(bf16[128,4096]{1,0:T(8,128)(2,1)} %param.25) | copy-start | bytes 3145732
  223.5 5.8 %copy-start.10 = (bf16[2048,128]{1,0:T(8,128)(2,1)S(1)}, bf16[2048,128]{1,0:T(8,128)(2,1)}, u32[]{:S(2)}) copy-start(bf16[2048,128]{1,0:T(8,128)(2,1)} %param.23) | copy-start | bytes 1572868
  229.3 1.6 copy-start.11
  346.9 81.3 %collective-permute-start.3 = (bf16[2,1024,128]{2,1,0:T(8,128)(2,1)}, bf16[2,1024,128]{2,1,0:T(8,128)(2,1)S(1)}, u32[]{:S(2)}, u32[]{:S(2)}) collective-permute-start(bf16[2,1024,128]{2,1,0:T(8,128)(2,1)} %get-tuple-element.34), channel_id=1, source_target_pairs={{16,0},{48,16},{80,32},{112,48},{96,64},{64,80},{32,96},{0,112},{1... | collective-permute-start | bytes 1572872 | tf_op jit(solution)/shard_map/ppermute | solution.py:631
  354.8 72.3 %collective-permute-start.2 = (bf16[2,1024,128]{2,1,0:T(8,128)(2,1)}, bf16[2,1024,128]{2,1,0:T(8,128)(2,1)}, u32[]{:S(2)}, u32[]{:S(2)}) collective-permute-start(bf16[2,1024,128]{2,1,0:T(8,128)(2,1)} %get-tuple-element.35), channel_id=1, source_target_pairs={{0,0},{32,16},{64,32},{96,48},{112,64},{80,80},{48,96},{16,112},{1... | collective-permute-start | bytes 1572872 | tf_op jit(solution)/shard_map/ppermute | solution.py:630
  376.9 53.9 %copy-start.1 = (bf16[2,4096,176]{1,2,0:T(8,128)(2,1)S(1)}, bf16[2,4096,176]{1,2,0:T(8,128)(2,1)}, u32[]{:S(2)}) copy-start(bf16[2,4096,176]{1,2,0:T(8,128)(2,1)} %param.15) | copy-start | bytes 8650756
  427.1 2.3 copy-start.14
  427.1 2.9 copy-start.12
Sparse Core Ops, SparseCore 0:
  85.9 123.7 reduce-scatter.3
Sparse Core Ops, SparseCore 1:
  87.9 107.5 all-gather.4
  197.7 93.2 all-gather.2

commit v2 on v1

--- a/solution.py
+++ b/solution.py
@@ -90,9 +90,14 @@
 AG_LANES = 14
 
 
-def gather_ring(pieces, place, lanes, base, arrived=None):
+def gather_ring(pieces, place, lanes, base, arrived=None, work=()):
     axis = place.axis
     n = len(pieces)
+    work = list(work)
+
+    def fill():
+        if work:
+            work.pop(0)()
 
     def send(k, block, half, dev):
         for i, piece in enumerate(pieces):
@@ -111,20 +116,26 @@
     send(1, p.me, 1, p.mate)
     send(3, p.me, 1, p.up)
     send(5, p.me, 0, p.down)
+    fill()
     recv(2, p.down, 0, p.down)
     send(6, p.down, 0, p.up)
     recv(4, p.up, 1, p.up)
     send(7, p.up, 1, p.down)
+    fill()
     recv(0, p.mate, 0, p.mate)
     send(8, p.mate, 0, p.up)
     send(10, p.mate, 0, p.down)
+    fill()
     recv(1, p.mate, 1, p.mate)
     send(11, p.mate, 1, p.down)
     send(9, p.mate, 1, p.up)
+    fill()
     recv(8, p.mate_down, 0, p.down)
     send(12, p.mate_down, 0, p.up)
     recv(11, p.mate_up, 1, p.up)
     send(13, p.mate_up, 1, p.down)
+    while work:
+        fill()
     recv(3, p.down, 1, p.down)
     recv(5, p.up, 0, p.up)
     recv(6, p.far, 0, p.down)
@@ -203,12 +214,54 @@
     return [(place.axis, place.up), (place.axis, place.down), (place.axis, place.mate)]
 
 
-def dispatch_kernel(mi_ref, og_ref, pick_ref, place_ref, out_ref, send, got, ss, rs):
-    ctx = Place("ctx")
+def deal_targets(g, n):
+    low = g < n // 2
+    return jnp.where(low, 2 * g, 2 * n - 1 - 2 * g), jnp.where(low, 2 * g + 1, 2 * n - 2 - 2 * g)
+
+
+def deal_sources(c, n):
+    even = lax.rem(c, 2) == 0
+    first = jnp.where(even, c // 2, (2 * n - 1 - c) // 2)
+    second = jnp.where(even, (2 * n - 2 - c) // 2, (c - 1) // 2)
+    return first, second
+
+
+def trade_start(lanes, base, moves, me):
+    for j, (src, dst, to, _) in enumerate(moves):
+
+        @pl.when(to != me)
+        def _(j=j, src=src, dst=dst, to=to):
+            lanes.copy(base + j, src, dst, "ctx", to).start()
+
+
+def trade_finish(lanes, base, moves, me):
+    for j, (src, dst, to, frm) in enumerate(moves):
+
+        @pl.when(to == me)
+        def _(src=src, dst=dst):
+            dst[...] = src[...]
+
+        @pl.when(frm != me)
+        def _(j=j, src=src, dst=dst, frm=frm):
+            lanes.copy(base + j, src, dst, "ctx", frm).wait_recv()
+
+        @pl.when(to != me)
+        def _(j=j, src=src, dst=dst, to=to):
+            lanes.copy(base + j, src, dst, "ctx", to).wait_send()
+
+
+def dispatch_kernel(
+    n_ctx, mi_ref, og_ref, pick_ref, place_ref, key_ref, val_ref,
+    mine_ref, k_out, v_out, send, got, ss, rs,
+):
     me = lax.axis_index("exp")
+    ctx_me = lax.axis_index("ctx")
     n_exp = send.shape[0]
-    peers = [("exp", lax.rem(me + d, n_exp)) for d in range(1, n_exp)]
-    greet(peers + around(ctx))
+    half = key_ref.shape[0] // 2
+    greet(
+        [("exp", lax.rem(me + d, n_exp)) for d in range(1, n_exp)]
+        + [("ctx", lax.rem(ctx_me + d, n_ctx)) for d in range(1, n_ctx)]
+    )
     lanes = Lanes(ss, rs)
     rows = jnp.dot(pick_ref[:, :128], mi_ref[...], preferred_element_type=F32)
     rows = rows + jnp.dot(pick_ref[:, 128:], og_ref[...], preferred_element_type=F32)
@@ -216,32 +269,33 @@
     for d in range(1, n_exp):
         to = lax.rem(me + d, n_exp)
         lanes.send(d - 1, send.at[to], got.at[d], "exp", to)
+    targets, sources = deal_targets(ctx_me, n_ctx), deal_sources(ctx_me, n_ctx)
+    moves = [
+        (ref.at[pl.ds(h * half, half)], out.at[h], targets[h], sources[h])
+        for h in range(2)
+        for ref, out in ((key_ref, k_out), (val_ref, v_out))
+    ]
+    trade_start(lanes, n_exp - 1, moves, ctx_me)
     got[0] = send[me]
     for d in range(1, n_exp):
         lanes.recv(d - 1, got.at[d], "exp", lax.rem(me + n_exp - d, n_exp))
     flat = got[...].astype(F32).reshape(n_exp * 8, got.shape[2]).astype(BF)
     mine = jnp.dot(place_ref[...], flat, preferred_element_type=F32).astype(BF)
-    mine = mine.reshape(2, 2, 16, got.shape[2])
-    for a in range(2):
-        for k in range(2):
-            out_ref[a, k, ctx.me] = mine[a, k]
-
-    def piece(block, half):
-        return out_ref.at[half, :, block]
-
-    gather_ring([piece], ctx, lanes, n_exp - 1)
+    mine_ref[...] = mine.reshape(2, 2, 16, got.shape[2])
+    trade_finish(lanes, n_exp - 1, moves, ctx_me)
     lanes.finish()
 
 
-def dispatch(moe_input, out_grad, pick, place):
+def dispatch(moe_input, out_grad, pick, place, keys, values):
     n_exp, n_ctx = lax.axis_size("exp"), lax.axis_size("ctx")
     width = moe_input.shape[1]
-    n_sem = n_exp - 1 + AG_LANES
+    dealt = jax.ShapeDtypeStruct((2, keys.shape[0] // 2, keys.shape[1]), BF)
+    n_sem = n_exp - 1 + 4
     return pl.pallas_call(
-        dispatch_kernel,
-        out_shape=jax.ShapeDtypeStruct((2, 2, n_ctx, 16, width), BF),
-        in_specs=[pl.BlockSpec(memory_space=VM)] * 4,
-        out_specs=pl.BlockSpec(memory_space=VM),
+        functools.partial(dispatch_kernel, n_ctx),
+        out_shape=(jax.ShapeDtypeStruct((2, 2, 16, width), BF), dealt, dealt),
+        in_specs=[pl.BlockSpec(memory_space=VM)] * 6,
+        out_specs=(pl.BlockSpec(memory_space=VM),) * 3,
         scratch_shapes=[
             VM((n_exp, 8, width), BF),
             VM((n_exp, 8, width), BF),
@@ -251,29 +305,61 @@
         compiler_params=pltpu.CompilerParams(
             collective_id=1, has_side_effects=True, vmem_limit_bytes=VLIM
         ),
-        cost_estimate=pl.CostEstimate(flops=10**9, bytes_accessed=150 * 10**6, transcendentals=0),
-    )(moe_input, out_grad, pick, place)
-
-
-def combine_kernel(part_ref, out_ref, buf, ss, rs):
+        cost_estimate=pl.CostEstimate(flops=10**6, bytes_accessed=10**6, transcendentals=0),
+    )(moe_input, out_grad, pick, place, keys, values)
+
+
+def share_kernel(mine_ref, out_ref, ss, rs):
+    ctx = Place("ctx")
+    greet(around(ctx))
+    lanes = Lanes(ss, rs)
+    for a in range(2):
+        for k in range(2):
+            out_ref[a, k, ctx.me] = mine_ref[a, k]
+    gather_ring([lambda block, half: out_ref.at[half, :, block]], ctx, lanes, 0)
+    lanes.finish()
+
+
+def share(mine):
+    n_ctx = lax.axis_size("ctx")
+    return pl.pallas_call(
+        share_kernel,
+        out_shape=jax.ShapeDtypeStruct(mine.shape[:2] + (n_ctx,) + mine.shape[2:], BF),
+        in_specs=[pl.BlockSpec(memory_space=VM)],
+        out_specs=pl.BlockSpec(memory_space=VM),
+        scratch_shapes=[
+            pltpu.SemaphoreType.DMA((AG_LANES,)),
+            pltpu.SemaphoreType.DMA((AG_LANES,)),
+        ],
+        compiler_params=pltpu.CompilerParams(
+            collective_id=5, has_side_effects=True, vmem_limit_bytes=VLIM
+        ),
+        cost_estimate=pl.CostEstimate(flops=10**6, bytes_accessed=10**6, transcendentals=0),
+    )(mine)
+
+
+def combine_kernel(part_ref, gate_ref, out_ref, gate_out, buf, gate_buf, ss, rs):
     ctx, exp = Place("ctx"), Place("exp")
     twin = exp.me + 1 - 2 * lax.rem(exp.me, 2)
     greet(around(ctx) + around(exp) + [("exp", twin)])
     lanes = Lanes(ss, rs)
     scatter_ring(
-        [lambda block, half: part_ref.at[half, block]],
+        [
+            lambda block, half: part_ref.at[half, block],
+            lambda block, half: gate_ref.at[half, block],
+        ],
         ctx,
         lanes,
         0,
-        [lambda s: buf.at[s]],
-        [lambda half: out_ref.at[exp.me, half]],
+        [lambda s: buf.at[s], lambda s: gate_buf.at[s]],
+        [lambda half: out_ref.at[exp.me, half], lambda half: gate_out.at[half]],
     )
 
     def piece(block, half):
         return out_ref.at[block, half]
 
-    base = AG_LANES
-    over = 2 * AG_LANES
+    base = 2 * AG_LANES
+    over = 3 * AG_LANES
     flip = 1 - 2 * lax.rem(exp.me, 2)
     for half in range(2):
         lanes.send(over + 14 + half, piece(exp.me, half), piece(exp.me, half), "exp", twin)
@@ -294,34 +380,78 @@
     lanes.finish()
 
 
-def combine(part):
+def combine(part, gate_part):
     n_exp = lax.axis_size("exp")
     rows, width = part.shape[2:]
-    n_sem = 2 * AG_LANES + 16
+    n_sem = 3 * AG_LANES + 16
     return pl.pallas_call(
         combine_kernel,
-        out_shape=jax.ShapeDtypeStruct((n_exp, 2, rows, width), BF),
-        in_specs=[pl.BlockSpec(memory_space=VM)],
-        out_specs=pl.BlockSpec(memory_space=VM),
+        out_shape=(
+            jax.ShapeDtypeStruct((n_exp, 2, rows, width), BF),
+            jax.ShapeDtypeStruct((2,) + gate_part.shape[2:], F32),
+        ),
+        in_specs=[pl.BlockSpec(memory_space=VM)] * 2,
+        out_specs=(pl.BlockSpec(memory_space=VM),) * 2,
         scratch_shapes=[
             VM((14, rows, width), BF),
+            VM((14,) + gate_part.shape[2:], F32),
             pltpu.SemaphoreType.DMA((n_sem,)),
             pltpu.SemaphoreType.DMA((n_sem,)),
         ],
         compiler_params=pltpu.CompilerParams(
             collective_id=2, has_side_effects=True, vmem_limit_bytes=VLIM
         ),
-        cost_estimate=pl.CostEstimate(flops=10**8, bytes_accessed=120 * 10**6, transcendentals=0),
-    )(part)
-
-
-def spread_kernel(do_ref, delta_ref, do_all, delta_all, ss, rs):
+        cost_estimate=pl.CostEstimate(flops=10**6, bytes_accessed=10**6, transcendentals=0),
+    )(part, gate_part)
+
+
+def spread_kernel(
+    do_ref, delta_ref, og_ref, o_ref, taken_ref, dx_ref,
+    do_all, delta_all, dw_ref, og_buf, dw_acc, ss, rs, load_sems,
+):
     ctx = Place("ctx")
     greet(around(ctx))
     lanes = Lanes(ss, rs)
     do_all[ctx.me] = do_ref[...]
     delta_all[ctx.me] = delta_ref[...]
     rows = do_ref.shape[0] // 2
+    load_rows = og_buf.shape[1]
+    n_load = og_ref.shape[0] // load_rows
+    n_out, _, part = dw_ref.shape
+
+    def load(j):
+        slot = lax.rem(j, 2)
+        return pltpu.make_async_copy(
+            og_ref.at[pl.ds(j * load_rows, load_rows)], og_buf.at[slot], load_sems.at[slot]
+        )
+
+    load(0).start()
+    dw_acc[...] = jnp.zeros_like(dw_acc)
+
+    def add_rows(j, carry):
+        @pl.when(j + 1 < n_load)
+        def _():
+            load(j + 1).start()
+
+        load(j).wait()
+        o = o_ref[pl.ds(j * load_rows, load_rows), :]
+        slot = lax.rem(j, 2)
+        for b in range(n_out):
+            cols = pl.ds(b * part, part)
+            dw_acc[:, cols] += contract_first(o, og_buf[slot, :, cols])
+        return carry
+
+    def stretch(first, last):
+        return lambda: lax.fori_loop(first, last, add_rows, 0)
+
+    def close():
+        for b in range(n_out):
+            cols = pl.ds(b * part, part)
+            total = dw_acc[:, cols] + contract_first(taken_ref[...], dx_ref[:, cols])
+            dw_ref[b] = total.astype(BF)
+
+    quarter = n_load // 4
+    work = [stretch(j * quarter, (j + 1) * quarter) for j in range(4)] + [close]
 
     def piece_do(block, half):
         return do_all.at[block, pl.ds(half * rows, rows)]
@@ -329,174 +459,237 @@
     def piece_delta(block, half):
         return delta_all.at[block, :, pl.ds(half * rows, rows)]
 
-    gather_ring([piece_do, piece_delta], ctx, lanes, 0)
+    gather_ring([piece_do, piece_delta], ctx, lanes, 0, work=work)
     lanes.finish()
 
 
-def spread(d_out, delta):
+def spread(d_out, delta, og_all, attn_out, out_taken, dx_all):
     n_ctx = lax.axis_size("ctx")
     n_sem = 2 * AG_LANES
+    width = og_all.shape[1]
+    head = d_out.shape[1]
+    vmem = pl.BlockSpec(memory_space=VM)
     return pl.pallas_call(
         spread_kernel,
         out_shape=(
             jax.ShapeDtypeStruct((n_ctx,) + d_out.shape, BF),
             jax.ShapeDtypeStruct((n_ctx,) + delta.shape, F32),
-        ),
-        in_specs=[pl.BlockSpec(memory_space=VM)] * 2,
-        out_specs=(pl.BlockSpec(memory_space=VM),) * 2,
+            jax.ShapeDtypeStruct((n_ctx, head, width // n_ctx), BF),
+        ),
+        in_specs=[vmem, vmem, pl.BlockSpec(memory_space=pl.ANY), vmem, vmem, vmem],
+        out_specs=(vmem,) * 3,
         scratch_shapes=[
+            VM((2, 256, width), BF),
+            VM((head, width), F32),
             pltpu.SemaphoreType.DMA((n_sem,)),
             pltpu.SemaphoreType.DMA((n_sem,)),
+            pltpu.SemaphoreType.DMA((2,)),
         ],
         compiler_params=pltpu.CompilerParams(
             collective_id=3, has_side_effects=True, vmem_limit_bytes=VLIM
         ),
-        cost_estimate=pl.CostEstimate(flops=10**6, bytes_accessed=120 * 10**6, transcendentals=0),
-    )(d_out, delta)
-
-
-def settle_kernel(dq_ref, dw_ref, dq_out, dw_out, dq_buf, dw_buf, ss, rs):
-    ctx = Place("ctx")
-    greet(around(ctx))
+        cost_estimate=pl.CostEstimate(flops=10**6, bytes_accessed=10**6, transcendentals=0),
+    )(d_out, delta, og_all, attn_out, out_taken, dx_all)
+
+
+CHUNK = 1024
+TILE = 512
+
+
+def attention_kernel(
+    scale, n_ctx, k_ref, v_ref, q_ref, do_ref, lse_ref, delta_ref, dw_ref,
+    gq_out, gw_out, gk_out, gv_out,
+    dq_part, dk_acc, dv_acc, dq_acc, back, dq_buf, dw_buf, ss, rs,
+):
+    p = Place("ctx")
+    c = p.me
+    greet([("ctx", lax.rem(c + d, n_ctx)) for d in range(1, n_ctx)])
     lanes = Lanes(ss, rs)
-    rows_q, rows_w = dq_ref.shape[1] // 2, dw_ref.shape[1] // 2
-    scatter_ring(
-        [
-            lambda block, half: dq_ref.at[block, pl.ds(half * rows_q, rows_q)],
-            lambda block, half: dw_ref.at[block, pl.ds(half * rows_w, rows_w)],
-        ],
-        ctx,
-        lanes,
-        0,
-        [lambda s: dq_buf.at[s], lambda s: dw_buf.at[s]],
-        [
-            lambda half: dq_out.at[pl.ds(half * rows_q, rows_q)],
-            lambda half: dw_out.at[pl.ds(half * rows_w, rows_w)],
-        ],
-    )
-    lanes.finish()
-
-
-def settle_grads(dq, dw):
-    n_sem = 2 * AG_LANES
+    n_chunk = 2 * n_ctx
+    first = jnp.where(lax.rem(c, 2) == 0, c, n_chunk - 1 - c)
+    ids = (first, n_chunk - 1 - first)
+    dk_acc[...] = jnp.zeros_like(dk_acc)
+    dv_acc[...] = jnp.zeros_like(dv_acc)
+
+    def tile(part, group, half, row, key, masked):
+        at = half * CHUNK + row
+        spot = group * 2 * CHUNK + at
+        q = q_ref[pl.ds(spot, TILE), :]
+        do = do_ref[group, pl.ds(at, TILE), :]
+        lse = lse_ref[:, pl.ds(spot, TILE)] * LOG2E
+        delta = delta_ref[group, :, pl.ds(at, TILE)]
+        k = k_ref[part, pl.ds(key, TILE), :]
+        v = v_ref[part, pl.ds(key, TILE), :]
+        s = contract_last(k, q) * (scale * LOG2E) - lse
+        if masked:
+            rk = lax.broadcasted_iota(jnp.int32, s.shape, 0)
+            cq = lax.broadcasted_iota(jnp.int32, s.shape, 1)
+            s = jnp.where(rk <= cq, s, -1e30)
+        probs = jnp.exp2(s)
+        dp = contract_last(v, do)
+        ds = (probs * (dp - delta)).astype(BF)
+        dv_acc[part, pl.ds(key, TILE), :] += jnp.dot(
+            probs.astype(BF), do, preferred_element_type=F32
+        )
+        dk_acc[part, pl.ds(key, TILE), :] += jnp.dot(ds, q, preferred_element_type=F32)
+        dq_acc[pl.ds(row, TILE), :] += contract_first(ds, k)
+
+    w_rows = dw_ref.shape[1] // 2
+    parts = (
+        lambda block, h: dq_part.at[block, pl.ds(h * CHUNK, CHUNK)],
+        lambda block, h: dw_ref.at[block, pl.ds(h * w_rows, w_rows)],
+    )
+    slots = (lambda s: dq_buf.at[s], lambda s: dw_buf.at[s])
+    n = len(parts)
+
+    def send(k, src, dev):
+        for i in range(n):
+            lanes.copy(k * n + i, src[i], slots[i](k), "ctx", dev).start()
+
+    def recv(k, dev):
+        for i in range(n):
+            lanes.copy(k * n + i, slots[i](k), slots[i](k), "ctx", dev).wait_recv()
+
+    def terms(block, h):
+        return [parts[i](block, h) for i in range(n)]
+
+    def plain(k, block, h, dev):
+        send(k, terms(block, h), dev)
+
+    def summed(k, into, others, block, h, dev):
+        for i in range(n):
+            add_into(
+                slots[i](into), slots[i](into), *[slots[i](o) for o in others], parts[i](block, h)
+            )
+        send(k, [slots[i](into) for i in range(n)], dev)
+
+    def near_up():
+        recv(0, p.down)
+        summed(2, 0, (), p.mate_up, 0, p.up)
+
+    def near_down():
+        recv(1, p.up)
+        summed(5, 1, (), p.mate_down, 1, p.down)
+
+    def over(h):
+        recv(2 + h, p.down)
+        recv(4 + h, p.up)
+        summed(12 + h, 2 + h, (4 + h,), p.mate, h, p.mate)
+
+    def own_up():
+        recv(6, p.down)
+        summed(8, 6, (), p.up, 0, p.up)
+
+    def own_down():
+        recv(7, p.up)
+        summed(11, 7, (), p.down, 1, p.down)
+
+    plan = {
+        0: [lambda: plain(0, p.mate_far, 0, p.up)],
+        1: [lambda: plain(1, p.mate_far, 1, p.down)],
+        3: [lambda: plain(3, p.mate_up, 1, p.up)],
+        4: [lambda: plain(4, p.mate_down, 0, p.down)],
+        8: [lambda: plain(6, p.far, 0, p.up), near_up],
+        9: [lambda: plain(7, p.far, 1, p.down), near_down],
+        11: [lambda: plain(9, p.up, 1, p.up), own_up, lambda: over(0)],
+        12: [lambda: plain(10, p.down, 0, p.down), lambda: over(1)],
+        13: [own_down],
+    }
+    order = [p.mate_far, p.mate_up, p.mate_down, p.mate, p.far, p.up, p.down, p.me]
+
+    def step(t, carry):
+        place = t // 2
+        half = lax.rem(t, 2)
+        group = order[0]
+        for j in range(1, len(order)):
+            group = jnp.where(place == j, order[j], group)
+        chunk = 2 * group + half
+        dq_acc[...] = jnp.zeros_like(dq_acc)
+        for part in range(2):
+
+            @pl.when(chunk > ids[part])
+            def _(part=part):
+                for row in range(0, CHUNK, TILE):
+                    for key in range(0, CHUNK, TILE):
+                        tile(part, group, half, row, key, False)
+
+            @pl.when(chunk == ids[part])
+            def _(part=part):
+                for row in range(0, CHUNK, TILE):
+                    for key in range(0, row + 1, TILE):
+                        tile(part, group, half, row, key, key == row)
+
+        dq_part[group, pl.ds(half * CHUNK, CHUNK), :] = (dq_acc[...] * scale).astype(BF)
+        for when, acts in plan.items():
+
+            @pl.when(t == when)
+            def _(acts=acts):
+                for act in acts:
+                    act()
+
+        return carry
+
+    lax.fori_loop(0, n_chunk, step, 0)
+
+    targets, sources = deal_targets(c, n_ctx), deal_sources(c, n_ctx)
+    for part in range(2):
+        back[part, 0] = (dk_acc[part] * scale).astype(BF)
+        back[part, 1] = dv_acc[part].astype(BF)
+    moves = [
+        (back.at[h, j], out.at[pl.ds(h * CHUNK, CHUNK)], sources[h], targets[h])
+        for h in range(2)
+        for j, out in enumerate((gk_out, gv_out))
+    ]
+    base = n * AG_LANES
+    trade_start(lanes, base, moves, c)
+    finals = (
+        lambda h: gq_out.at[pl.ds(h * CHUNK, CHUNK)],
+        lambda h: gw_out.at[pl.ds(h * w_rows, w_rows)],
+    )
+    for h in range(2):
+        recv(8 + h, p.down)
+        recv(10 + h, p.up)
+        recv(12 + h, p.mate)
+        for i in range(n):
+            add_into(
+                finals[i](h), slots[i](8 + h), slots[i](10 + h), slots[i](12 + h),
+                parts[i](p.me, h),
+            )
+    for k in range(AG_LANES):
+        for i in range(n):
+            lanes.copy(k * n + i, slots[i](k), slots[i](k), "ctx", p.up).wait_send()
+    trade_finish(lanes, base, moves, c)
+
+
+def attention(k, v, q_all, do_all, lse, delta_all, dw_part, scale):
+    total, head = q_all.shape
+    n_ctx, tok_ctx, _ = do_all.shape
+    vmem = pl.BlockSpec(memory_space=VM)
+    own = jax.ShapeDtypeStruct((tok_ctx, head), BF)
+    n_sem = 2 * AG_LANES + 4
     return pl.pallas_call(
-        settle_kernel,
-        out_shape=(
-            jax.ShapeDtypeStruct(dq.shape[1:], BF),
-            jax.ShapeDtypeStruct(dw.shape[1:], BF),
-        ),
-        in_specs=[pl.BlockSpec(memory_space=VM)] * 2,
-        out_specs=(pl.BlockSpec(memory_space=VM),) * 2,
+        functools.partial(attention_kernel, scale, n_ctx),
+        out_shape=(own, jax.ShapeDtypeStruct(dw_part.shape[1:], BF), own, own),
+        in_specs=[vmem] * 7,
+        out_specs=(vmem,) * 4,
         scratch_shapes=[
-            VM((14, dq.shape[1] // 2, dq.shape[2]), BF),
-            VM((14, dw.shape[1] // 2, dw.shape[2]), BF),
+            VM(do_all.shape, BF),
+            VM((2, CHUNK, head), F32),
+            VM((2, CHUNK, head), F32),
+            VM((CHUNK, head), F32),
+            VM((2, 2, CHUNK, head), BF),
+            VM((AG_LANES, CHUNK, head), BF),
+            VM((AG_LANES, dw_part.shape[1] // 2, dw_part.shape[2]), BF),
             pltpu.SemaphoreType.DMA((n_sem,)),
             pltpu.SemaphoreType.DMA((n_sem,)),
         ],
         compiler_params=pltpu.CompilerParams(
             collective_id=4, has_side_effects=True, vmem_limit_bytes=VLIM
         ),
-        cost_estimate=pl.CostEstimate(flops=10**7, bytes_accessed=120 * 10**6, transcendentals=0),
-    )(dq, dw)
-
-
-CHUNK = 1024
-TILE = 512
-
-
-def attention_kernel(
-    scale, n_chunk, k_ref, v_ref, q_ref, do_ref, lse_ref, delta_ref,
-    dq_ref, dk_ref, dv_ref, dk_acc, dv_acc, dq_acc,
-):
-    i = pl.program_id(0)
-    c = lax.axis_index("ctx")
-    first = jnp.where(lax.rem(c, 2) == 0, c, n_chunk - 1 - c)
-    ids = (first, n_chunk - 1 - first)
-
-    @pl.when(i == 0)
-    def _():
-        dk_acc[...] = jnp.zeros_like(dk_acc)
-        dv_acc[...] = jnp.zeros_like(dv_acc)
-
-    dq_acc[...] = jnp.zeros_like(dq_acc)
-
-    def tile(part, row, key, key_len, masked):
-        q = q_ref[pl.ds(row, TILE), :]
-        do = do_ref[0, pl.ds(row, TILE), :]
-        lse = lse_ref[:, pl.ds(row, TILE)] * LOG2E
-        delta = delta_ref[0, :, pl.ds(row, TILE)]
-        k = k_ref[part, pl.ds(key, key_len), :]
-        v = v_ref[part, pl.ds(key, key_len), :]
-        s = contract_last(k, q) * (scale * LOG2E) - lse
-        if masked:
-            rk = lax.broadcasted_iota(jnp.int32, s.shape, 0)
-            cq = lax.broadcasted_iota(jnp.int32, s.shape, 1)
-            s = jnp.where(rk <= cq, s, -1e30)
-        p = jnp.exp2(s)
-        dp = contract_last(v, do)
-        ds = (p * (dp - delta)).astype(BF)
-        dv_acc[part, pl.ds(key, key_len), :] += jnp.dot(
-            p.astype(BF), do, preferred_element_type=F32
-        )
-        dk_acc[part, pl.ds(key, key_len), :] += jnp.dot(ds, q, preferred_element_type=F32)
-        dq_acc[pl.ds(row, TILE), :] += contract_first(ds, k)
-
-    for part in range(2):
-
-        @pl.when(i > ids[part])
-        def _(part=part):
-            for row in range(0, CHUNK, TILE):
-                for key in range(0, CHUNK, TILE):
-                    tile(part, row, key, TILE, False)
-
-        @pl.when(i == ids[part])
-        def _(part=part):
-            for row in range(0, CHUNK, TILE):
-                for key in range(0, row + 1, TILE):
-                    tile(part, row, key, TILE, key == row)
-
-    dq_ref[...] = (dq_acc[...] * scale).astype(BF)
-
-    @pl.when(i == n_chunk - 1)
-    def _():
-        dk_ref[...] = (dk_acc[...] * scale).astype(BF)
-        dv_ref[...] = dv_acc[...].astype(BF)
-
-
-def attention(k, v, q_all, do_all, lse, delta_all, scale):
-    total, head = q_all.shape
-    n_chunk = total // CHUNK
-    per = do_all.shape[1] // CHUNK
-    whole = pl.BlockSpec((2, CHUNK, head), lambda i: (0, 0, 0))
-    return pl.pallas_call(
-        functools.partial(attention_kernel, scale, n_chunk),
-        grid=(n_chunk,),
-        out_shape=(
-            jax.ShapeDtypeStruct((total, head), BF),
-            jax.ShapeDtypeStruct(k.shape, BF),
-            jax.ShapeDtypeStruct(v.shape, BF),
-        ),
-        in_specs=[
-            whole,
-            whole,
-            pl.BlockSpec((CHUNK, head), lambda i: (i, 0)),
-            pl.BlockSpec((1, CHUNK, head), lambda i: (i // per, i % per, 0)),
-            pl.BlockSpec((1, CHUNK), lambda i: (0, i)),
-            pl.BlockSpec((1, 1, CHUNK), lambda i: (i // per, 0, i % per)),
-        ],
-        out_specs=(pl.BlockSpec((CHUNK, head), lambda i: (i, 0)), whole, whole),
-        scratch_shapes=[
-            VM((2, CHUNK, head), F32),
-            VM((2, CHUNK, head), F32),
-            VM((CHUNK, head), F32),
-        ],
-        compiler_params=pltpu.CompilerParams(
-            dimension_semantics=("arbitrary",), vmem_limit_bytes=VLIM
-        ),
         cost_estimate=pl.CostEstimate(
             flops=40 * 10**9, bytes_accessed=20 * 10**6, transcendentals=17 * 10**6
         ),
-    )(k, v, q_all, do_all, lse, delta_all)
+    )(k, v, q_all, do_all, lse, delta_all, dw_part)
 
 
 def body(
@@ -525,19 +718,6 @@
     key_scale = head_dim ** (-0.5)
     i32 = jnp.int32
 
-    og_all = lax.all_gather(out_grad, "exp", axis=0, tiled=True)
-    q_all = lax.all_gather(queries, "ctx", axis=0, tiled=True)
-
-    half = tok_ctx // 2
-    top = 2 * n_ctx - 1
-    to_even = [(g, 2 * g if g < n_ctx // 2 else top - 2 * g) for g in range(n_ctx)]
-    to_odd = [(g, 2 * g + 1 if g < n_ctx // 2 else top - 1 - 2 * g) for g in range(n_ctx)]
-    kv = jnp.stack([attn_keys, values])
-    kv_first = lax.ppermute(kv[:, :half], "ctx", to_even)
-    kv_second = lax.ppermute(kv[:, half:], "ctx", to_odd)
-    k_dealt = jnp.stack([kv_first[0], kv_second[0]])
-    v_dealt = jnp.stack([kv_first[1], kv_second[1]])
-
     base_row = (ctx_id * n_exp + exp_id) * tok_dev
     below = jnp.sum((expert_picks < base_row).astype(i32), axis=1, keepdims=True)
     inside = (expert_picks >= base_row) & (expert_picks < base_row + tok_dev)
@@ -568,7 +748,12 @@
     spots = jnp.stack([spot_x, spot_x + n_local * MOST]).reshape(-1)
     place = (spots[:, None] == jnp.arange(8 * n_exp, dtype=i32)[None, :]).astype(BF)
 
-    slots = dispatch(moe_input, out_grad, pick, place)
+    mine, k_dealt, v_dealt = dispatch(moe_input, out_grad, pick, place, attn_keys, values)
+    og_late, mine = lax.optimization_barrier((out_grad, mine))
+    og_all = lax.all_gather(og_late, "exp", axis=0, tiled=True)
+    slots = share(mine)
+    q_late, slots = lax.optimization_barrier((queries, slots))
+    q_all = lax.all_gather(q_late, "ctx", axis=0, tiled=True)
     slots = slots.reshape(2, n_local, n_ctx * group_picks, feat_width)
     slot_rows, slot_grads = slots[0], slots[1]
 
@@ -579,7 +764,8 @@
     hidden_full = gated_act * pre_up
     hidden = hidden_full.astype(BF)
     down_back = jnp.einsum("kcd,kfd->kcf", slot_grads, w_down, preferred_element_type=F32)
-    gate_part = jnp.sum(down_back * hidden_full, axis=2).astype(BF)
+    gate_part = jnp.sum(down_back * hidden_full, axis=2).reshape(n_local, n_ctx, 1, group_picks)
+    gate_part = jnp.pad(gate_part, ((0, 0), (0, 0), (0, 0), (0, 128 - group_picks)))
     scaled = gate_rows[..., None] * down_back
     d_gate = (scaled * pre_up * act_slope).astype(BF)
     d_up = (scaled * gated_act).astype(BF)
@@ -587,9 +773,10 @@
         jnp.einsum("kcf,kdf->kcd", d_gate, w_gate, preferred_element_type=F32)
         + jnp.einsum("kcf,kdf->kcd", d_up, w_up, preferred_element_type=F32)
     ).astype(BF)
-    d_gates = lax.psum_scatter(gate_part, "ctx", scatter_dimension=1, tiled=True).astype(F32)
-
-    dx_all = combine(dx_part.reshape(n_local, n_ctx, group_picks, feat_width))
+    dx_all, gate_sum = combine(
+        dx_part.reshape(n_local, n_ctx, group_picks, feat_width), gate_part
+    )
+    d_gates = gate_sum[:, 0, :group_picks]
     dx_all = dx_all.reshape(-1, feat_width)
 
     weighted = (gate_rows[..., None] * slot_grads.astype(F32)).astype(BF)
@@ -616,23 +803,13 @@
         jnp.ones((1, head_dim), F32), product, (((1,), (1,)), ((), ())),
         precision=lax.Precision.HIGHEST, preferred_element_type=F32,
     )
-    do_all, delta_all = spread(d_out, delta)
-
-    dq, dk, dv = attention(k_dealt, v_dealt, q_all, do_all, log_norm, delta_all, key_scale)
-
     out_taken = contract_first(spread_hot, attn_out).astype(BF)
-    dw_part = contract_first(attn_out, og_all) + contract_first(out_taken, dx_all)
-    dw_part = dw_part.astype(BF).reshape(head_dim, n_ctx, -1).transpose(1, 0, 2)
-
-    back = jnp.stack([dk, dv], axis=1)
-    from_even = [(b, a) for a, b in to_even]
-    from_odd = [(b, a) for a, b in to_odd]
-    kv_low = lax.ppermute(back[0], "ctx", from_even)
-    kv_high = lax.ppermute(back[1], "ctx", from_odd)
-    grad_kv = jnp.concatenate([kv_low, kv_high], axis=1)
-    grad_q, dw_out = settle_grads(dq.reshape(n_ctx, tok_ctx, head_dim), dw_part)
+    do_all, delta_all, dw_part = spread(d_out, delta, og_all, attn_out, out_taken, dx_all)
+    grad_q, dw_out, grad_k, grad_v = attention(
+        k_dealt, v_dealt, q_all, do_all, log_norm, delta_all, dw_part, key_scale
+    )
     return (
-        d_resid, dw_gate, dw_up, dw_down, d_gates, dw_out, grad_q, grad_kv[0], grad_kv[1],
+        d_resid, dw_gate, dw_up, dw_down, d_gates, dw_out, grad_q, grad_k, grad_v,
     )
 
 

time: 445 us -> 372 us (0.84)
  waiting for transfers between devices: 23.8 us -> 0.06 us
  starting transfers between devices: 18.7 us -> 0.08 us
  matrix products: 45.6 us -> 33.3 us
  Pallas kernels: 305 us -> 298 us
  other arithmetic: 10.5 us -> 4.44 us
    unnamed x4 -> x2, waiting for transfers between devices: 23.7 us -> 0.03 us
    ppermute x4 -> x0, starting transfers between devices: 18.6 us -> none  [the longest x1 7.92 us: body(): kv_high = lax.ppermute(back[1], 'ctx', from_odd)]
    dot_general x2 -> x1, matrix products: 13.8 us -> 1.97 us  [contract_first(): lax.dot_general(left, right, (((0,), (0,)), ((), ())), preferred_element_...]
    pallas_call x4, Pallas kernels: 244 us -> 238 us  [the longest x1 91.5 us: attention(): pl.pallas_call(functools.partial(attention_kernel, scale, n_ctx), out_sha...]
    unnamed x39 -> x37, local copies, waits for them, and re-layouts: 9.22 us -> 11.3 us
  transfers between devices with their start and end apart: 7 -> 2, of which waited for: 1 -> 0; matrix products, arithmetic and copies ran while one was open for 12% -> 10% of each run, Pallas kernels for 43% -> 43%
where the time goes in v2:
time: 372 us; the launch traced here: 366 us
  Pallas kernels  298 us (80%)
  matrix products  33.3 us (9%)
  local copies, waits for them, and re-layouts  16.1 us (4%)
  between operations  14.3 us (4%)
  other arithmetic  4.44 us (1%)
    pallas_call x1, Pallas kernels, attention(): pl.pallas_call(functools.partial(attention_kernel, scale, n_ctx), out_sha...  91.5 us
    pallas_call x1, Pallas kernels, spread(): pl.pallas_call(spread_kernel, out_shape=(jax.ShapeDtypeStruct((n_ctx,) +...  59.9 us
    pallas_call x1, Pallas kernels, combine(): pl.pallas_call(combine_kernel, out_shape=(jax.ShapeDtypeStruct((n_exp, 2,...  56.5 us
    pallas_call x1, Pallas kernels, dispatch(): pl.pallas_call(functools.partial(dispatch_kernel, n_ctx), out_shape=(jax....  49.3 us
    pallas_call x1, Pallas kernels, share(): pl.pallas_call(share_kernel, out_shape=jax.ShapeDtypeStruct(mine.shape[:2...  40.5 us
    unnamed x37, local copies, waits for them, and re-layouts  11.3 us
    dot_general x1, matrix products, contract_last(): lax.dot_general(left, right, (((1,), (1,)), ((), ())), preferred_element_...  9.18 us
  transfers between devices with their start and end apart: 2, of which 0 were waited for; matrix products, arithmetic and copies ran while one was open for 10% of the time, Pallas kernels for 43%

profile of v2, /device:TPU:0, one launch (start us, length us, event | category | flops | bytes accessed | tf_op | source)
XLA Modules:
  0.0 366.0 jit_solution(6779205478134820169)
XLA Ops:
  7.3 1.0 convert_reduce_fusion.1
  12.0 49.3 %shard_map.196 = (bf16[2,2,16,4096]{3,2,1,0:T(8,128)(2,1)}, bf16[2,1024,128]{2,1,0:T(8,128)(2,1)}, bf16[2,1024,128]{2,1,0:T(8,128)(2,1)}) custom-call(bf16[128,4096]{1,0:T(8,128)(2,1)} %mi_ref.1, bf16[128,4096]{1,0:T(8,128)(2,1)} %og_ref.1, bf16[128,256]{1,0:T(8,128)(2,1)} %fusion.18.pick_ref, bf16[64,128]{1,0:T(8,128)(2,1)} %fusion.21.place_ref, ...), custom_call_target="tpu_custom_call" | custom-call | flops 1000000 | bytes 1000000 | tf_op jit(solution)/shard_map/pallas_call | solution.py:294
  61.4 40.5 %shard_map.197 = bf16[2,2,8,16,4096]{4,3,2,1,0:T(8,128)(2,1)} custom-call(bf16[2,2,16,4096]{3,2,1,0:T(8,128)(2,1)} %get-tuple-element.26.mine_ref), custom_call_target="tpu_custom_call" | custom-call | flops 1000000 | bytes 1000000 | tf_op jit(solution)/shard_map/pallas_call | solution.py:325
  102.6 3.0 fusion.34
  106.8 1.1 fusion.36
  108.0 1.1 copy-done.14
  109.1 0.9 multiply_reduce_fusion
  111.7 1.2 copy-done.6
  112.9 2.1 fusion
  115.0 56.5 %shard_map.198 = (bf16[16,2,16,4096]{3,2,1,0:T(8,128)(2,1)}, f32[2,1,128]{2,1,0:T(1,128)}) custom-call(bf16[2,8,16,4096]{3,2,1,0:T(8,128)(2,1)} %bitcast.43, f32[2,8,1,128]{3,2,1,0:T(1,128)} %pad.4.gate_ref), custom_call_target="tpu_custom_call" | custom-call | flops 1000000 | bytes 1000000 | tf_op jit(solution)/shard_map/pallas_call | solution.py:387
  171.5 2.0 fusion.9.taken_ref
  173.5 2.5 convolution_convert_fusion
  175.9 2.5 convolution_convert_fusion.1
  178.4 2.6 convolution_convert_fusion.2
  182.0 1.8 fusion.1
  183.8 9.2 %fusion.38 = f32[2048,128]{1,0:T(8,128)} fusion(bf16[2048,4096]{1,0:T(8,128)(2,1)} %all-gather.5.cloned.1.call-done.og_ref, bf16[128,4096]{1,0:T(8,128)(2,1)S(1)} %copy-done.15), kind=kOutput, calls=%fused_computation.75 | convolution fusion | flops 2147483648 | bytes 18874368 | tf_op jit(solution)/shard_map/dot_general | solution.py:30
  193.0 5.4 %fusion.5.do_ref = bf16[2048,128]{1,0:T(8,128)(2,1)S(1)} fusion(f32[2048,128]{1,0:T(8,128)} %fusion.38, s32[512]{0:T(512)S(1)} %sub.71, bf16[512,4096]{1,0:T(8,128)(2,1)} %bitcast.38, bf16[128,4096]{1,0:T(8,128)(2,1)S(1)} %copy-done.15), kind=kOutput, calls=%fused_computation.12 | convolution fusion | flops 806944768 | bytes 6817792 | tf_op jit(solution)/shard_map/dot_general | solution.py:800
  198.4 1.6 fusion.10.delta_ref
  200.0 59.9 %shard_map.199 = (bf16[8,2048,128]{2,1,0:T(8,128)(2,1)}, f32[8,1,2048]{2,1,0:T(1,128)}, bf16[8,128,512]{2,1,0:T(8,128)(2,1)}) custom-call(bf16[2048,128]{1,0:T(8,128)(2,1)} %copy-done.11, f32[1,2048]{1,0:T(1,128)} %fusion.10.delta_ref, bf16[2048,4096]{1,0:T(8,128)(2,1)} %all-gather.5.cloned.1.call-done.og_ref, bf16[2048,128]{1,0:T(8,128)(2,1)} %o_ref.1, ...), custom_call_target="tpu_custom_call" | custom-call | flops 1000000 | bytes 1000000 | tf_op jit(solution)/shard_map/pallas_call | solution.py:472
  259.9 91.5 %shard_map.200 = (bf16[2048,128]{1,0:T(8,128)(2,1)}, bf16[128,512]{1,0:T(8,128)(2,1)}, bf16[2048,128]{1,0:T(8,128)(2,1)}, bf16[2048,128]{1,0:T(8,128)(2,1)}) custom-call(bf16[2,1024,128]{2,1,0:T(8,128)(2,1)} %get-tuple-element.30.k_ref, bf16[2,1024,128]{2,1,0:T(8,128)(2,1)} %get-tuple-element.31.v_ref, ...), custom_call_target="tpu_custom_call" | custom-call | flops 40000000000 | bytes 20000000 | tf_op jit(solution)/shard_map/pallas_call | solution.py:670
  352.0 1.6 copy.38
  353.6 1.9 copy.39
  355.4 1.9 copy.40
  357.3 1.9 copy.41
  (62 shorter events, 8.9 us)
Async XLA Ops:
  7.2 99.6 %copy-start = (bf16[2,4096,176]{1,2,0:T(8,128)(2,1)S(1)}, bf16[2,4096,176]{1,2,0:T(8,128)(2,1)}, u32[]{:S(2)}) copy-start(bf16[2,4096,176]{1,2,0:T(8,128)(2,1)} %param.15) | copy-start | bytes 8650756
  7.2 176.6 %all-gather.5.cloned.1.call-start = ((), (), s32[]{:S(2)}) async-start(), calls=%async_computation.1 | async-start | bytes 17825792 | tf_op jit(solution)/shard_map/all_gather | solution.py:753
  61.3 198.6 %all-gather.3.cloned.1.call-start = ((), (), s32[]{:S(2)}) async-start(), calls=%async_computation | async-start | bytes 4718592 | tf_op jit(solution)/shard_map/all_gather | solution.py:756
  102.6 3.3 copy-start.5
  105.7 2.3 copy-start.2
  105.7 2.3 copy-start.8
  106.8 2.3 copy-start.14
  107.9 2.2 copy-start.12
  110.9 1.9 copy-start.6
  112.9 58.6 %copy-start.10 = (bf16[2048,128]{1,0:T(8,128)(2,1)S(1)}, bf16[2048,128]{1,0:T(8,128)(2,1)}, u32[]{:S(2)}) copy-start(bf16[2048,128]{1,0:T(8,128)(2,1)} %o_ref.1) | copy-start | bytes 1572868
  115.0 58.5 %copy-start.3 = (bf16[1,2,8,16,4096]{4,3,2,1,0:T(8,128)(2,1)S(1)}, bf16[1,2,8,16,4096]{4,3,2,1,0:T(8,128)(2,1)}, u32[]{:S(2)}) copy-start(bf16[1,2,8,16,4096]{4,3,2,1,0:T(8,128)(2,1)} %copy-done.2) | copy-start | bytes 6291460
  175.9 2.5 copy-start.9
  178.4 2.8 copy-start.4
  178.4 3.5 copy-start.7
  182.0 1.8 copy-start.15
  198.4 1.6 copy-start.11
  259.9 91.5 %copy-start.13 = (f32[2,1,128]{2,1,0:T(1,128)S(1)}, f32[2,1,128]{2,1,0:T(1,128)}, u32[]{:S(2)}) copy-start(f32[2,1,128]{2,1,0:T(1,128)} %get-tuple-element.29) | copy-start | bytes 3076
  259.9 99.3 %copy-start.1 = (bf16[2,4096,176]{1,2,0:T(8,128)(2,1)S(1)}, bf16[2,4096,176]{1,2,0:T(8,128)(2,1)}, u32[]{:S(2)}) copy-start(bf16[2,4096,176]{1,2,0:T(8,128)(2,1)} %param.15) | copy-start | bytes 8650756
Sparse Core Ops, SparseCore 0:
  61.4 104.6 all-gather.4
  168.5 87.3 all-gather.2

commit v3 on v2

--- a/solution.py
+++ b/solution.py
@@ -51,6 +51,9 @@
         self.mate = at(other, pos)
         self.mate_up, self.mate_down = at(other, pos + 1), at(other, pos - 1)
         self.mate_far = at(other, pos + 2)
+        self.spots = tuple(lax.rem(pos + d, 4) for d in (0, 1, 3, 2))
+        self.flip = 1 - 2 * low
+        self.twin, self.mate_twin = me + self.flip, self.mate + self.flip
 
 
 def greet(peers):
@@ -90,7 +93,7 @@
 AG_LANES = 14
 
 
-def gather_ring(pieces, place, lanes, base, arrived=None, work=()):
+def gather_ring(pieces, place, lanes, base, arrived=None, work=(), ready=None):
     axis = place.axis
     n = len(pieces)
     work = list(work)
@@ -110,12 +113,16 @@
             arrived(k, block, half)
 
     p = place
+    if ready is not None:
+        ready(0)
     send(0, p.me, 0, p.mate)
     send(2, p.me, 0, p.up)
+    send(5, p.me, 0, p.down)
+    if ready is not None:
+        ready(1)
     send(4, p.me, 1, p.down)
     send(1, p.me, 1, p.mate)
     send(3, p.me, 1, p.up)
-    send(5, p.me, 0, p.down)
     fill()
     recv(2, p.down, 0, p.down)
     send(6, p.down, 0, p.up)
@@ -146,6 +153,45 @@
     recv(13, p.mate_far, 1, p.up)
 
 
+RING_LANES = 6
+
+
+class Ring:
+    def __init__(self, piece, place, lanes, base):
+        self.piece, self.place, self.lanes, self.base = piece, place, lanes, base
+        self.pos = place.spots
+
+    def send(self, k, pos, half, dev):
+        one = self.piece(pos, half)
+        self.lanes.send(self.base + k, one, one, self.place.axis, dev)
+
+    def recv(self, k, pos, half, dev):
+        self.lanes.recv(self.base + k, self.piece(pos, half), self.place.axis, dev)
+
+    def begin(self, half):
+        me, up, down, far = self.pos
+        if half == 0:
+            self.send(0, me, 0, self.place.up)
+            self.send(2, me, 0, self.place.down)
+        else:
+            self.send(3, me, 1, self.place.down)
+            self.send(1, me, 1, self.place.up)
+
+    def forward(self):
+        me, up, down, far = self.pos
+        self.recv(0, down, 0, self.place.down)
+        self.send(4, down, 0, self.place.up)
+        self.recv(3, up, 1, self.place.up)
+        self.send(5, up, 1, self.place.down)
+
+    def end(self):
+        me, up, down, far = self.pos
+        self.recv(1, down, 1, self.place.down)
+        self.recv(2, up, 0, self.place.up)
+        self.recv(4, far, 0, self.place.down)
+        self.recv(5, far, 1, self.place.up)
+
+
 def add_into(dst, *srcs):
     total = srcs[0][...].astype(F32)
     for src in srcs[1:]:
@@ -153,7 +199,7 @@
     dst[...] = total.astype(dst.dtype)
 
 
-def scatter_ring(parts, place, lanes, base, bufs, outs):
+def scatter_ring(parts, place, lanes, base, bufs, outs, started=None):
     axis = place.axis
     n = len(parts)
     p = place
@@ -179,8 +225,8 @@
         for i in every:
             send(6 * g + 3, i, parts[i](up, 1), 6 * g + 3, p.up)
             send(6 * g + 4, i, parts[i](down, 0), 6 * g + 4, p.down)
-        if g == 0:
-            continue
+    if started is not None:
+        started()
     for g, (far, up, down, own) in enumerate(groups):
         for i in every:
             recv(6 * g + 0, i, 6 * g + 0, p.down)
@@ -214,53 +260,18 @@
     return [(place.axis, place.up), (place.axis, place.down), (place.axis, place.mate)]
 
 
-def deal_targets(g, n):
-    low = g < n // 2
-    return jnp.where(low, 2 * g, 2 * n - 1 - 2 * g), jnp.where(low, 2 * g + 1, 2 * n - 2 - 2 * g)
-
-
-def deal_sources(c, n):
-    even = lax.rem(c, 2) == 0
-    first = jnp.where(even, c // 2, (2 * n - 1 - c) // 2)
-    second = jnp.where(even, (2 * n - 2 - c) // 2, (c - 1) // 2)
-    return first, second
-
-
-def trade_start(lanes, base, moves, me):
-    for j, (src, dst, to, _) in enumerate(moves):
-
-        @pl.when(to != me)
-        def _(j=j, src=src, dst=dst, to=to):
-            lanes.copy(base + j, src, dst, "ctx", to).start()
-
-
-def trade_finish(lanes, base, moves, me):
-    for j, (src, dst, to, frm) in enumerate(moves):
-
-        @pl.when(to == me)
-        def _(src=src, dst=dst):
-            dst[...] = src[...]
-
-        @pl.when(frm != me)
-        def _(j=j, src=src, dst=dst, frm=frm):
-            lanes.copy(base + j, src, dst, "ctx", frm).wait_recv()
-
-        @pl.when(to != me)
-        def _(j=j, src=src, dst=dst, to=to):
-            lanes.copy(base + j, src, dst, "ctx", to).wait_send()
-
-
 def dispatch_kernel(
-    n_ctx, mi_ref, og_ref, pick_ref, place_ref, key_ref, val_ref,
-    mine_ref, k_out, v_out, send, got, ss, rs,
+    n_ctx, mi_ref, og_ref, pick_ref, place_ref, key_ref, val_ref, q_ref,
+    mine_ref, k_out, v_out, q_row, send, got, ss, rs,
 ):
     me = lax.axis_index("exp")
-    ctx_me = lax.axis_index("ctx")
+    ctx = Place("ctx")
+    swap = n_ctx - 1 - ctx.me
     n_exp = send.shape[0]
     half = key_ref.shape[0] // 2
     greet(
         [("exp", lax.rem(me + d, n_exp)) for d in range(1, n_exp)]
-        + [("ctx", lax.rem(ctx_me + d, n_ctx)) for d in range(1, n_ctx)]
+        + [("ctx", dev) for dev in (ctx.up, ctx.down, swap)]
     )
     lanes = Lanes(ss, rs)
     rows = jnp.dot(pick_ref[:, :128], mi_ref[...], preferred_element_type=F32)
@@ -269,33 +280,41 @@
     for d in range(1, n_exp):
         to = lax.rem(me + d, n_exp)
         lanes.send(d - 1, send.at[to], got.at[d], "exp", to)
-    targets, sources = deal_targets(ctx_me, n_ctx), deal_sources(ctx_me, n_ctx)
-    moves = [
-        (ref.at[pl.ds(h * half, half)], out.at[h], targets[h], sources[h])
-        for h in range(2)
-        for ref, out in ((key_ref, k_out), (val_ref, v_out))
-    ]
-    trade_start(lanes, n_exp - 1, moves, ctx_me)
+    upper = pl.ds(half, half)
+    lanes.send(n_exp - 1, key_ref.at[upper], k_out, "ctx", swap)
+    lanes.send(n_exp, val_ref.at[upper], v_out, "ctx", swap)
+    q_row[lax.rem(ctx.me, 4)] = q_ref[...]
+    ring = Ring(lambda pos, h: q_row.at[pos, pl.ds(h * half, half)], ctx, lanes, n_exp + 1)
+    ring.begin(0)
+    ring.begin(1)
     got[0] = send[me]
+    ring.forward()
     for d in range(1, n_exp):
         lanes.recv(d - 1, got.at[d], "exp", lax.rem(me + n_exp - d, n_exp))
     flat = got[...].astype(F32).reshape(n_exp * 8, got.shape[2]).astype(BF)
     mine = jnp.dot(place_ref[...], flat, preferred_element_type=F32).astype(BF)
     mine_ref[...] = mine.reshape(2, 2, 16, got.shape[2])
-    trade_finish(lanes, n_exp - 1, moves, ctx_me)
+    lanes.recv(n_exp - 1, k_out, "ctx", swap)
+    lanes.recv(n_exp, v_out, "ctx", swap)
+    ring.end()
     lanes.finish()
 
 
-def dispatch(moe_input, out_grad, pick, place, keys, values):
+def dispatch(moe_input, out_grad, pick, place, keys, values, queries):
     n_exp, n_ctx = lax.axis_size("exp"), lax.axis_size("ctx")
     width = moe_input.shape[1]
-    dealt = jax.ShapeDtypeStruct((2, keys.shape[0] // 2, keys.shape[1]), BF)
-    n_sem = n_exp - 1 + 4
+    dealt = jax.ShapeDtypeStruct((keys.shape[0] // 2, keys.shape[1]), BF)
+    n_sem = n_exp + 1 + RING_LANES
     return pl.pallas_call(
         functools.partial(dispatch_kernel, n_ctx),
-        out_shape=(jax.ShapeDtypeStruct((2, 2, 16, width), BF), dealt, dealt),
-        in_specs=[pl.BlockSpec(memory_space=VM)] * 6,
-        out_specs=(pl.BlockSpec(memory_space=VM),) * 3,
+        out_shape=(
+            jax.ShapeDtypeStruct((2, 2, 16, width), BF),
+            dealt,
+            dealt,
+            jax.ShapeDtypeStruct((4,) + queries.shape, BF),
+        ),
+        in_specs=[pl.BlockSpec(memory_space=VM)] * 7,
+        out_specs=(pl.BlockSpec(memory_space=VM),) * 4,
         scratch_shapes=[
             VM((n_exp, 8, width), BF),
             VM((n_exp, 8, width), BF),
@@ -306,43 +325,125 @@
             collective_id=1, has_side_effects=True, vmem_limit_bytes=VLIM
         ),
         cost_estimate=pl.CostEstimate(flops=10**6, bytes_accessed=10**6, transcendentals=0),
-    )(moe_input, out_grad, pick, place, keys, values)
-
-
-def share_kernel(mine_ref, out_ref, ss, rs):
-    ctx = Place("ctx")
-    greet(around(ctx))
+    )(moe_input, out_grad, pick, place, keys, values, queries)
+
+
+def member_of(e):
+    return (e // 8) * 2 + lax.rem(e, 2)
+
+
+def share_kernel(
+    mine_ref, og_ref, w_ref, o_ref, out_ref, og_row, w_group, o_group, ss, rs
+):
+    ctx, exp = Place("ctx"), Place("exp")
+    others = (exp.twin, exp.mate, exp.mate_twin)
+    greet(around(ctx) + [("exp", d) for d in (exp.up, exp.down) + others])
     lanes = Lanes(ss, rs)
     for a in range(2):
         for k in range(2):
             out_ref[a, k, ctx.me] = mine_ref[a, k]
-    gather_ring([lambda block, half: out_ref.at[half, :, block]], ctx, lanes, 0)
+    half_rows = og_ref.shape[0] // 2
+    ring = Ring(
+        lambda pos, h: og_row.at[pos, pl.ds(h * half_rows, half_rows)], exp, lanes, AG_LANES
+    )
+    og_row[exp.spots[0]] = og_ref[...]
+    me = member_of(exp.me)
+    w_group[me] = w_ref[...]
+    o_group[me] = o_ref[exp.me // 8, :, lax.rem(exp.me, 2)]
+    base = AG_LANES + RING_LANES
+
+    def more():
+        ring.begin(0)
+        ring.begin(1)
+        lanes.send(base, w_ref, w_group.at[me], "exp", exp.mate)
+        lanes.send(base + 1, w_ref, w_group.at[me], "exp", exp.twin)
+        for j, dev in enumerate(others):
+            lanes.send(
+                base + 3 + j, o_ref.at[dev // 8, :, lax.rem(dev, 2)], o_group.at[me], "exp", dev
+            )
+
+    def pass_on():
+        block = w_group.at[member_of(exp.mate)]
+        lanes.recv(base, block, "exp", exp.mate)
+        lanes.send(base + 2, block, block, "exp", exp.twin)
+
+    nothing = lambda: None
+    work = [more, ring.forward, nothing, nothing, pass_on]
+    gather_ring([lambda block, half: out_ref.at[half, :, block]], ctx, lanes, 0, work=work)
+    ring.end()
+    lanes.recv(base + 1, w_group.at[member_of(exp.twin)], "exp", exp.twin)
+    lanes.recv(base + 2, w_group.at[member_of(exp.mate_twin)], "exp", exp.twin)
+    for j, dev in enumerate(others):
+        lanes.recv(base + 3 + j, o_group.at[member_of(dev)], "exp", dev)
     lanes.finish()
 
 
-def share(mine):
+def share(mine, out_grad, w_out, attn_out):
     n_ctx = lax.axis_size("ctx")
+    rows, head = out_grad.shape[0], attn_out.shape[1]
+    n_sem = AG_LANES + RING_LANES + 6
+    vmem = pl.BlockSpec(memory_space=VM)
     return pl.pallas_call(
         share_kernel,
-        out_shape=jax.ShapeDtypeStruct(mine.shape[:2] + (n_ctx,) + mine.shape[2:], BF),
-        in_specs=[pl.BlockSpec(memory_space=VM)],
-        out_specs=pl.BlockSpec(memory_space=VM),
+        out_shape=(
+            jax.ShapeDtypeStruct(mine.shape[:2] + (n_ctx,) + mine.shape[2:], BF),
+            jax.ShapeDtypeStruct((4,) + out_grad.shape, BF),
+            jax.ShapeDtypeStruct((4,) + w_out.shape, BF),
+            jax.ShapeDtypeStruct((4, 4, rows, head), BF),
+        ),
+        in_specs=[vmem] * 4,
+        out_specs=(vmem,) * 4,
         scratch_shapes=[
-            pltpu.SemaphoreType.DMA((AG_LANES,)),
-            pltpu.SemaphoreType.DMA((AG_LANES,)),
+            pltpu.SemaphoreType.DMA((n_sem,)),
+            pltpu.SemaphoreType.DMA((n_sem,)),
         ],
         compiler_params=pltpu.CompilerParams(
             collective_id=5, has_side_effects=True, vmem_limit_bytes=VLIM
         ),
         cost_estimate=pl.CostEstimate(flops=10**6, bytes_accessed=10**6, transcendentals=0),
-    )(mine)
-
-
-def combine_kernel(part_ref, gate_ref, out_ref, gate_out, buf, gate_buf, ss, rs):
+    )(mine, out_grad, w_out, attn_out.reshape(2, 4, 2, rows, head))
+
+
+def combine_kernel(
+    part_ref, gate_ref, q_ref, og_row, w_group, out_ref, gate_out, q_mate, base_out,
+    buf, gate_buf, base_send, ss, rs,
+):
     ctx, exp = Place("ctx"), Place("exp")
-    twin = exp.me + 1 - 2 * lax.rem(exp.me, 2)
-    greet(around(ctx) + around(exp) + [("exp", twin)])
+    twin = exp.twin
+    greet(around(ctx) + around(exp) + [("exp", twin), ("exp", exp.mate_twin)])
     lanes = Lanes(ss, rs)
+    rows = q_ref.shape[0] // 2
+    pos = lax.rem(ctx.me, 4)
+    q_base = 3 * AG_LANES + 16
+    d_base = q_base + 2 + RING_LANES
+    others = (exp.twin, exp.mate, exp.mate_twin)
+
+    def q_piece(at, half):
+        return q_mate.at[at, pl.ds(half * rows, rows)]
+
+    def q_start():
+        for half in range(2):
+            src = q_ref.at[pl.ds(half * rows, rows)]
+            lanes.send(q_base + half, src, q_piece(pos, half), "ctx", ctx.mate)
+        rows_og = og_row[...].reshape(-1, og_row.shape[2])
+        y_lo, core = exp.me // 8, lax.rem(exp.me, 2)
+        for j, dev in enumerate(others + (exp.me,)):
+            value = contract_last(rows_og, w_group[member_of(dev)]).astype(BF)
+            value = value.reshape(base_send.shape[1:])
+            if j < 3:
+                base_send[j] = value
+                lanes.send(
+                    d_base + j, base_send.at[j], base_out.at[y_lo, :, core], "exp", dev
+                )
+            else:
+                base_out[y_lo, :, core] = value
+
+    ring = Ring(q_piece, ctx, lanes, q_base + 2)
+
+    def q_ring(half):
+        lanes.recv(q_base + half, q_piece(pos, half), "ctx", ctx.mate)
+        ring.begin(half)
+
     scatter_ring(
         [
             lambda block, half: part_ref.at[half, block],
@@ -353,6 +454,7 @@
         0,
         [lambda s: buf.at[s], lambda s: gate_buf.at[s]],
         [lambda half: out_ref.at[exp.me, half], lambda half: gate_out.at[half]],
+        q_start,
     )
 
     def piece(block, half):
@@ -360,14 +462,16 @@
 
     base = 2 * AG_LANES
     over = 3 * AG_LANES
-    flip = 1 - 2 * lax.rem(exp.me, 2)
+    flip = exp.flip
     for half in range(2):
         lanes.send(over + 14 + half, piece(exp.me, half), piece(exp.me, half), "exp", twin)
 
     def arrived(k, block, half):
         lanes.send(over + k, piece(block, half), piece(block, half), "exp", twin)
 
-    gather_ring([piece], exp, lanes, base, arrived)
+    work = [lambda: q_ring(0), lambda: q_ring(1), ring.forward]
+    gather_ring([piece], exp, lanes, base, arrived, work)
+    ring.end()
     srcs = {
         0: (exp.mate, 0), 1: (exp.mate, 1), 2: (exp.down, 0), 3: (exp.down, 1),
         4: (exp.up, 1), 5: (exp.up, 0), 6: (exp.far, 0), 7: (exp.far, 1),
@@ -377,24 +481,30 @@
     }
     for k, (block, half) in srcs.items():
         lanes.recv(over + k, piece(block + flip, half), "exp", twin)
+    for j, dev in enumerate(others):
+        lanes.recv(d_base + j, base_out.at[dev // 8, :, lax.rem(dev, 2)], "exp", dev)
     lanes.finish()
 
 
-def combine(part, gate_part):
+def combine(part, gate_part, queries, og_row, w_group):
     n_exp = lax.axis_size("exp")
     rows, width = part.shape[2:]
-    n_sem = 3 * AG_LANES + 16
+    n_sem = 3 * AG_LANES + 16 + 2 + RING_LANES + 3
+    tok, head = og_row.shape[1], queries.shape[1]
     return pl.pallas_call(
         combine_kernel,
         out_shape=(
             jax.ShapeDtypeStruct((n_exp, 2, rows, width), BF),
             jax.ShapeDtypeStruct((2,) + gate_part.shape[2:], F32),
-        ),
-        in_specs=[pl.BlockSpec(memory_space=VM)] * 2,
-        out_specs=(pl.BlockSpec(memory_space=VM),) * 2,
+            jax.ShapeDtypeStruct((4,) + queries.shape, BF),
+            jax.ShapeDtypeStruct((2, 4, 2, tok, head), BF),
+        ),
+        in_specs=[pl.BlockSpec(memory_space=VM)] * 5,
+        out_specs=(pl.BlockSpec(memory_space=VM),) * 4,
         scratch_shapes=[
             VM((14, rows, width), BF),
             VM((14,) + gate_part.shape[2:], F32),
+            VM((3, 4, tok, head), BF),
             pltpu.SemaphoreType.DMA((n_sem,)),
             pltpu.SemaphoreType.DMA((n_sem,)),
         ],
@@ -402,56 +512,87 @@
             collective_id=2, has_side_effects=True, vmem_limit_bytes=VLIM
         ),
         cost_estimate=pl.CostEstimate(flops=10**6, bytes_accessed=10**6, transcendentals=0),
-    )(part, gate_part)
+    )(part, gate_part, queries, og_row, w_group)
 
 
 def spread_kernel(
-    do_ref, delta_ref, og_ref, o_ref, taken_ref, dx_ref,
-    do_all, delta_all, dw_ref, og_buf, dw_acc, ss, rs, load_sems,
+    base_ref, w_ref, o_ref, ids_ref, dx_ref, og_row, o_group,
+    do_all, delta_all, dw_ref, dw_acc, dx_out, taken, dw_buf, ss, rs,
 ):
-    ctx = Place("ctx")
-    greet(around(ctx))
+    ctx, exp = Place("ctx"), Place("exp")
+    greet(around(ctx) + [("exp", exp.twin), ("exp", exp.mate)])
     lanes = Lanes(ss, rs)
-    do_all[ctx.me] = do_ref[...]
-    delta_all[ctx.me] = delta_ref[...]
-    rows = do_ref.shape[0] // 2
-    load_rows = og_buf.shape[1]
-    n_load = og_ref.shape[0] // load_rows
+    chunk = 256
+    rows = base_ref.shape[0] // 2
     n_out, _, part = dw_ref.shape
-
-    def load(j):
-        slot = lax.rem(j, 2)
-        return pltpu.make_async_copy(
-            og_ref.at[pl.ds(j * load_rows, load_rows)], og_buf.at[slot], load_sems.at[slot]
-        )
-
-    load(0).start()
-    dw_acc[...] = jnp.zeros_like(dw_acc)
-
-    def add_rows(j, carry):
-        @pl.when(j + 1 < n_load)
-        def _():
-            load(j + 1).start()
-
-        load(j).wait()
-        o = o_ref[pl.ds(j * load_rows, load_rows), :]
-        slot = lax.rem(j, 2)
+    taken[...] = jnp.zeros_like(taken)
+    dx_out[...] = contract_last(dx_ref[...], w_ref[...]).astype(BF)
+    ones = jnp.ones((8, o_ref.shape[1]), BF)
+
+    def project(j, carry):
+        here = pl.ds(pl.multiple_of(j * chunk, chunk), chunk)
+        o = o_ref[here, :]
+        at = lax.broadcasted_iota(jnp.int32, (chunk, ids_ref.shape[1]), 0) + j * chunk
+        pick = jnp.where(at == ids_ref[...], 1.0, 0.0).astype(BF)
+        value = base_ref[here, :].astype(F32)
+        value = value + jnp.dot(pick, dx_out[...], preferred_element_type=F32)
+        value = value.astype(BF)
+        do_all[ctx.me, here, :] = value
+        taken[...] += contract_first(pick, o)
+        rest = value.astype(F32) * o.astype(F32)
+        total = jnp.zeros((8, chunk), F32)
+        for _ in range(3):
+            term = rest.astype(BF)
+            total = total + contract_last(ones, term)
+            rest = rest - term.astype(F32)
+        delta_all[ctx.me, :, here] = total[0:1]
+        return carry
+
+    def ready(half):
+        first = half * (rows // chunk)
+        lax.fori_loop(first, first + rows // chunk, project, 0)
+
+    base = 2 * AG_LANES
+    n_rows = og_row.shape[0] * og_row.shape[1]
+
+    def term(dev, cols):
+        o = o_group[member_of(dev)].reshape(n_rows, o_ref.shape[1])
+        return contract_first(o, og_row[:, :, cols].reshape(n_rows, part))
+
+    def fill(slot, dev):
         for b in range(n_out):
             cols = pl.ds(b * part, part)
-            dw_acc[:, cols] += contract_first(o, og_buf[slot, :, cols])
-        return carry
-
-    def stretch(first, last):
-        return lambda: lax.fori_loop(first, last, add_rows, 0)
-
-    def close():
+            dw_buf[slot, :, cols] = term(dev, cols).astype(BF)
+
+    def first():
+        fill(0, exp.mate_twin)
+        lanes.send(base, dw_buf.at[0], dw_buf.at[3], "exp", exp.twin)
+        fill(1, exp.mate)
+
+    def second():
+        lanes.recv(base, dw_buf.at[3], "exp", exp.twin)
+        add_into(dw_buf.at[1], dw_buf.at[1], dw_buf.at[3])
+        lanes.send(base + 1, dw_buf.at[1], dw_buf.at[4], "exp", exp.mate)
+
+    def third():
+        fill(2, exp.twin)
+        lanes.send(base + 2, dw_buf.at[2], dw_buf.at[5], "exp", exp.twin)
+
+    def fourth():
+        rows_taken = taken[...].astype(BF)
         for b in range(n_out):
             cols = pl.ds(b * part, part)
-            total = dw_acc[:, cols] + contract_first(taken_ref[...], dx_ref[:, cols])
+            dw_acc[:, cols] = term(exp.me, cols) + contract_first(rows_taken, dx_ref[:, cols])
+
+    def close():
+        lanes.recv(base + 2, dw_buf.at[5], "exp", exp.twin)
+        lanes.recv(base + 1, dw_buf.at[4], "exp", exp.mate)
+        for b in range(n_out):
+            cols = pl.ds(b * part, part)
+            total = dw_acc[:, cols]
+            for slot in (4, 5):
+                total = total + dw_buf[slot, :, cols].astype(F32)
             dw_ref[b] = total.astype(BF)
-
-    quarter = n_load // 4
-    work = [stretch(j * quarter, (j + 1) * quarter) for j in range(4)] + [close]
 
     def piece_do(block, half):
         return do_all.at[block, pl.ds(half * rows, rows)]
@@ -459,37 +600,42 @@
     def piece_delta(block, half):
         return delta_all.at[block, :, pl.ds(half * rows, rows)]
 
-    gather_ring([piece_do, piece_delta], ctx, lanes, 0, work=work)
+    gather_ring(
+        [piece_do, piece_delta], ctx, lanes, 0,
+        work=[first, second, third, fourth], ready=ready,
+    )
+    close()
     lanes.finish()
 
 
-def spread(d_out, delta, og_all, attn_out, out_taken, dx_all):
+def spread(d_base, w_out, attn_out, ids, dx_all, og_row, o_group):
     n_ctx = lax.axis_size("ctx")
-    n_sem = 2 * AG_LANES
-    width = og_all.shape[1]
-    head = d_out.shape[1]
+    n_sem = 2 * AG_LANES + 3
+    tokens, head = d_base.shape
+    width = w_out.shape[1]
     vmem = pl.BlockSpec(memory_space=VM)
     return pl.pallas_call(
         spread_kernel,
         out_shape=(
-            jax.ShapeDtypeStruct((n_ctx,) + d_out.shape, BF),
-            jax.ShapeDtypeStruct((n_ctx,) + delta.shape, F32),
+            jax.ShapeDtypeStruct((n_ctx, tokens, head), BF),
+            jax.ShapeDtypeStruct((n_ctx, 1, tokens), F32),
             jax.ShapeDtypeStruct((n_ctx, head, width // n_ctx), BF),
         ),
-        in_specs=[vmem, vmem, pl.BlockSpec(memory_space=pl.ANY), vmem, vmem, vmem],
+        in_specs=[vmem] * 7,
         out_specs=(vmem,) * 3,
         scratch_shapes=[
-            VM((2, 256, width), BF),
             VM((head, width), F32),
+            VM((dx_all.shape[0], head), BF),
+            VM((dx_all.shape[0], head), F32),
+            VM((6, head, width), BF),
             pltpu.SemaphoreType.DMA((n_sem,)),
             pltpu.SemaphoreType.DMA((n_sem,)),
-            pltpu.SemaphoreType.DMA((2,)),
         ],
         compiler_params=pltpu.CompilerParams(
             collective_id=3, has_side_effects=True, vmem_limit_bytes=VLIM
         ),
         cost_estimate=pl.CostEstimate(flops=10**6, bytes_accessed=10**6, transcendentals=0),
-    )(d_out, delta, og_all, attn_out, out_taken, dx_all)
+    )(d_base, w_out, attn_out, ids, dx_all, og_row, o_group)
 
 
 CHUNK = 1024
@@ -497,24 +643,34 @@
 
 
 def attention_kernel(
-    scale, n_ctx, k_ref, v_ref, q_ref, do_ref, lse_ref, delta_ref, dw_ref,
-    gq_out, gw_out, gk_out, gv_out,
-    dq_part, dk_acc, dv_acc, dq_acc, back, dq_buf, dw_buf, ss, rs,
+    scale, n_ctx, k_own, k_far, v_own, v_far, q_row, q_mate, do_ref, lse_ref, delta_ref, dw_ref,
+    grads_out, gw_out,
+    q_ref, k_ref, v_ref, dq_part, dk_acc, dv_acc, dq_acc, back, dq_buf, dw_buf, ss, rs, load_sems,
 ):
     p = Place("ctx")
     c = p.me
-    greet([("ctx", lax.rem(c + d, n_ctx)) for d in range(1, n_ctx)])
+    swap = n_ctx - 1 - c
+    n_ring = q_row.shape[0]
+    low = c // n_ring
+    loads = [
+        pltpu.make_async_copy(src, q_ref.at[pl.ds(at * n_ring, n_ring)], load_sems.at[j])
+        for j, (src, at) in enumerate(((q_row, low), (q_mate, 1 - low)))
+    ]
+    for one in loads:
+        one.start()
+    greet(around(p) + [("ctx", swap)])
     lanes = Lanes(ss, rs)
     n_chunk = 2 * n_ctx
-    first = jnp.where(lax.rem(c, 2) == 0, c, n_chunk - 1 - c)
-    ids = (first, n_chunk - 1 - first)
+    ids = (2 * c, n_chunk - 1 - 2 * c)
+    k_ref[0], k_ref[1] = k_own[:CHUNK, :], k_far[...]
+    v_ref[0], v_ref[1] = v_own[:CHUNK, :], v_far[...]
     dk_acc[...] = jnp.zeros_like(dk_acc)
     dv_acc[...] = jnp.zeros_like(dv_acc)
 
     def tile(part, group, half, row, key, masked):
         at = half * CHUNK + row
         spot = group * 2 * CHUNK + at
-        q = q_ref[pl.ds(spot, TILE), :]
+        q = q_ref[group, pl.ds(at, TILE), :]
         do = do_ref[group, pl.ds(at, TILE), :]
         lse = lse_ref[:, pl.ds(spot, TILE)] * LOG2E
         delta = delta_ref[group, :, pl.ds(at, TILE)]
@@ -584,17 +740,22 @@
         recv(7, p.up)
         summed(11, 7, (), p.down, 1, p.down)
 
-    plan = {
-        0: [lambda: plain(0, p.mate_far, 0, p.up)],
-        1: [lambda: plain(1, p.mate_far, 1, p.down)],
-        3: [lambda: plain(3, p.mate_up, 1, p.up)],
-        4: [lambda: plain(4, p.mate_down, 0, p.down)],
-        8: [lambda: plain(6, p.far, 0, p.up), near_up],
-        9: [lambda: plain(7, p.far, 1, p.down), near_down],
-        11: [lambda: plain(9, p.up, 1, p.up), own_up, lambda: over(0)],
-        12: [lambda: plain(10, p.down, 0, p.down), lambda: over(1)],
-        13: [own_down],
-    }
+    plan = [
+        (0, 0, lambda: plain(0, p.mate_far, 0, p.up)),
+        (1, 1, lambda: plain(1, p.mate_far, 1, p.down)),
+        (3, 3, lambda: plain(3, p.mate_up, 1, p.up)),
+        (4, 4, lambda: plain(4, p.mate_down, 0, p.down)),
+        (3, 9, near_up),
+        (5, 9, near_down),
+        (7, 11, lambda: over(0)),
+        (8, 12, lambda: over(1)),
+        (8, 8, lambda: plain(6, p.far, 0, p.up)),
+        (9, 9, lambda: plain(7, p.far, 1, p.down)),
+        (11, 11, lambda: plain(9, p.up, 1, p.up)),
+        (12, 12, lambda: plain(10, p.down, 0, p.down)),
+        (13, 13, own_up),
+        (13, 13, own_down),
+    ]
     order = [p.mate_far, p.mate_up, p.mate_down, p.mate, p.far, p.up, p.down, p.me]
 
     def step(t, carry):
@@ -620,30 +781,22 @@
                         tile(part, group, half, row, key, key == row)
 
         dq_part[group, pl.ds(half * CHUNK, CHUNK), :] = (dq_acc[...] * scale).astype(BF)
-        for when, acts in plan.items():
-
-            @pl.when(t == when)
-            def _(acts=acts):
-                for act in acts:
-                    act()
+        for early, late, act in plan:
+            pl.when(t == jnp.where(low == 0, early, late))(act)
 
         return carry
 
+    for one in loads:
+        one.wait()
     lax.fori_loop(0, n_chunk, step, 0)
 
-    targets, sources = deal_targets(c, n_ctx), deal_sources(c, n_ctx)
-    for part in range(2):
-        back[part, 0] = (dk_acc[part] * scale).astype(BF)
-        back[part, 1] = dv_acc[part].astype(BF)
-    moves = [
-        (back.at[h, j], out.at[pl.ds(h * CHUNK, CHUNK)], sources[h], targets[h])
-        for h in range(2)
-        for j, out in enumerate((gk_out, gv_out))
-    ]
     base = n * AG_LANES
-    trade_start(lanes, base, moves, c)
+    for j, (acc, factor) in enumerate(((dk_acc, scale), (dv_acc, 1.0))):
+        back[j] = (acc[1] * factor).astype(BF)
+        lanes.send(base + j, back.at[j], grads_out.at[1 + j, pl.ds(CHUNK, CHUNK)], "ctx", swap)
+        grads_out[1 + j, :CHUNK, :] = (acc[0] * factor).astype(BF)
     finals = (
-        lambda h: gq_out.at[pl.ds(h * CHUNK, CHUNK)],
+        lambda h: grads_out.at[0, pl.ds(h * CHUNK, CHUNK)],
         lambda h: gw_out.at[pl.ds(h * w_rows, w_rows)],
     )
     for h in range(2):
@@ -658,30 +811,38 @@
     for k in range(AG_LANES):
         for i in range(n):
             lanes.copy(k * n + i, slots[i](k), slots[i](k), "ctx", p.up).wait_send()
-    trade_finish(lanes, base, moves, c)
-
-
-def attention(k, v, q_all, do_all, lse, delta_all, dw_part, scale):
-    total, head = q_all.shape
-    n_ctx, tok_ctx, _ = do_all.shape
+    for j in range(2):
+        lanes.recv(base + j, grads_out.at[1 + j, pl.ds(CHUNK, CHUNK)], "ctx", swap)
+    lanes.finish()
+
+
+def attention(keys, k_far, values, v_far, q_row, q_mate, do_all, lse, delta_all, dw_part, scale):
+    n_ctx, tok_ctx, head = do_all.shape
     vmem = pl.BlockSpec(memory_space=VM)
-    own = jax.ShapeDtypeStruct((tok_ctx, head), BF)
-    n_sem = 2 * AG_LANES + 4
+    anyw = pl.BlockSpec(memory_space=pl.ANY)
+    n_sem = 2 * AG_LANES + 2
     return pl.pallas_call(
         functools.partial(attention_kernel, scale, n_ctx),
-        out_shape=(own, jax.ShapeDtypeStruct(dw_part.shape[1:], BF), own, own),
-        in_specs=[vmem] * 7,
-        out_specs=(vmem,) * 4,
+        out_shape=(
+            jax.ShapeDtypeStruct((3, tok_ctx, head), BF),
+            jax.ShapeDtypeStruct(dw_part.shape[1:], BF),
+        ),
+        in_specs=[vmem] * 4 + [anyw] * 2 + [vmem] * 4,
+        out_specs=(vmem,) * 2,
         scratch_shapes=[
+            VM(do_all.shape, BF),
+            VM((2, CHUNK, head), BF),
+            VM((2, CHUNK, head), BF),
             VM(do_all.shape, BF),
             VM((2, CHUNK, head), F32),
             VM((2, CHUNK, head), F32),
             VM((CHUNK, head), F32),
-            VM((2, 2, CHUNK, head), BF),
+            VM((2, CHUNK, head), BF),
             VM((AG_LANES, CHUNK, head), BF),
             VM((AG_LANES, dw_part.shape[1] // 2, dw_part.shape[2]), BF),
             pltpu.SemaphoreType.DMA((n_sem,)),
             pltpu.SemaphoreType.DMA((n_sem,)),
+            pltpu.SemaphoreType.DMA((2,)),
         ],
         compiler_params=pltpu.CompilerParams(
             collective_id=4, has_side_effects=True, vmem_limit_bytes=VLIM
@@ -689,7 +850,7 @@
         cost_estimate=pl.CostEstimate(
             flops=40 * 10**9, bytes_accessed=20 * 10**6, transcendentals=17 * 10**6
         ),
-    )(k, v, q_all, do_all, lse, delta_all, dw_part)
+    )(keys, k_far, values, v_far, q_row, q_mate, do_all, lse, delta_all, dw_part)
 
 
 def body(
@@ -748,12 +909,10 @@
     spots = jnp.stack([spot_x, spot_x + n_local * MOST]).reshape(-1)
     place = (spots[:, None] == jnp.arange(8 * n_exp, dtype=i32)[None, :]).astype(BF)
 
-    mine, k_dealt, v_dealt = dispatch(moe_input, out_grad, pick, place, attn_keys, values)
-    og_late, mine = lax.optimization_barrier((out_grad, mine))
-    og_all = lax.all_gather(og_late, "exp", axis=0, tiled=True)
-    slots = share(mine)
-    q_late, slots = lax.optimization_barrier((queries, slots))
-    q_all = lax.all_gather(q_late, "ctx", axis=0, tiled=True)
+    mine, k_far, v_far, q_row = dispatch(
+        moe_input, out_grad, pick, place, attn_keys, values, queries
+    )
+    slots, og_row, w_group, o_group = share(mine, out_grad, w_out, attn_out)
     slots = slots.reshape(2, n_local, n_ctx * group_picks, feat_width)
     slot_rows, slot_grads = slots[0], slots[1]
 
@@ -773,8 +932,12 @@
         jnp.einsum("kcf,kdf->kcd", d_gate, w_gate, preferred_element_type=F32)
         + jnp.einsum("kcf,kdf->kcd", d_up, w_up, preferred_element_type=F32)
     ).astype(BF)
-    dx_all, gate_sum = combine(
-        dx_part.reshape(n_local, n_ctx, group_picks, feat_width), gate_part
+    dx_all, gate_sum, q_mate, d_base = combine(
+        dx_part.reshape(n_local, n_ctx, group_picks, feat_width),
+        gate_part,
+        queries,
+        og_row,
+        w_group,
     )
     d_gates = gate_sum[:, 0, :group_picks]
     dx_all = dx_all.reshape(-1, feat_width)
@@ -787,7 +950,6 @@
     group_ids = lax.dynamic_slice_in_dim(
         expert_picks, ctx_id * group_picks, group_picks, 1
     ).reshape(-1) - ctx_id * tok_ctx
-    spread_hot = (jnp.arange(tok_ctx, dtype=i32)[:, None] == group_ids[None, :]).astype(BF)
     own_hot = (
         (jnp.arange(tok_dev, dtype=i32) + exp_id * tok_dev)[:, None] == group_ids[None, :]
     ).astype(BF)
@@ -795,21 +957,16 @@
         out_grad.astype(F32) + jnp.dot(own_hot, dx_all, preferred_element_type=F32)
     ).astype(BF)
 
-    d_out_base = contract_last(og_all, w_out)
-    dx_out = contract_last(dx_all, w_out).astype(BF)
-    d_out = (d_out_base + jnp.dot(spread_hot, dx_out, preferred_element_type=F32)).astype(BF)
-    product = d_out.astype(F32) * attn_out.astype(F32)
-    delta = lax.dot_general(
-        jnp.ones((1, head_dim), F32), product, (((1,), (1,)), ((), ())),
-        precision=lax.Precision.HIGHEST, preferred_element_type=F32,
-    )
-    out_taken = contract_first(spread_hot, attn_out).astype(BF)
-    do_all, delta_all, dw_part = spread(d_out, delta, og_all, attn_out, out_taken, dx_all)
-    grad_q, dw_out, grad_k, grad_v = attention(
-        k_dealt, v_dealt, q_all, do_all, log_norm, delta_all, dw_part, key_scale
+    do_all, delta_all, dw_part = spread(
+        d_base.reshape(tok_ctx, head_dim), w_out, attn_out, group_ids[None, :], dx_all,
+        og_row, o_group,
+    )
+    grads, dw_out = attention(
+        attn_keys, k_far, values, v_far, q_row, q_mate, do_all, log_norm, delta_all, dw_part,
+        key_scale,
     )
     return (
-        d_resid, dw_gate, dw_up, dw_down, d_gates, dw_out, grad_q, grad_k, grad_v,
+        d_resid, dw_gate, dw_up, dw_down, d_gates, dw_out, grads[0], grads[1], grads[2],
     )
 
 

time: 372 us -> 328 us (0.88); the launches traced: 366 us -> 328 us
  matrix products: 33.3 us -> 17.7 us
  between operations: 14.3 us -> 0.85 us
  local copies, waits for them, and re-layouts: 16.1 us -> 9.79 us
    dot_general x4 -> x0, matrix products: 18.1 us -> none  [the longest x1 9.18 us: contract_last(): lax.dot_general(left, right, (((1,), (1,)), ((), ())), preferred_element_...]
    unnamed x37 -> x22, local copies, waits for them, and re-layouts: 11.3 us -> 1.7 us
    pallas_call x1, Pallas kernels: 49.3 us -> 42.3 us  [dispatch(): pl.pallas_call(functools.partial(dispatch_kernel, n_ctx), out_shape=(jax....]
    pallas_call x1, Pallas kernels: 56.5 us -> 60.8 us  [combine(): pl.pallas_call(combine_kernel, out_shape=(jax.ShapeDtypeStruct((n_exp, 2,...]
  transfers between devices with their start and end apart: 2 -> 0, of which waited for: 0 -> 0; matrix products, arithmetic and copies ran while one was open for 10% -> 0% of each run, Pallas kernels for 43% -> 0%
where the time goes in v3:
time: 328 us
  Pallas kernels  295 us (90%)
  matrix products  17.7 us (5%)
  local copies, waits for them, and re-layouts  9.79 us (3%)
  other arithmetic  4.45 us (1%)
    pallas_call x1, Pallas kernels, attention(): pl.pallas_call(functools.partial(attention_kernel, scale, n_ctx), out_sha...  88.1 us
    pallas_call x1, Pallas kernels, combine(): pl.pallas_call(combine_kernel, out_shape=(jax.ShapeDtypeStruct((n_exp, 2,...  60.8 us
    pallas_call x1, Pallas kernels, spread(): pl.pallas_call(spread_kernel, out_shape=(jax.ShapeDtypeStruct((n_ctx, tok...  52.4 us
    pallas_call x1, Pallas kernels, share(): pl.pallas_call(share_kernel, out_shape=(jax.ShapeDtypeStruct(mine.shape[:...  51.1 us
    pallas_call x1, Pallas kernels, dispatch(): pl.pallas_call(functools.partial(dispatch_kernel, n_ctx), out_shape=(jax....  42.3 us

profile of v3, /device:TPU:0, one launch (start us, length us, event | category | flops | bytes accessed | tf_op | source)
XLA Modules:
  0.0 327.5 jit_solution(13473950065748299165)
XLA Ops:
  0.7 0.9 broadcast_multiply_fusion
  1.9 0.7 fusion.10.place_ref
  2.6 0.8 convert_reduce_fusion.1
  3.5 0.9 select_reduce_fusion.1
  4.7 0.7 fusion.7.pick_ref
  5.4 42.3 %shard_map.196 = (bf16[2,2,16,4096]{3,2,1,0:T(8,128)(2,1)}, bf16[1024,128]{1,0:T(8,128)(2,1)}, bf16[1024,128]{1,0:T(8,128)(2,1)}, bf16[4,2048,128]{2,1,0:T(8,128)(2,1)}) custom-call(bf16[128,4096]{1,0:T(8,128)(2,1)} %mi_ref.1, bf16[128,4096]{1,0:T(8,128)(2,1)} %og_ref.3, bf16[128,256]{1,0:T(8,128)(2,1)} %fusion.7.pick_ref, ...), custom_call_target="tpu_custom_call" | custom-call | flops 1000000 | bytes 1000000 | tf_op jit(solution)/shard_map/pallas_call | solution.py:308
  47.7 51.1 %shard_map.197 = (bf16[2,2,8,16,4096]{4,3,2,1,0:T(8,128)(2,1)}, bf16[4,128,4096]{2,1,0:T(8,128)(2,1)}, bf16[4,128,4096]{2,1,0:T(8,128)(2,1)}, bf16[4,4,128,128]{3,2,1,0:T(8,128)(2,1)}) custom-call(bf16[2,2,16,4096]{3,2,1,0:T(8,128)(2,1)} %get-tuple-element.26.mine_ref, bf16[128,4096]{1,0:T(8,128)(2,1)} %og_ref.3, bf16[128,4096]{1,0:T(8,128)(2,1)} %w_ref.3, ...), custom_call_target="tpu_custom_call" | custom-call | flops 1000000 | bytes 1000000 | tf_op jit(solution)/shard_map/pallas_call | solution.py:386
  98.8 2.9 fusion.21
  101.9 0.9 fusion.22
  102.8 1.1 fusion.23
  103.9 0.7 constant_dynamic-slice_fusion
  104.9 0.9 multiply_reduce_fusion
  105.9 0.8 fusion.24
  106.6 2.2 fusion
  109.5 60.8 %shard_map.198 = (bf16[16,2,16,4096]{3,2,1,0:T(8,128)(2,1)}, f32[2,1,128]{2,1,0:T(1,128)}, bf16[4,2048,128]{2,1,0:T(8,128)(2,1)}, bf16[2,4,2,128,128]{4,3,2,1,0:T(8,128)(2,1)}) custom-call(bf16[2,8,16,4096]{3,2,1,0:T(8,128)(2,1)} %bitcast.44, f32[2,8,1,128]{3,2,1,0:T(1,128)} %pad.4.gate_ref, bf16[2048,128]{1,0:T(8,128)(2,1)} %q_ref.3, ...), custom_call_target="tpu_custom_call" | custom-call | flops 1000000 | bytes 1000000 | tf_op jit(solution)/shard_map/pallas_call | solution.py:494
  170.4 0.7 sub.95.ids_ref
  171.1 52.4 %shard_map.199 = (bf16[8,2048,128]{2,1,0:T(8,128)(2,1)}, f32[8,1,2048]{2,1,0:T(1,128)}, bf16[8,128,512]{2,1,0:T(8,128)(2,1)}) custom-call(bf16[2048,128]{1,0:T(8,128)(2,1)} %bitcast.46, bf16[128,4096]{1,0:T(8,128)(2,1)} %w_ref.3, bf16[2048,128]{1,0:T(8,128)(2,1)} %o_ref.1, s32[1,512]{1,0:T(1,128)} %sub.95.ids_ref, bf16[512,4096]{1,0:T(8,128)(2,1)} %bitcast.40, ...), custom_call_target="tpu_custom_call" | custom-call | flops 1000000 | bytes 1000000 | tf_op jit(solution)/shard_map/pallas_call | solution.py:617
  223.5 88.1 %shard_map.200 = (bf16[3,2048,128]{2,1,0:T(8,128)(2,1)}, bf16[128,512]{1,0:T(8,128)(2,1)}) custom-call(bf16[2048,128]{1,0:T(8,128)(2,1)} %k_own.1, bf16[1024,128]{1,0:T(8,128)(2,1)} %get-tuple-element.32.k_far, bf16[2048,128]{1,0:T(8,128)(2,1)} %v_own.1, bf16[1024,128]{1,0:T(8,128)(2,1)} %get-tuple-element.33.v_far, ...), custom_call_target="tpu_custom_call" | custom-call | flops 40000000000 | bytes 20000000 | tf_op jit(solution)/shard_map/pallas_call | solution.py:824
  311.7 2.7 slice_bitcast_fusion
  314.4 2.6 convolution_convert_fusion.2
  317.0 2.5 convolution_convert_fusion
  319.5 2.5 convolution_convert_fusion.1
  322.0 4.2 %fusion.1 = bf16[128,4096]{1,0:T(8,128)(2,1)} fusion(bf16[512,4096]{1,0:T(8,128)(2,1)} %bitcast.41, bf16[128,4096]{1,0:T(8,128)(2,1)} %og_ref.3, s32[512]{0:T(512)S(1)} %sub.78, s32[128]{0:T(128)S(1)} %iota_add_fusion), kind=kOutput, calls=%fused_computation.6 | convolution fusion | flops 538509312 | bytes 6294016 | tf_op jit(solution)/shard_map/dot_general | solution.py:957
  326.9 0.7 copy.35
  (39 shorter events, 2.6 us)
Async XLA Ops:
  0.6 102.1 %copy-start = (bf16[2,4096,176]{1,2,0:T(8,128)(2,1)S(1)}, bf16[2,4096,176]{1,2,0:T(8,128)(2,1)}, u32[]{:S(2)}) copy-start(bf16[2,4096,176]{1,2,0:T(8,128)(2,1)} %param.15) | copy-start | bytes 8650756
  98.8 3.1 copy-start.3
  101.7 2.2 copy-start.1
  101.7 3.0 copy-start.4
  102.8 2.1 copy-start.9
  109.5 60.9 %copy-start.6 = (s32[32,128]{1,0:T(8,128)S(1)}, s32[32,128]{1,0:T(8,128)}, u32[]{:S(2)}) copy-start(s32[32,128]{1,0:T(8,128)} %param.18) | copy-start | bytes 49156
  311.7 2.7 copy-start.5
  314.4 2.6 copy-start.2
  322.0 4.3 %copy-start.8 = (f32[2,1,128]{2,1,0:T(1,128)S(1)}, f32[2,1,128]{2,1,0:T(1,128)}, u32[]{:S(2)}) copy-start(f32[2,1,128]{2,1,0:T(1,128)} %get-tuple-element.31) | copy-start | bytes 3076
  322.0 4.8 %copy-start.7 = (bf16[128,512]{1,0:T(8,128)(2,1)S(1)}, bf16[128,512]{1,0:T(8,128)(2,1)}, u32[]{:S(2)}) copy-start(bf16[128,512]{1,0:T(8,128)(2,1)} %get-tuple-element.74) | copy-start | bytes 393220

commit v4 on v3

--- a/solution.py
+++ b/solution.py
@@ -15,6 +15,8 @@
 F32 = jnp.float32
 VLIM = 56 * 1024 * 1024
 VM = pltpu.VMEM
+VMEM_SPEC = pl.BlockSpec(memory_space=pltpu.VMEM)
+ANY_SPEC = pl.BlockSpec(memory_space=pl.ANY)
 
 
 def activation(pre_act):
@@ -65,7 +67,7 @@
 
 class Lanes:
     def __init__(self, send_sems, recv_sems):
-        self.send_sems, self.recv_sems, self.sent = send_sems, recv_sems, []
+        self.send_sems, self.recv_sems, self.sent, self.local = send_sems, recv_sems, [], []
 
     def copy(self, k, src, dst, axis, dev):
         return pltpu.make_async_remote_copy(
@@ -88,12 +90,19 @@
     def finish(self):
         for one in self.sent:
             one.wait_send()
+        for one in self.local:
+            one.wait()
+
+    def keep(self, sem, src, dst):
+        one = pltpu.make_async_copy(src, dst, sem)
+        one.start()
+        self.local.append(one)
 
 
 AG_LANES = 14
 
 
-def gather_ring(pieces, place, lanes, base, arrived=None, work=(), ready=None):
+def gather_ring(pieces, place, lanes, base, arrived=None, work=(), ready=None, own=None):
     axis = place.axis
     n = len(pieces)
     work = list(work)
@@ -104,7 +113,8 @@
 
     def send(k, block, half, dev):
         for i, piece in enumerate(pieces):
-            lanes.send(base + k * n + i, piece(block, half), piece(block, half), axis, dev)
+            src = piece(block, half) if own is None or k > 5 else own[i](half)
+            lanes.send(base + k * n + i, src, piece(block, half), axis, dev)
 
     def recv(k, block, half, dev):
         for i, piece in enumerate(pieces):
@@ -157,13 +167,15 @@
 
 
 class Ring:
-    def __init__(self, piece, place, lanes, base):
+    def __init__(self, piece, place, lanes, base, own=None):
         self.piece, self.place, self.lanes, self.base = piece, place, lanes, base
+        self.own = own
         self.pos = place.spots
 
     def send(self, k, pos, half, dev):
         one = self.piece(pos, half)
-        self.lanes.send(self.base + k, one, one, self.place.axis, dev)
+        src = one if self.own is None or k > 3 else self.own(half)
+        self.lanes.send(self.base + k, src, one, self.place.axis, dev)
 
     def recv(self, k, pos, half, dev):
         self.lanes.recv(self.base + k, self.piece(pos, half), self.place.axis, dev)
@@ -262,7 +274,7 @@
 
 def dispatch_kernel(
     n_ctx, mi_ref, og_ref, pick_ref, place_ref, key_ref, val_ref, q_ref,
-    mine_ref, k_out, v_out, q_row, send, got, ss, rs,
+    mine_ref, k_out, v_out, q_row, send, got, ss, rs, keep_sem,
 ):
     me = lax.axis_index("exp")
     ctx = Place("ctx")
@@ -274,19 +286,22 @@
         + [("ctx", dev) for dev in (ctx.up, ctx.down, swap)]
     )
     lanes = Lanes(ss, rs)
+    upper = pl.ds(half, half)
+    ring = Ring(
+        lambda pos, h: q_row.at[pos, pl.ds(h * half, half)], ctx, lanes, n_exp + 1,
+        lambda h: q_ref.at[pl.ds(h * half, half)],
+    )
+    ring.begin(0)
+    ring.begin(1)
+    lanes.send(n_exp - 1, key_ref.at[upper], k_out, "ctx", swap)
+    lanes.send(n_exp, val_ref.at[upper], v_out, "ctx", swap)
+    lanes.keep(keep_sem, q_ref, q_row.at[ctx.spots[0]])
     rows = jnp.dot(pick_ref[:, :128], mi_ref[...], preferred_element_type=F32)
     rows = rows + jnp.dot(pick_ref[:, 128:], og_ref[...], preferred_element_type=F32)
     send[...] = rows.reshape(n_exp, 8, rows.shape[1]).astype(BF)
     for d in range(1, n_exp):
         to = lax.rem(me + d, n_exp)
         lanes.send(d - 1, send.at[to], got.at[d], "exp", to)
-    upper = pl.ds(half, half)
-    lanes.send(n_exp - 1, key_ref.at[upper], k_out, "ctx", swap)
-    lanes.send(n_exp, val_ref.at[upper], v_out, "ctx", swap)
-    q_row[lax.rem(ctx.me, 4)] = q_ref[...]
-    ring = Ring(lambda pos, h: q_row.at[pos, pl.ds(h * half, half)], ctx, lanes, n_exp + 1)
-    ring.begin(0)
-    ring.begin(1)
     got[0] = send[me]
     ring.forward()
     for d in range(1, n_exp):
@@ -313,13 +328,14 @@
             dealt,
             jax.ShapeDtypeStruct((4,) + queries.shape, BF),
         ),
-        in_specs=[pl.BlockSpec(memory_space=VM)] * 7,
-        out_specs=(pl.BlockSpec(memory_space=VM),) * 4,
+        in_specs=[VMEM_SPEC] * 4 + [ANY_SPEC] * 3,
+        out_specs=(VMEM_SPEC,) + (ANY_SPEC,) * 3,
         scratch_shapes=[
             VM((n_exp, 8, width), BF),
             VM((n_exp, 8, width), BF),
             pltpu.SemaphoreType.DMA((n_sem,)),
             pltpu.SemaphoreType.DMA((n_sem,)),
+            pltpu.SemaphoreType.DMA,
         ],
         compiler_params=pltpu.CompilerParams(
             collective_id=1, has_side_effects=True, vmem_limit_bytes=VLIM
@@ -333,26 +349,26 @@
 
 
 def share_kernel(
-    mine_ref, og_ref, w_ref, o_ref, out_ref, og_row, w_group, o_group, ss, rs
+    mine_ref, og_ref, w_ref, o_ref, out_ref, og_row, w_group, o_group, ss, rs, keep_sems
 ):
     ctx, exp = Place("ctx"), Place("exp")
     others = (exp.twin, exp.mate, exp.mate_twin)
     greet(around(ctx) + [("exp", d) for d in (exp.up, exp.down) + others])
     lanes = Lanes(ss, rs)
-    for a in range(2):
-        for k in range(2):
-            out_ref[a, k, ctx.me] = mine_ref[a, k]
     half_rows = og_ref.shape[0] // 2
     ring = Ring(
-        lambda pos, h: og_row.at[pos, pl.ds(h * half_rows, half_rows)], exp, lanes, AG_LANES
-    )
-    og_row[exp.spots[0]] = og_ref[...]
+        lambda pos, h: og_row.at[pos, pl.ds(h * half_rows, half_rows)], exp, lanes, AG_LANES,
+        lambda h: og_ref.at[pl.ds(h * half_rows, half_rows)],
+    )
     me = member_of(exp.me)
-    w_group[me] = w_ref[...]
-    o_group[me] = o_ref[exp.me // 8, :, lax.rem(exp.me, 2)]
     base = AG_LANES + RING_LANES
 
     def more():
+        lanes.keep(keep_sems.at[0], mine_ref, out_ref.at[:, :, ctx.me])
+        lanes.keep(keep_sems.at[1], og_ref, og_row.at[exp.spots[0]])
+        lanes.keep(keep_sems.at[2], w_ref, w_group.at[me])
+        own_o = o_ref.at[exp.me // 8, :, lax.rem(exp.me, 2)]
+        lanes.keep(keep_sems.at[3], own_o, o_group.at[me])
         ring.begin(0)
         ring.begin(1)
         lanes.send(base, w_ref, w_group.at[me], "exp", exp.mate)
@@ -369,7 +385,10 @@
 
     nothing = lambda: None
     work = [more, ring.forward, nothing, nothing, pass_on]
-    gather_ring([lambda block, half: out_ref.at[half, :, block]], ctx, lanes, 0, work=work)
+    gather_ring(
+        [lambda block, half: out_ref.at[half, :, block]], ctx, lanes, 0, work=work,
+        own=[lambda half: mine_ref.at[half]],
+    )
     ring.end()
     lanes.recv(base + 1, w_group.at[member_of(exp.twin)], "exp", exp.twin)
     lanes.recv(base + 2, w_group.at[member_of(exp.mate_twin)], "exp", exp.twin)
@@ -392,10 +411,11 @@
             jax.ShapeDtypeStruct((4, 4, rows, head), BF),
         ),
         in_specs=[vmem] * 4,
-        out_specs=(vmem,) * 4,
+        out_specs=(vmem,) + (ANY_SPEC,) * 3,
         scratch_shapes=[
             pltpu.SemaphoreType.DMA((n_sem,)),
             pltpu.SemaphoreType.DMA((n_sem,)),
+            pltpu.SemaphoreType.DMA((4,)),
         ],
         compiler_params=pltpu.CompilerParams(
             collective_id=5, has_side_effects=True, vmem_limit_bytes=VLIM
@@ -405,11 +425,17 @@
 
 
 def combine_kernel(
-    part_ref, gate_ref, q_ref, og_row, w_group, out_ref, gate_out, q_mate, base_out,
-    buf, gate_buf, base_send, ss, rs,
+    part_ref, gate_ref, q_ref, og_far, w_far, out_ref, gate_out, q_mate, base_out,
+    buf, gate_buf, base_send, own_dx, og_row, w_group, ss, rs, keep_sems,
 ):
     ctx, exp = Place("ctx"), Place("exp")
     twin = exp.twin
+    loads = [
+        pltpu.make_async_copy(src, dst, keep_sems.at[j])
+        for j, (src, dst) in enumerate(((og_far, og_row), (w_far, w_group)))
+    ]
+    for one in loads:
+        one.start()
     greet(around(ctx) + around(exp) + [("exp", twin), ("exp", exp.mate_twin)])
     lanes = Lanes(ss, rs)
     rows = q_ref.shape[0] // 2
@@ -425,18 +451,19 @@
         for half in range(2):
             src = q_ref.at[pl.ds(half * rows, rows)]
             lanes.send(q_base + half, src, q_piece(pos, half), "ctx", ctx.mate)
+        for one in loads:
+            one.wait()
         rows_og = og_row[...].reshape(-1, og_row.shape[2])
         y_lo, core = exp.me // 8, lax.rem(exp.me, 2)
         for j, dev in enumerate(others + (exp.me,)):
             value = contract_last(rows_og, w_group[member_of(dev)]).astype(BF)
             value = value.reshape(base_send.shape[1:])
+            base_send[j] = value
+            to = base_out.at[y_lo, :, core]
             if j < 3:
-                base_send[j] = value
-                lanes.send(
-                    d_base + j, base_send.at[j], base_out.at[y_lo, :, core], "exp", dev
-                )
+                lanes.send(d_base + j, base_send.at[j], to, "exp", dev)
             else:
-                base_out[y_lo, :, core] = value
+                lanes.keep(keep_sems.at[2], base_send.at[j], to)
 
     ring = Ring(q_piece, ctx, lanes, q_base + 2)
 
@@ -453,7 +480,7 @@
         lanes,
         0,
         [lambda s: buf.at[s], lambda s: gate_buf.at[s]],
-        [lambda half: out_ref.at[exp.me, half], lambda half: gate_out.at[half]],
+        [lambda half: own_dx.at[half], lambda half: gate_out.at[half]],
         q_start,
     )
 
@@ -464,13 +491,14 @@
     over = 3 * AG_LANES
     flip = exp.flip
     for half in range(2):
-        lanes.send(over + 14 + half, piece(exp.me, half), piece(exp.me, half), "exp", twin)
+        lanes.send(over + 14 + half, own_dx.at[half], piece(exp.me, half), "exp", twin)
+    lanes.keep(keep_sems.at[3], own_dx, out_ref.at[exp.me])
 
     def arrived(k, block, half):
         lanes.send(over + k, piece(block, half), piece(block, half), "exp", twin)
 
     work = [lambda: q_ring(0), lambda: q_ring(1), ring.forward]
-    gather_ring([piece], exp, lanes, base, arrived, work)
+    gather_ring([piece], exp, lanes, base, arrived, work, own=[lambda half: own_dx.at[half]])
     ring.end()
     srcs = {
         0: (exp.mate, 0), 1: (exp.mate, 1), 2: (exp.down, 0), 3: (exp.down, 1),
@@ -499,14 +527,18 @@
             jax.ShapeDtypeStruct((4,) + queries.shape, BF),
             jax.ShapeDtypeStruct((2, 4, 2, tok, head), BF),
         ),
-        in_specs=[pl.BlockSpec(memory_space=VM)] * 5,
-        out_specs=(pl.BlockSpec(memory_space=VM),) * 4,
+        in_specs=[VMEM_SPEC] * 2 + [ANY_SPEC] * 3,
+        out_specs=(ANY_SPEC, VMEM_SPEC, ANY_SPEC, ANY_SPEC),
         scratch_shapes=[
             VM((14, rows, width), BF),
             VM((14,) + gate_part.shape[2:], F32),
-            VM((3, 4, tok, head), BF),
+            VM((4, 4, tok, head), BF),
+            VM((2, rows, width), BF),
+            VM(og_row.shape, BF),
+            VM(w_group.shape, BF),
             pltpu.SemaphoreType.DMA((n_sem,)),
             pltpu.SemaphoreType.DMA((n_sem,)),
+            pltpu.SemaphoreType.DMA((4,)),
         ],
         compiler_params=pltpu.CompilerParams(
             collective_id=2, has_side_effects=True, vmem_limit_bytes=VLIM
@@ -516,10 +548,13 @@
 
 
 def spread_kernel(
-    base_ref, w_ref, o_ref, ids_ref, dx_ref, og_row, o_group,
-    do_all, delta_all, dw_ref, dw_acc, dx_out, taken, dw_buf, ss, rs,
+    base_ref, w_ref, o_ref, ids_ref, dx_ref, og_far, o_group,
+    do_all, delta_all, dw_ref,
+    own_do, own_delta, og_row, dw_acc, dx_out, taken, dw_buf, ss, rs, keep_sems,
 ):
     ctx, exp = Place("ctx"), Place("exp")
+    load = pltpu.make_async_copy(og_far, og_row, keep_sems.at[0])
+    load.start()
     greet(around(ctx) + [("exp", exp.twin), ("exp", exp.mate)])
     lanes = Lanes(ss, rs)
     chunk = 256
@@ -537,7 +572,7 @@
         value = base_ref[here, :].astype(F32)
         value = value + jnp.dot(pick, dx_out[...], preferred_element_type=F32)
         value = value.astype(BF)
-        do_all[ctx.me, here, :] = value
+        own_do[here, :] = value
         taken[...] += contract_first(pick, o)
         rest = value.astype(F32) * o.astype(F32)
         total = jnp.zeros((8, chunk), F32)
@@ -545,7 +580,7 @@
             term = rest.astype(BF)
             total = total + contract_last(ones, term)
             rest = rest - term.astype(F32)
-        delta_all[ctx.me, :, here] = total[0:1]
+        own_delta[:, here] = total[0:1]
         return carry
 
     def ready(half):
@@ -565,6 +600,9 @@
             dw_buf[slot, :, cols] = term(dev, cols).astype(BF)
 
     def first():
+        lanes.keep(keep_sems.at[1], own_do, do_all.at[ctx.me])
+        lanes.keep(keep_sems.at[2], own_delta, delta_all.at[ctx.me])
+        load.wait()
         fill(0, exp.mate_twin)
         lanes.send(base, dw_buf.at[0], dw_buf.at[3], "exp", exp.twin)
         fill(1, exp.mate)
@@ -603,6 +641,10 @@
     gather_ring(
         [piece_do, piece_delta], ctx, lanes, 0,
         work=[first, second, third, fourth], ready=ready,
+        own=[
+            lambda half: own_do.at[pl.ds(half * rows, rows)],
+            lambda half: own_delta.at[:, pl.ds(half * rows, rows)],
+        ],
     )
     close()
     lanes.finish()
@@ -621,15 +663,19 @@
             jax.ShapeDtypeStruct((n_ctx, 1, tokens), F32),
             jax.ShapeDtypeStruct((n_ctx, head, width // n_ctx), BF),
         ),
-        in_specs=[vmem] * 7,
-        out_specs=(vmem,) * 3,
+        in_specs=[vmem] * 5 + [ANY_SPEC, vmem],
+        out_specs=(ANY_SPEC, ANY_SPEC, vmem),
         scratch_shapes=[
+            VM((tokens, head), BF),
+            VM((1, tokens), F32),
+            VM(og_row.shape, BF),
             VM((head, width), F32),
             VM((dx_all.shape[0], head), BF),
             VM((dx_all.shape[0], head), F32),
             VM((6, head, width), BF),
             pltpu.SemaphoreType.DMA((n_sem,)),
             pltpu.SemaphoreType.DMA((n_sem,)),
+            pltpu.SemaphoreType.DMA((3,)),
         ],
         compiler_params=pltpu.CompilerParams(
             collective_id=3, has_side_effects=True, vmem_limit_bytes=VLIM
@@ -643,21 +689,23 @@
 
 
 def attention_kernel(
-    scale, n_ctx, k_own, k_far, v_own, v_far, q_row, q_mate, do_ref, lse_ref, delta_ref, dw_ref,
+    scale, n_ctx, k_own, k_far, v_own, v_far, q_row, q_mate, do_far, lse_ref, delta_ref, dw_ref,
     grads_out, gw_out,
-    q_ref, k_ref, v_ref, dq_part, dk_acc, dv_acc, dq_acc, back, dq_buf, dw_buf, ss, rs, load_sems,
+    q_ref, do_ref, k_ref, v_ref, hold, dq_part, dk_acc, dv_acc, dq_acc, back, dq_buf, dw_buf, ss, rs, load_sems,
 ):
     p = Place("ctx")
     c = p.me
     swap = n_ctx - 1 - c
     n_ring = q_row.shape[0]
     low = c // n_ring
-    loads = [
-        pltpu.make_async_copy(src, q_ref.at[pl.ds(at * n_ring, n_ring)], load_sems.at[j])
-        for j, (src, at) in enumerate(((q_row, low), (q_mate, 1 - low)))
-    ]
-    for one in loads:
-        one.start()
+    order = [p.mate_far, p.mate_up, p.mate_down, p.mate, p.far, p.up, p.down, p.me]
+    for j in (4, 0, 5, 1, 6, 2, 3, 7):
+        src = q_row if j > 3 else q_mate
+        block = order[j]
+        pltpu.make_async_copy(
+            src.at[lax.rem(block, n_ring)], q_ref.at[block], load_sems.at[0, j]
+        ).start()
+        pltpu.make_async_copy(do_far.at[block], do_ref.at[block], load_sems.at[1, j]).start()
     greet(around(p) + [("ctx", swap)])
     lanes = Lanes(ss, rs)
     n_chunk = 2 * n_ctx
@@ -698,112 +746,144 @@
     slots = (lambda s: dq_buf.at[s], lambda s: dw_buf.at[s])
     n = len(parts)
 
-    def send(k, src, dev):
-        for i in range(n):
-            lanes.copy(k * n + i, src[i], slots[i](k), "ctx", dev).start()
-
-    def recv(k, dev):
-        for i in range(n):
-            lanes.copy(k * n + i, slots[i](k), slots[i](k), "ctx", dev).wait_recv()
-
-    def terms(block, h):
-        return [parts[i](block, h) for i in range(n)]
-
-    def plain(k, block, h, dev):
-        send(k, terms(block, h), dev)
-
-    def summed(k, into, others, block, h, dev):
-        for i in range(n):
-            add_into(
-                slots[i](into), slots[i](into), *[slots[i](o) for o in others], parts[i](block, h)
-            )
-        send(k, [slots[i](into) for i in range(n)], dev)
-
-    def near_up():
-        recv(0, p.down)
-        summed(2, 0, (), p.mate_up, 0, p.up)
-
-    def near_down():
-        recv(1, p.up)
-        summed(5, 1, (), p.mate_down, 1, p.down)
-
-    def over(h):
-        recv(2 + h, p.down)
-        recv(4 + h, p.up)
-        summed(12 + h, 2 + h, (4 + h,), p.mate, h, p.mate)
-
-    def own_up():
-        recv(6, p.down)
-        summed(8, 6, (), p.up, 0, p.up)
-
-    def own_down():
-        recv(7, p.up)
-        summed(11, 7, (), p.down, 1, p.down)
-
-    plan = [
-        (0, 0, lambda: plain(0, p.mate_far, 0, p.up)),
-        (1, 1, lambda: plain(1, p.mate_far, 1, p.down)),
-        (3, 3, lambda: plain(3, p.mate_up, 1, p.up)),
-        (4, 4, lambda: plain(4, p.mate_down, 0, p.down)),
-        (3, 9, near_up),
-        (5, 9, near_down),
-        (7, 11, lambda: over(0)),
-        (8, 12, lambda: over(1)),
-        (8, 8, lambda: plain(6, p.far, 0, p.up)),
-        (9, 9, lambda: plain(7, p.far, 1, p.down)),
-        (11, 11, lambda: plain(9, p.up, 1, p.up)),
-        (12, 12, lambda: plain(10, p.down, 0, p.down)),
-        (13, 13, own_up),
-        (13, 13, own_down),
+    def send(i, k, src, dev):
+        lanes.copy(k * n + i, src, slots[i](k), "ctx", dev).start()
+
+    def recv(i, k, dev):
+        lanes.copy(k * n + i, slots[i](k), slots[i](k), "ctx", dev).wait_recv()
+
+    def plain(i, k, block, h, dev):
+        send(i, k, parts[i](block, h), dev)
+
+    def summed(i, k, into, others, block, h, dev):
+        add_into(
+            slots[i](into), slots[i](into), *[slots[i](o) for o in others], parts[i](block, h)
+        )
+        send(i, k, slots[i](into), dev)
+
+    def near_up(i, g, block):
+        recv(i, 6 * g, p.down)
+        summed(i, 6 * g + 2, 6 * g, (), block, 0, p.up)
+
+    def near_down(i, g, block):
+        recv(i, 6 * g + 1, p.up)
+        summed(i, 6 * g + 5, 6 * g + 1, (), block, 1, p.down)
+
+    def over(i, h):
+        recv(i, 2 + h, p.down)
+        recv(i, 4 + h, p.up)
+        summed(i, 12 + h, 2 + h, (4 + h,), p.mate, h, p.mate)
+
+    rows = ((p.mate_far, p.mate_up, p.mate_down), (p.far, p.up, p.down))
+    base = n * AG_LANES
+    last = n_chunk - 1
+
+    def give_back():
+        for j, (acc, factor) in enumerate(((dk_acc, scale), (dv_acc, 1.0))):
+            back[j] = (acc[1] * factor).astype(BF)
+            back_copy(j).start()
+
+    def back_copy(j):
+        return lanes.copy(
+            base + j, back.at[j], grads_out.at[1 + j, pl.ds(CHUNK, CHUNK)], "ctx", swap
+        )
+
+    plan = []
+    for g, (far, up, down) in enumerate(rows):
+        early = 0 if g == 1 else 2
+        late = 2 - early
+        plan += [
+            (early, late, functools.partial(plain, 0, 6 * g, far, 0, p.up)),
+            (early + 1, late + 1, functools.partial(plain, 0, 6 * g + 1, far, 1, p.down)),
+            (early + 5, late + 5, functools.partial(plain, 0, 6 * g + 3, up, 1, p.up)),
+            (early + 5, late + 5, functools.partial(near_up, 0, g, up)),
+            (early + 8, late + 8, functools.partial(plain, 0, 6 * g + 4, down, 0, p.down)),
+            (early + 9, late + 9, functools.partial(near_down, 0, g, down)),
+            (3, 3, functools.partial(near_up, 1, g, up)),
+            (3, 3, functools.partial(near_down, 1, g, down)),
+        ]
+    plan += [
+        (6, 6, functools.partial(over, 1, 0)),
+        (6, 6, functools.partial(over, 1, 1)),
+        (12, 12, functools.partial(over, 0, 0)),
+        (13, 13, functools.partial(over, 0, 1)),
+        (last, last, give_back),
     ]
-    order = [p.mate_far, p.mate_up, p.mate_down, p.mate, p.far, p.up, p.down, p.me]
+    for g, (far, up, down) in enumerate(rows):
+        plain(1, 6 * g, far, 0, p.up)
+        plain(1, 6 * g + 1, far, 1, p.down)
+        plain(1, 6 * g + 3, up, 1, p.up)
+        plain(1, 6 * g + 4, down, 0, p.down)
+    first_row = (4, 0, 5, 1, 6, 2, 3, 7, 7)
+    other_row = (0, 4, 1, 5, 2, 6, 3, 7, 7)
 
     def step(t, carry):
         place = t // 2
         half = lax.rem(t, 2)
+        spot = jnp.where(low == 0, first_row[0], other_row[0])
+        for j in range(1, len(first_row)):
+            spot = jnp.where(place == j, jnp.where(low == 0, first_row[j], other_row[j]), spot)
         group = order[0]
         for j in range(1, len(order)):
-            group = jnp.where(place == j, order[j], group)
+            group = jnp.where(spot == j, order[j], group)
         chunk = 2 * group + half
-        dq_acc[...] = jnp.zeros_like(dq_acc)
+
+        @pl.when((half == 0) & (t < n_chunk))
+        def _():
+            pltpu.make_async_copy(q_row.at[0], q_ref.at[group], load_sems.at[0, spot]).wait()
+            pltpu.make_async_copy(do_far.at[0], do_ref.at[group], load_sems.at[1, spot]).wait()
+
+        @pl.when(t < n_chunk)
+        def _():
+            dq_acc[...] = jnp.zeros_like(dq_acc)
+
+        @pl.when(t >= n_chunk)
+        def _():
+            dq_acc[...] = hold[half]
+
+        busy = ((t < n_chunk - 2) | (t >= n_chunk), t < n_chunk)
         for part in range(2):
 
-            @pl.when(chunk > ids[part])
+            @pl.when((chunk > ids[part]) & busy[part])
             def _(part=part):
                 for row in range(0, CHUNK, TILE):
                     for key in range(0, CHUNK, TILE):
                         tile(part, group, half, row, key, False)
 
-            @pl.when(chunk == ids[part])
+            @pl.when((chunk == ids[part]) & busy[part])
             def _(part=part):
                 for row in range(0, CHUNK, TILE):
                     for key in range(0, row + 1, TILE):
                         tile(part, group, half, row, key, key == row)
 
-        dq_part[group, pl.ds(half * CHUNK, CHUNK), :] = (dq_acc[...] * scale).astype(BF)
+        keep = (t >= n_chunk - 2) & (t < n_chunk)
+
+        @pl.when(keep)
+        def _():
+            hold[half] = dq_acc[...]
+
+        @pl.when(jnp.logical_not(keep))
+        def _():
+            dq_part[group, pl.ds(half * CHUNK, CHUNK), :] = (dq_acc[...] * scale).astype(BF)
+
         for early, late, act in plan:
             pl.when(t == jnp.where(low == 0, early, late))(act)
 
         return carry
 
-    for one in loads:
-        one.wait()
-    lax.fori_loop(0, n_chunk, step, 0)
-
-    base = n * AG_LANES
+    lax.fori_loop(0, n_chunk + 2, step, 0)
+
     for j, (acc, factor) in enumerate(((dk_acc, scale), (dv_acc, 1.0))):
-        back[j] = (acc[1] * factor).astype(BF)
-        lanes.send(base + j, back.at[j], grads_out.at[1 + j, pl.ds(CHUNK, CHUNK)], "ctx", swap)
         grads_out[1 + j, :CHUNK, :] = (acc[0] * factor).astype(BF)
     finals = (
         lambda h: grads_out.at[0, pl.ds(h * CHUNK, CHUNK)],
         lambda h: gw_out.at[pl.ds(h * w_rows, w_rows)],
     )
     for h in range(2):
-        recv(8 + h, p.down)
-        recv(10 + h, p.up)
-        recv(12 + h, p.mate)
         for i in range(n):
+            recv(i, 8 + h, p.down)
+            recv(i, 10 + h, p.up)
+            recv(i, 12 + h, p.mate)
             add_into(
                 finals[i](h), slots[i](8 + h), slots[i](10 + h), slots[i](12 + h),
                 parts[i](p.me, h),
@@ -812,8 +892,7 @@
         for i in range(n):
             lanes.copy(k * n + i, slots[i](k), slots[i](k), "ctx", p.up).wait_send()
     for j in range(2):
-        lanes.recv(base + j, grads_out.at[1 + j, pl.ds(CHUNK, CHUNK)], "ctx", swap)
-    lanes.finish()
+        back_copy(j).wait()
 
 
 def attention(keys, k_far, values, v_far, q_row, q_mate, do_all, lse, delta_all, dw_part, scale):
@@ -827,12 +906,14 @@
             jax.ShapeDtypeStruct((3, tok_ctx, head), BF),
             jax.ShapeDtypeStruct(dw_part.shape[1:], BF),
         ),
-        in_specs=[vmem] * 4 + [anyw] * 2 + [vmem] * 4,
+        in_specs=[vmem] * 4 + [anyw] * 3 + [vmem] * 3,
         out_specs=(vmem,) * 2,
         scratch_shapes=[
             VM(do_all.shape, BF),
+            VM(do_all.shape, BF),
             VM((2, CHUNK, head), BF),
             VM((2, CHUNK, head), BF),
+            VM((2, CHUNK, head), F32),
             VM(do_all.shape, BF),
             VM((2, CHUNK, head), F32),
             VM((2, CHUNK, head), F32),
@@ -842,7 +923,7 @@
             VM((AG_LANES, dw_part.shape[1] // 2, dw_part.shape[2]), BF),
             pltpu.SemaphoreType.DMA((n_sem,)),
             pltpu.SemaphoreType.DMA((n_sem,)),
-            pltpu.SemaphoreType.DMA((2,)),
+            pltpu.SemaphoreType.DMA((2, 8)),
         ],
         compiler_params=pltpu.CompilerParams(
             collective_id=4, has_side_effects=True, vmem_limit_bytes=VLIM

time: 328 us -> 312 us (0.951)
  Pallas kernels: 295 us -> 278 us
    pallas_call x1, Pallas kernels: 88.1 us -> 81.7 us  [attention(): pl.pallas_call(functools.partial(attention_kernel, scale, n_ctx), out_sha...]
    pallas_call x1, Pallas kernels: 60.8 us -> 57 us  [combine(): pl.pallas_call(combine_kernel, out_shape=(jax.ShapeDtypeStruct((n_exp, 2,...]
where the time goes in v4:
time: 312 us; the launch traced here: 311 us
  Pallas kernels  278 us (89%)
  matrix products  17.7 us (6%)
  local copies, waits for them, and re-layouts  9.8 us (3%)
  other arithmetic  4.45 us (1%)
    pallas_call x1, Pallas kernels, attention(): pl.pallas_call(functools.partial(attention_kernel, scale, n_ctx), out_sha...  81.7 us
    pallas_call x1, Pallas kernels, combine(): pl.pallas_call(combine_kernel, out_shape=(jax.ShapeDtypeStruct((n_exp, 2,...  57 us
    pallas_call x1, Pallas kernels, spread(): pl.pallas_call(spread_kernel, out_shape=(jax.ShapeDtypeStruct((n_ctx, tok...  49.9 us
    pallas_call x1, Pallas kernels, share(): pl.pallas_call(share_kernel, out_shape=(jax.ShapeDtypeStruct(mine.shape[:...  49.3 us
    pallas_call x1, Pallas kernels, dispatch(): pl.pallas_call(functools.partial(dispatch_kernel, n_ctx), out_shape=(jax....  40.4 us

profile of v4, /device:TPU:0, one launch (start us, length us, event | category | flops | bytes accessed | tf_op | source)
XLA Modules:
  0.0 311.1 jit_solution(7225938544907251736)
XLA Ops:
  0.7 0.9 broadcast_multiply_fusion
  1.9 0.7 fusion.10.place_ref
  2.6 0.8 convert_reduce_fusion.1
  3.5 0.9 select_reduce_fusion.1
  4.7 0.7 fusion.7.pick_ref
  5.4 40.4 %shard_map.196 = (bf16[2,2,16,4096]{3,2,1,0:T(8,128)(2,1)}, bf16[1024,128]{1,0:T(8,128)(2,1)}, bf16[1024,128]{1,0:T(8,128)(2,1)}, bf16[4,2048,128]{2,1,0:T(8,128)(2,1)}) custom-call(bf16[128,4096]{1,0:T(8,128)(2,1)} %mi_ref.1, bf16[128,4096]{1,0:T(8,128)(2,1)} %og_ref.3, bf16[128,256]{1,0:T(8,128)(2,1)} %fusion.7.pick_ref, ...), custom_call_target="tpu_custom_call" | custom-call | flops 1000000 | bytes 1000000 | tf_op jit(solution)/shard_map/pallas_call | solution.py:323
  45.8 49.3 %shard_map.197 = (bf16[2,2,8,16,4096]{4,3,2,1,0:T(8,128)(2,1)}, bf16[4,128,4096]{2,1,0:T(8,128)(2,1)}, bf16[4,128,4096]{2,1,0:T(8,128)(2,1)}, bf16[4,4,128,128]{3,2,1,0:T(8,128)(2,1)}) custom-call(bf16[2,2,16,4096]{3,2,1,0:T(8,128)(2,1)} %get-tuple-element.26.mine_ref, bf16[128,4096]{1,0:T(8,128)(2,1)} %og_ref.3, bf16[128,4096]{1,0:T(8,128)(2,1)} %w_ref.3, ...), custom_call_target="tpu_custom_call" | custom-call | flops 1000000 | bytes 1000000 | tf_op jit(solution)/shard_map/pallas_call | solution.py:405
  95.2 2.9 fusion.21
  98.2 0.9 fusion.22
  99.2 1.1 fusion.23
  100.3 0.7 constant_dynamic-slice_fusion
  101.3 0.9 multiply_reduce_fusion
  102.2 0.8 fusion.24
  103.0 2.2 fusion
  105.9 57.0 %shard_map.198 = (bf16[16,2,16,4096]{3,2,1,0:T(8,128)(2,1)}, f32[2,1,128]{2,1,0:T(1,128)}, bf16[4,2048,128]{2,1,0:T(8,128)(2,1)}, bf16[2,4,2,128,128]{4,3,2,1,0:T(8,128)(2,1)}) custom-call(bf16[2,8,16,4096]{3,2,1,0:T(8,128)(2,1)} %bitcast.44, f32[2,8,1,128]{3,2,1,0:T(1,128)} %pad.4.gate_ref, bf16[2048,128]{1,0:T(8,128)(2,1)} %q_ref.3, ...), custom_call_target="tpu_custom_call" | custom-call | flops 1000000 | bytes 1000000 | tf_op jit(solution)/shard_map/pallas_call | solution.py:522
  163.0 0.7 sub.95.ids_ref
  163.6 49.9 %shard_map.199 = (bf16[8,2048,128]{2,1,0:T(8,128)(2,1)}, f32[8,1,2048]{2,1,0:T(1,128)}, bf16[8,128,512]{2,1,0:T(8,128)(2,1)}) custom-call(bf16[2048,128]{1,0:T(8,128)(2,1)} %bitcast.46, bf16[128,4096]{1,0:T(8,128)(2,1)} %w_ref.3, bf16[2048,128]{1,0:T(8,128)(2,1)} %o_ref.1, s32[1,512]{1,0:T(1,128)} %sub.95.ids_ref, bf16[512,4096]{1,0:T(8,128)(2,1)} %bitcast.40, ...), custom_call_target="tpu_custom_call" | custom-call | flops 1000000 | bytes 1000000 | tf_op jit(solution)/shard_map/pallas_call | solution.py:659
  213.6 81.7 %shard_map.200 = (bf16[3,2048,128]{2,1,0:T(8,128)(2,1)}, bf16[128,512]{1,0:T(8,128)(2,1)}) custom-call(bf16[2048,128]{1,0:T(8,128)(2,1)} %k_own.1, bf16[1024,128]{1,0:T(8,128)(2,1)} %get-tuple-element.32.k_far, bf16[2048,128]{1,0:T(8,128)(2,1)} %v_own.1, bf16[1024,128]{1,0:T(8,128)(2,1)} %get-tuple-element.33.v_far, ...), custom_call_target="tpu_custom_call" | custom-call | flops 40000000000 | bytes 20000000 | tf_op jit(solution)/shard_map/pallas_call | solution.py:903
  295.3 2.7 slice_bitcast_fusion
  298.0 2.6 convolution_convert_fusion.2
  300.6 2.5 convolution_convert_fusion
  303.1 2.5 convolution_convert_fusion.1
  305.7 4.2 %fusion.1 = bf16[128,4096]{1,0:T(8,128)(2,1)} fusion(bf16[512,4096]{1,0:T(8,128)(2,1)} %bitcast.41, bf16[128,4096]{1,0:T(8,128)(2,1)} %og_ref.3, s32[512]{0:T(512)S(1)} %sub.78, s32[128]{0:T(128)S(1)} %iota_add_fusion), kind=kOutput, calls=%fused_computation.6 | convolution fusion | flops 538509312 | bytes 6294016 | tf_op jit(solution)/shard_map/dot_general | solution.py:1038
  310.5 0.7 copy.35
  (39 shorter events, 2.6 us)
Async XLA Ops:
  0.6 98.5 %copy-start = (bf16[2,4096,176]{1,2,0:T(8,128)(2,1)S(1)}, bf16[2,4096,176]{1,2,0:T(8,128)(2,1)}, u32[]{:S(2)}) copy-start(bf16[2,4096,176]{1,2,0:T(8,128)(2,1)} %param.15) | copy-start | bytes 8650756
  95.2 3.1 copy-start.3
  98.0 2.2 copy-start.1
  98.0 3.0 copy-start.4
  99.2 2.1 copy-start.9
  105.9 57.0 %copy-start.6 = (s32[32,128]{1,0:T(8,128)S(1)}, s32[32,128]{1,0:T(8,128)}, u32[]{:S(2)}) copy-start(s32[32,128]{1,0:T(8,128)} %param.18) | copy-start | bytes 49156
  295.3 2.7 copy-start.5
  298.0 2.6 copy-start.2
  305.6 4.3 %copy-start.8 = (f32[2,1,128]{2,1,0:T(1,128)S(1)}, f32[2,1,128]{2,1,0:T(1,128)}, u32[]{:S(2)}) copy-start(f32[2,1,128]{2,1,0:T(1,128)} %get-tuple-element.31) | copy-start | bytes 3076
  305.7 4.8 %copy-start.7 = (bf16[128,512]{1,0:T(8,128)(2,1)S(1)}, bf16[128,512]{1,0:T(8,128)(2,1)}, u32[]{:S(2)}) copy-start(bf16[128,512]{1,0:T(8,128)(2,1)} %get-tuple-element.74) | copy-start | bytes 393220

commit v5 on v4

--- a/solution.py
+++ b/solution.py
@@ -349,7 +349,7 @@
 
 
 def share_kernel(
-    mine_ref, og_ref, w_ref, o_ref, out_ref, og_row, w_group, o_group, ss, rs, keep_sems
+    mine_ref, og_ref, w_ref, o_ref, x_all, y_all, og_row, w_group, o_group, ss, rs, keep_sems
 ):
     ctx, exp = Place("ctx"), Place("exp")
     others = (exp.twin, exp.mate, exp.mate_twin)
@@ -364,7 +364,8 @@
     base = AG_LANES + RING_LANES
 
     def more():
-        lanes.keep(keep_sems.at[0], mine_ref, out_ref.at[:, :, ctx.me])
+        lanes.keep(keep_sems.at[0], mine_ref.at[0], x_all.at[:, ctx.me])
+        lanes.keep(keep_sems.at[4], mine_ref.at[1], y_all.at[:, ctx.me])
         lanes.keep(keep_sems.at[1], og_ref, og_row.at[exp.spots[0]])
         lanes.keep(keep_sems.at[2], w_ref, w_group.at[me])
         own_o = o_ref.at[exp.me // 8, :, lax.rem(exp.me, 2)]
@@ -386,7 +387,7 @@
     nothing = lambda: None
     work = [more, ring.forward, nothing, nothing, pass_on]
     gather_ring(
-        [lambda block, half: out_ref.at[half, :, block]], ctx, lanes, 0, work=work,
+        [lambda block, half: (x_all, y_all)[half].at[:, block]], ctx, lanes, 0, work=work,
         own=[lambda half: mine_ref.at[half]],
     )
     ring.end()
@@ -401,21 +402,23 @@
     n_ctx = lax.axis_size("ctx")
     rows, head = out_grad.shape[0], attn_out.shape[1]
     n_sem = AG_LANES + RING_LANES + 6
+    slots = jax.ShapeDtypeStruct((mine.shape[1], n_ctx) + mine.shape[2:], BF)
     vmem = pl.BlockSpec(memory_space=VM)
     return pl.pallas_call(
         share_kernel,
         out_shape=(
-            jax.ShapeDtypeStruct(mine.shape[:2] + (n_ctx,) + mine.shape[2:], BF),
+            slots,
+            slots,
             jax.ShapeDtypeStruct((4,) + out_grad.shape, BF),
             jax.ShapeDtypeStruct((4,) + w_out.shape, BF),
             jax.ShapeDtypeStruct((4, 4, rows, head), BF),
         ),
         in_specs=[vmem] * 4,
-        out_specs=(vmem,) + (ANY_SPEC,) * 3,
+        out_specs=(vmem,) * 2 + (ANY_SPEC,) * 3,
         scratch_shapes=[
             pltpu.SemaphoreType.DMA((n_sem,)),
             pltpu.SemaphoreType.DMA((n_sem,)),
-            pltpu.SemaphoreType.DMA((4,)),
+            pltpu.SemaphoreType.DMA((5,)),
         ],
         compiler_params=pltpu.CompilerParams(
             collective_id=5, has_side_effects=True, vmem_limit_bytes=VLIM
@@ -993,9 +996,9 @@
     mine, k_far, v_far, q_row = dispatch(
         moe_input, out_grad, pick, place, attn_keys, values, queries
     )
-    slots, og_row, w_group, o_group = share(mine, out_grad, w_out, attn_out)
-    slots = slots.reshape(2, n_local, n_ctx * group_picks, feat_width)
-    slot_rows, slot_grads = slots[0], slots[1]
+    slot_rows, slot_grads, og_row, w_group, o_group = share(mine, out_grad, w_out, attn_out)
+    slot_rows = slot_rows.reshape(n_local, n_ctx * group_picks, feat_width)
+    slot_grads = slot_grads.reshape(n_local, n_ctx * group_picks, feat_width)
 
     gate_rows = lax.dynamic_slice_in_dim(gate_probs, exp_id * n_local, n_local, 0)
     pre_gate = jnp.einsum("kcd,kdf->kcf", slot_rows, w_gate, preferred_element_type=F32)

time: 312 us -> 311 us (level)
  no operation moved by 1% of the time
where the time goes in v5:
time: 311 us; the launch traced here: 310 us
  Pallas kernels  279 us (90%)
  matrix products  19.2 us (6%)
  local copies, waits for them, and re-layouts  7.27 us (2%)
  other arithmetic  4.45 us (1%)
    pallas_call x1, Pallas kernels, attention(): pl.pallas_call(functools.partial(attention_kernel, scale, n_ctx), out_sha...  81.8 us
    pallas_call x1, Pallas kernels, combine(): pl.pallas_call(combine_kernel, out_shape=(jax.ShapeDtypeStruct((n_exp, 2,...  57 us
    pallas_call x1, Pallas kernels, spread(): pl.pallas_call(spread_kernel, out_shape=(jax.ShapeDtypeStruct((n_ctx, tok...  49.9 us
    pallas_call x1, Pallas kernels, share(): pl.pallas_call(share_kernel, out_shape=(slots, slots, jax.ShapeDtypeStruc...  49.4 us
    pallas_call x1, Pallas kernels, dispatch(): pl.pallas_call(functools.partial(dispatch_kernel, n_ctx), out_shape=(jax....  40.5 us

profile of v5, /device:TPU:0, one launch (start us, length us, event | category | flops | bytes accessed | tf_op | source)
XLA Modules:
  0.0 310.3 jit_solution(14579775128073749152)
XLA Ops:
  0.7 0.9 broadcast_multiply_fusion
  1.9 0.7 fusion.10.place_ref
  2.6 0.8 convert_reduce_fusion.1
  3.5 0.9 select_reduce_fusion.1
  4.7 0.7 fusion.7.pick_ref
  5.4 40.5 %shard_map.196 = (bf16[2,2,16,4096]{3,2,1,0:T(8,128)(2,1)}, bf16[1024,128]{1,0:T(8,128)(2,1)}, bf16[1024,128]{1,0:T(8,128)(2,1)}, bf16[4,2048,128]{2,1,0:T(8,128)(2,1)}) custom-call(bf16[128,4096]{1,0:T(8,128)(2,1)} %mi_ref.1, bf16[128,4096]{1,0:T(8,128)(2,1)} %og_ref.3, bf16[128,256]{1,0:T(8,128)(2,1)} %fusion.7.pick_ref, ...), custom_call_target="tpu_custom_call" | custom-call | flops 1000000 | bytes 1000000 | tf_op jit(solution)/shard_map/pallas_call | solution.py:323
  45.9 49.4 %shard_map.197 = (bf16[2,8,16,4096]{3,2,1,0:T(8,128)(2,1)}, bf16[2,8,16,4096]{3,2,1,0:T(8,128)(2,1)}, bf16[4,128,4096]{2,1,0:T(8,128)(2,1)}, bf16[4,128,4096]{2,1,0:T(8,128)(2,1)}, bf16[4,4,128,128]{3,2,1,0:T(8,128)(2,1)}) custom-call(bf16[2,2,16,4096]{3,2,1,0:T(8,128)(2,1)} %get-tuple-element.27.mine_ref, bf16[128,4096]{1,0:T(8,128)(2,1)} %og_ref.3, ...), custom_call_target="tpu_custom_call" | custom-call | flops 1000000 | bytes 1000000 | tf_op jit(solution)/shard_map/pallas_call | solution.py:407
  95.3 2.6 fusion.21
  98.0 0.9 fusion.22
  98.9 1.2 constant_dynamic-slice_fusion
  100.5 0.9 multiply_reduce_fusion
  101.4 0.8 fusion.23
  102.1 2.2 fusion
  104.4 0.6 pad.4.gate_ref
  105.0 57.0 %shard_map.198 = (bf16[16,2,16,4096]{3,2,1,0:T(8,128)(2,1)}, f32[2,1,128]{2,1,0:T(1,128)}, bf16[4,2048,128]{2,1,0:T(8,128)(2,1)}, bf16[2,4,2,128,128]{4,3,2,1,0:T(8,128)(2,1)}) custom-call(bf16[2,8,16,4096]{3,2,1,0:T(8,128)(2,1)} %bitcast.42, f32[2,8,1,128]{3,2,1,0:T(1,128)} %pad.4.gate_ref, bf16[2048,128]{1,0:T(8,128)(2,1)} %q_ref.3, ...), custom_call_target="tpu_custom_call" | custom-call | flops 1000000 | bytes 1000000 | tf_op jit(solution)/shard_map/pallas_call | solution.py:525
  162.1 0.7 sub.95.ids_ref
  162.8 49.9 %shard_map.199 = (bf16[8,2048,128]{2,1,0:T(8,128)(2,1)}, f32[8,1,2048]{2,1,0:T(1,128)}, bf16[8,128,512]{2,1,0:T(8,128)(2,1)}) custom-call(bf16[2048,128]{1,0:T(8,128)(2,1)} %bitcast.46, bf16[128,4096]{1,0:T(8,128)(2,1)} %w_ref.3, bf16[2048,128]{1,0:T(8,128)(2,1)} %o_ref.1, s32[1,512]{1,0:T(1,128)} %sub.95.ids_ref, bf16[512,4096]{1,0:T(8,128)(2,1)} %bitcast.40, ...), custom_call_target="tpu_custom_call" | custom-call | flops 1000000 | bytes 1000000 | tf_op jit(solution)/shard_map/pallas_call | solution.py:662
  212.7 81.8 %shard_map.200 = (bf16[3,2048,128]{2,1,0:T(8,128)(2,1)}, bf16[128,512]{1,0:T(8,128)(2,1)}) custom-call(bf16[2048,128]{1,0:T(8,128)(2,1)} %k_own.1, bf16[1024,128]{1,0:T(8,128)(2,1)} %get-tuple-element.34.k_far, bf16[2048,128]{1,0:T(8,128)(2,1)} %v_own.1, bf16[1024,128]{1,0:T(8,128)(2,1)} %get-tuple-element.35.v_far, ...), custom_call_target="tpu_custom_call" | custom-call | flops 40000000000 | bytes 20000000 | tf_op jit(solution)/shard_map/pallas_call | solution.py:906
  294.5 2.7 slice_bitcast_fusion
  297.2 2.6 convolution_convert_fusion.2
  299.8 2.5 convolution_convert_fusion
  302.3 2.5 convolution_convert_fusion.1
  304.9 4.2 %fusion.1 = bf16[128,4096]{1,0:T(8,128)(2,1)} fusion(bf16[512,4096]{1,0:T(8,128)(2,1)} %bitcast.41, bf16[128,4096]{1,0:T(8,128)(2,1)} %og_ref.3, s32[512]{0:T(512)S(1)} %sub.78, s32[128]{0:T(128)S(1)} %iota_add_fusion), kind=kOutput, calls=%fused_computation.6 | convolution fusion | flops 538509312 | bytes 6294016 | tf_op jit(solution)/shard_map/dot_general | solution.py:1041
  309.7 0.7 copy.35
  (38 shorter events, 1.9 us)
Async XLA Ops:
  0.6 97.3 %copy-start = (bf16[2,4096,176]{1,2,0:T(8,128)(2,1)S(1)}, bf16[2,4096,176]{1,2,0:T(8,128)(2,1)}, u32[]{:S(2)}) copy-start(bf16[2,4096,176]{1,2,0:T(8,128)(2,1)} %param.15) | copy-start | bytes 8650756
  5.4 89.9 %copy-start.3 = (bf16[2,4096,176]{1,2,0:T(8,128)(2,1)S(1)}, bf16[2,4096,176]{1,2,0:T(8,128)(2,1)}, u32[]{:S(2)}) copy-start(bf16[2,4096,176]{1,2,0:T(8,128)(2,1)} %param.16) | copy-start | bytes 8650756
  95.3 2.7 copy-start.1
  98.0 2.1 copy-start.4
  98.0 2.5 copy-start.9
  105.0 57.0 %copy-start.6 = (s32[32,128]{1,0:T(8,128)S(1)}, s32[32,128]{1,0:T(8,128)}, u32[]{:S(2)}) copy-start(s32[32,128]{1,0:T(8,128)} %param.18) | copy-start | bytes 49156
  294.5 2.7 copy-start.5
  297.2 2.6 copy-start.2
  304.8 4.3 %copy-start.8 = (f32[2,1,128]{2,1,0:T(1,128)S(1)}, f32[2,1,128]{2,1,0:T(1,128)}, u32[]{:S(2)}) copy-start(f32[2,1,128]{2,1,0:T(1,128)} %get-tuple-element.33) | copy-start | bytes 3076
  304.8 4.8 %copy-start.7 = (bf16[128,512]{1,0:T(8,128)(2,1)S(1)}, bf16[128,512]{1,0:T(8,128)(2,1)}, u32[]{:S(2)}) copy-start(bf16[128,512]{1,0:T(8,128)(2,1)} %get-tuple-element.74) | copy-start | bytes 393220
